TPU v7x, 256 devices: a whole 4x4x8 slice. The times are simulated.
256 devices in a mesh: head: 4 (over y_hi, core), seq: 64 (over x, y_lo, z).
Axes of the slice: x: 4, y: 4 (y_hi: 2, y_lo: 2; y = y_hi * 2 + y_lo), z: 8, core: 2. Of those that a mesh axis runs over, the one named last changes fastest.
Arguments:
- queries: bfloat16 [32768, 4096], P('seq', 'head'), may hold values from -6 to 6
- keys: bfloat16 [32768, 4096], P('seq', 'head'), may hold values from -6 to 6
- values: bfloat16 [32768, 4096], P('seq', 'head'), may hold values from -6 to 6
- rate: float32 [8, 32768], P('head', 'seq'), may hold values from 0.0001 to 0.001
- fast_gate: float32 [8, 512, 512], P('head', 'seq'), may hold values from -3 to 3
- fast_up: float32 [8, 512, 512], P('head', 'seq'), may hold values from -3 to 3
- fast_down: float32 [8, 512, 512], P('head', 'seq'), may hold values from -8 to 8
- out_gain: float32 [4096], P('head'), may hold values from 0.25 to 1.75
Outputs:
- mixed: bfloat16 [32768, 4096], P('seq', 'head')
- new_gate: float32 [8, 512, 512], P('head', 'seq')
- new_up: float32 [8, 512, 512], P('head', 'seq')
- new_down: float32 [8, 512, 512], P('head', 'seq')
All inputs are finite; a program needn't handle non-finite values.
Results may differ from a plain program's by a relative error of at most 0.012.
Values may be sent and summed in bfloat16 or wider, within the bound.
No kernel may reach another device: no remote copies, remote signals or barrier semaphores. Data moves between devices by JAX's collectives and lax.ppermute only.
A program may use at most 128 MiB of HBM per device.

v0:
```python
import math

import jax
import jax.numpy as jnp
from jax import lax
from jax.sharding import PartitionSpec as P

HEADS = 8
HD = 512
WINDOW = 512


EPS = 1e-06


def from_behind(block, axis, distance):
    devices = range(lax.axis_size(axis))
    route = [(i - distance, i) for i in devices if i - distance in devices]
    return lax.ppermute(block, axis, route)


def column_sq(matrix):
    return jnp.sum(matrix * matrix, axis=1)


def apply_ratio(upd, old_sq, new_sq):
    return upd * (jnp.sqrt(old_sq) / jnp.sqrt(new_sq + EPS))[:, None, :]


def gradients(k_three, scaled, w_oneb, w_threeb, w_twob):
    pre_a = jnp.einsum("thd,hdf->thf", k_three, w_oneb, preferred_element_type=jnp.float32)
    pre_b = jnp.einsum("thd,hdf->thf", k_three, w_threeb, preferred_element_type=jnp.float32)
    sigma = jax.nn.sigmoid(pre_a)
    hidden = (pre_a * sigma * pre_b).astype(jnp.bfloat16)
    grad_two = jnp.einsum("thf,thd->hfd", hidden, scaled, preferred_element_type=jnp.float32)
    back = jnp.einsum("thd,hfd->thf", scaled, w_twob, preferred_element_type=jnp.float32)
    d_gate = (back * pre_b * sigma * (1.0 + pre_a * (1.0 - sigma))).astype(jnp.bfloat16)
    d_up = (back * pre_a * sigma).astype(jnp.bfloat16)
    grad_one = jnp.einsum("thd,thf->hdf", k_three, d_gate, preferred_element_type=jnp.float32)
    grad_three = jnp.einsum("thd,thf->hdf", k_three, d_up, preferred_element_type=jnp.float32)
    return (grad_one, grad_three, grad_two)


def local(queries, keys, values, rate, fast_gate, fast_up, fast_down, out_gain):
    rows, width = queries.shape
    heads = fast_gate.shape[0]
    head_dim = width // heads
    seq_pos = lax.axis_index("seq")
    q_three = queries.reshape(rows, heads, head_dim)
    k_three = keys.reshape(rows, heads, head_dim)
    v_three = values.reshape(rows, heads, head_dim)
    prev_k, prev_v = from_behind((keys, values), "seq", 1)
    blocks = rows // WINDOW
    ext_k = jnp.concatenate([prev_k, keys], axis=0).reshape(blocks + 1, WINDOW, heads, head_dim)
    ext_v = jnp.concatenate([prev_v, values], axis=0).reshape(blocks + 1, WINDOW, heads, head_dim)
    k_win = jnp.concatenate([ext_k[:-1], ext_k[1:]], axis=1)
    v_win = jnp.concatenate([ext_v[:-1], ext_v[1:]], axis=1)
    q_blocks = q_three.reshape(blocks, WINDOW, heads, head_dim)
    scores = jnp.einsum("bqhd,bkhd->bhqk", q_blocks, k_win, preferred_element_type=jnp.float32)
    scores = scores * (1.0 / math.sqrt(head_dim))
    rows_i = jnp.arange(WINDOW, dtype=jnp.int32)[None, :, None]
    cols_j = jnp.arange(2 * WINDOW, dtype=jnp.int32)[None, None, :]
    block_at = jnp.arange(blocks, dtype=jnp.int32)[:, None, None] * WINDOW
    valid = (
        (cols_j > rows_i)
        & (cols_j <= rows_i + WINDOW)
        & (block_at + cols_j + seq_pos * rows >= WINDOW)
    )
    scores = jnp.where(valid[:, None], scores, -jnp.inf)
    top = jnp.max(scores, axis=-1, keepdims=True)
    expo = jnp.exp(scores - top)
    probs = (expo / jnp.sum(expo, axis=-1, keepdims=True)).astype(jnp.bfloat16)
    attn = jnp.einsum("bhqk,bkhd->bqhd", probs, v_win, preferred_element_type=jnp.float32)
    attn = attn.reshape(rows, heads, head_dim)
    scaled = (rate.T[:, :, None] * v_three.astype(jnp.float32)).astype(jnp.bfloat16)
    full_one, full_three, full_two = (
        lax.all_gather(fast_gate, "seq", axis=1, tiled=True),
        lax.all_gather(fast_up, "seq", axis=1, tiled=True),
        lax.all_gather(fast_down, "seq", axis=1, tiled=True),
    )
    grad_one, grad_three, grad_two = gradients(
        k_three,
        scaled,
        full_one.astype(jnp.bfloat16),
        full_three.astype(jnp.bfloat16),
        full_two.astype(jnp.bfloat16),
    )
    grad_one, grad_three, grad_two = lax.psum((grad_one, grad_three, grad_two), "seq")
    upd_one = full_one + grad_one
    upd_three = full_three + grad_three
    upd_two = full_two + grad_two
    whole_one = apply_ratio(upd_one, column_sq(full_one), column_sq(upd_one))
    whole_three = apply_ratio(upd_three, column_sq(full_three), column_sq(upd_three))
    whole_two = apply_ratio(upd_two, column_sq(full_two), column_sq(upd_two))
    use_one = whole_one.astype(jnp.bfloat16)
    use_three = whole_three.astype(jnp.bfloat16)
    use_two = whole_two.astype(jnp.bfloat16)
    shard = fast_gate.shape[1]
    first = seq_pos * shard
    new_gate = lax.dynamic_slice_in_dim(whole_one, first, shard, 1)
    new_up = lax.dynamic_slice_in_dim(whole_three, first, shard, 1)
    new_down = lax.dynamic_slice_in_dim(whole_two, first, fast_down.shape[1], 1)
    apply_a = jnp.einsum("thd,hdf->thf", q_three, use_one, preferred_element_type=jnp.float32)
    apply_b = jnp.einsum("thd,hdf->thf", q_three, use_three, preferred_element_type=jnp.float32)
    apply_h = (apply_a * jax.nn.sigmoid(apply_a) * apply_b).astype(jnp.bfloat16)
    branch = jnp.einsum("thf,hfd->thd", apply_h, use_two, preferred_element_type=jnp.float32)
    local_sq = jnp.sum(branch * branch, axis=(1, 2))
    total_sq = lax.psum(local_sq, "head")
    inv = lax.rsqrt(total_sq / (HEADS * HD) + EPS)
    gain = out_gain.reshape(heads, head_dim)
    mixed = (attn + branch * inv[:, None, None] * gain[None]).astype(jnp.bfloat16)
    return (mixed.reshape(rows, width), new_gate, new_up, new_down)


def solution(mesh):
    in_specs = (
        P("seq", "head"),
        P("seq", "head"),
        P("seq", "head"),
        P("head", "seq"),
        P("head", "seq", None),
        P("head", "seq", None),
        P("head", "seq", None),
        P("head"),
    )
    out_specs = (
        P("seq", "head"),
        P("head", "seq", None),
        P("head", "seq", None),
        P("head", "seq", None),
    )
    return jax.shard_map(local, mesh=mesh, in_specs=in_specs, out_specs=out_specs, check_vma=False)
```

profile of v0, /device:TPU:1, one launch (start us, length us, event | category | flops | bytes accessed | tf_op | source)
XLA Modules:
  0.0 1580.3 jit_solution(9105765221458743855)
XLA Ops:
  7.2 1.4 copy.60
  8.7 1.4 copy.63
  10.9 2.8 convert_element_type.61
  13.7 256.3 %all-gather.6.cloned.1.call-done = f32[2,512,512]{2,0,1:T(2,128)} async-done(((f32[2,8,512]{2,0,1:T(2,128)}), f32[2,512,512]{2,0,1:T(2,128)}) %all-gather.6.cloned.1.call-update) | async-done | bytes 2097168 | tf_op jit(solution)/shard_map/all_gather | solution.py:77
  270.0 2.7 copy.61
  272.8 296.6 %all-gather.8.cloned.1.call-done = f32[2,512,512]{2,0,1:T(2,128)} async-done(((f32[2,8,512]{2,0,1:T(2,128)}), f32[2,512,512]{2,0,1:T(2,128)}) %all-gather.8.cloned.1.call-update) | async-done | bytes 2097168 | tf_op jit(solution)/shard_map/all_gather | solution.py:78
  569.4 4.1 copy.64
  577.2 1.0 copy-done.5
  578.2 2.1 fusion.52
  580.3 288.1 %all-gather.4.cloned.1.call-done = f32[2,512,512]{2,1,0:T(8,128)} async-done(((f32[2,8,512]{2,1,0:T(8,128)}), f32[2,512,512]{2,1,0:T(8,128)}) %all-gather.4.cloned.1.call-update) | async-done | bytes 2097168 | tf_op jit(solution)/shard_map/all_gather | solution.py:79
  868.4 3.2 fusion.44
  871.9 2.6 convolution_bitcast_fusion.1
  874.5 2.1 convolution_bitcast_fusion
  876.6 1.3 copy.54
  877.9 3.5 collective-permute-start.1
  881.5 2.3 collective-permute-start
  883.7 2.3 copy.53
  886.1 1.3 copy.57
  887.4 1.2 fusion.27
  888.6 4.3 collective-permute-done.1
  892.9 2.4 copy.56
  895.3 9.3 collective-permute-done
  904.5 2.3 copy.52
  906.8 2.9 fusion.6
  909.7 4.1 fusion.72
  916.3 582.8 %all-reduce.3.cloned.1.call-done = (f32[2,512,512]{1,2,0:T(8,128)}, f32[2,512,512]{1,2,0:T(8,128)}, f32[2,512,512]{2,1,0:T(8,128)}) async-done(((f32[2,512,512]{1,2,0:T(8,128)}, f32[2,512,512]{1,2,0:T(8,128)}, f32[2,512,512]{2,1,0:T(8,128)}), (f32[2,512,512]{1,2,0:T(8,128)}, f32[2,512,512]{1,2,0:T(8,128)}, f32[2,512,512]{2,1,0:T(8,128)})) %all-reduce.3.cloned.1.call-update) | async-done | bytes 6291472 | tf_op jit(solution)/shard_map/psum | solution.py:88
  1499.1 3.4 multiply_reduce_fusion.1
  1502.7 2.1 fusion.38
  1508.1 5.4 multiply_reduce_fusion
  1513.5 52.7 %psum.31 = f32[512]{0:T(512)S(1)} all-reduce(f32[512]{0:T(512)S(1)} %get-tuple-element.28), channel_id=1, replica_groups=mesh['head'=4,'seq'=64] {'head'}, use_global_device_ids=true, to_apply=%region_12.13 | all-reduce | flops 512 | bytes 4096 | tf_op jit(solution)/shard_map/psum | solution.py:108
  1566.2 4.7 fusion.9
  1570.9 1.3 copy.76
  (61 shorter events, 12.4 us)
Async XLA Ops:
  7.2 262.9 %all-gather.6.cloned.1.call-start = ((), (), s32[]{:S(2)}) async-start(), calls=%async_computation.1 | async-start | bytes 2129920 | tf_op jit(solution)/shard_map/all_gather | solution.py:77
  8.6 560.7 %all-gather.8.cloned.1.call-start = ((), (), s32[]{:S(2)}) async-start(), calls=%async_computation.2 | async-start | bytes 2129920 | tf_op jit(solution)/shard_map/all_gather | solution.py:78
  10.1 858.3 %all-gather.4.cloned.1.call-start = ((), (), s32[]{:S(2)}) async-start(), calls=%async_computation | async-start | bytes 2129920 | tf_op jit(solution)/shard_map/all_gather | solution.py:79
  10.8 1488.3 %all-reduce.3.cloned.1.call-start = ((), (), s32[]{:S(2)}) async-start(), calls=%async_computation.3 | async-start | bytes 12582912 | tf_op jit(solution)/shard_map/psum | solution.py:88
  272.8 300.7 %copy-start.1 = (bf16[512,1024]{1,0:T(8,128)(2,1)S(1)}, bf16[512,1024]{1,0:T(8,128)(2,1)}, u32[]{:S(2)}) copy-start(bf16[512,1024]{1,0:T(8,128)(2,1)} %param.9) | copy-start | bytes 3145732
  573.5 1.6 copy-start
  575.1 1.3 copy-start.9
  575.1 3.1 copy-start.5
  575.1 3.1 copy-start.16
  575.9 1.4 copy-start.11
  868.4 3.2 copy-start.10
  868.4 3.5 copy-start.12
  877.9 8.1 copy-start.6
  877.9 15.0 collective-permute-start.1
  881.5 23.1 %collective-permute-start = (bf16[512,1024]{1,0:T(8,128)(2,1)}, bf16[512,1024]{1,0:T(8,128)(2,1)}, u32[]{:S(2)}, u32[]{:S(2)}) collective-permute-start(bf16[512,1024]{1,0:T(8,128)(2,1)} %param.10), channel_id=1, source_target_pairs={{0,1},{1,2},{2,3},{3,4},{4,5},{5,6},{6,7},{7,8},{8,9},{9,10},{10,1... | collective-permute-start | bytes 3145736 | tf_op jit(solution)/shard_map/ppermute | solution.py:19
  883.7 3.6 copy-start.15
  892.9 13.9 copy-start.13
  906.8 2.9 copy-start.14
  909.7 4.1 copy-start.3
  913.8 1.6 copy-start.2
  1502.7 2.3 copy-start.4
  1502.7 3.0 copy-start.8
  1506.5 1.4 copy-start.7
Sparse Core Ops, SparseCore 0:
  10.4 259.6 all-gather.5
  272.4 296.9 all-gather.7
  571.2 297.2 all-gather.3
  876.7 622.3 all-reduce.2
where the time goes:
time: 1580 us
  waiting for transfers between devices  1440 us (91%)
  blocking collectives  52.7 us (3%)
  local copies, waits for them, and re-layouts  28.4 us (2%)
  matrix products  26.6 us (2%)
    psum x1, waiting for transfers between devices, local(): lax.psum((grad_one, grad_three, grad_two), 'seq')  583 us
    all_gather x1, waiting for transfers between devices, local(): lax.all_gather(fast_up, 'seq', axis=1, tiled=True)  297 us
    all_gather x1, waiting for transfers between devices, local(): lax.all_gather(fast_down, 'seq', axis=1, tiled=True)  288 us
    all_gather x1, waiting for transfers between devices, local(): lax.all_gather(fast_gate, 'seq', axis=1, tiled=True)  256 us
    psum x1, blocking collectives, local(): total_sq = lax.psum(local_sq, 'head')  52.7 us
  transfers between devices with their start and end apart: 6, of which 6 were waited for; matrix products, arithmetic and copies ran while one was open for 2% of the time, Pallas kernels for 0%

commit v1 on v0

v1 whole, which is shorter than its diff:
```python
import functools
import math

import jax
import jax.numpy as jnp
from jax import lax
from jax.experimental import pallas as pl
from jax.experimental.pallas import tpu as pltpu
from jax.sharding import PartitionSpec as P

HEADS = 8
HD = 512
BLK = 512
EPS = 1e-06
NEG = -1e30
VMEM_LIMIT = 56 * 1024 * 1024
F32 = jnp.float32
BF16 = jnp.bfloat16

ZQ, XY = 4, 8


def move_xor(value, mask):
    n = lax.axis_size("seq")
    return lax.ppermute(value, "seq", [(i, i ^ mask) for i in range(n)])


def shift(value, step):
    n = lax.axis_size("seq")
    return lax.ppermute(value, "seq", [(i, (i + step) % n) for i in range(n)])


def dot(a, b):
    return lax.dot_general(a, b, (((1,), (0,)), ((), ())), preferred_element_type=F32)


def dot_rows(a, b):
    return lax.dot_general(a, b, (((0,), (0,)), ((), ())), preferred_element_type=F32)


def dot_cols(a, b):
    return lax.dot_general(a, b, (((1,), (1,)), ((), ())), preferred_element_type=F32)


def whole(shape):
    rank = len(shape)
    return pl.BlockSpec(shape, lambda i, s: (0,) * rank)


def head_block(pick):
    return pl.BlockSpec((BLK, HD), lambda i, s: (0, s[pick]))


def call(kernel, scalars, ins, in_specs, outs, scratch=(), flops=0):
    multi = isinstance(outs, list)
    out_list = outs if multi else [outs]
    nbytes = sum(a.size * a.dtype.itemsize for a in ins)
    specs = [whole(o.shape) for o in out_list]
    return pl.pallas_call(
        kernel,
        out_shape=outs,
        grid_spec=pltpu.PrefetchScalarGridSpec(
            num_scalar_prefetch=1,
            grid=(1,),
            in_specs=in_specs,
            out_specs=specs if multi else specs[0],
            scratch_shapes=list(scratch),
        ),
        compiler_params=pltpu.CompilerParams(vmem_limit_bytes=VMEM_LIMIT),
        cost_estimate=pl.CostEstimate(flops=flops, transcendentals=0, bytes_accessed=nbytes),
    )(scalars, *ins)


def row_start(s_ref, index):
    return pl.multiple_of(s_ref[index], 16)


def fill_rows(s_ref, blocks, rows_ref):
    for j, block in enumerate(blocks):
        for k in range(ZQ):
            at = pl.multiple_of(row_start(s_ref, 4 + j) + row_start(s_ref, 12 + k), 16)
            for m in range(3):
                rows_ref[m, pl.ds(at, 16), :] = block[k, m]


def columns_sq(rows_ref, m):
    w = rows_ref[m].astype(F32)
    return jnp.sum(w * w, axis=0, keepdims=True)


def as_column(row):
    return jnp.broadcast_to(row, (128, row.shape[1])).T


def gradient_kernel(s_ref, halo, k_own, v_own, rate_prev, rate_own, *rest):
    blocks, rest = rest[:XY], rest[XY:]
    own_out, outs, old_sq = rest[0], rest[1:XY], rest[XY]
    w_rows, k_all, gv, hid, d_gate, d_up, grads = rest[XY + 1:]
    fill_rows(s_ref, blocks, w_rows)
    for m in range(3):
        old_sq[m:m + 1, :] = columns_sq(w_rows, m)
    for part in range(2):
        rows = slice(part * BLK, (part + 1) * BLK)
        k = halo[0] if part == 0 else k_own[...]
        v = (halo[1] if part == 0 else v_own[...]).astype(F32)
        eta = as_column((rate_prev if part == 0 else rate_own)[0:1, :])
        scaled = jnp.concatenate(
            [eta * v[:, c * 128:(c + 1) * 128] for c in range(HD // 128)], axis=1
        ).astype(BF16)
        k_all[rows, :] = k
        gv[rows, :] = scaled
        pre_a = dot(k, w_rows[0])
        pre_b = dot(k, w_rows[1])
        back = dot_cols(scaled, w_rows[2])
        sigma = jax.nn.sigmoid(pre_a)
        gated = pre_a * sigma
        hid[rows, :] = (gated * pre_b).astype(BF16)
        d_gate[rows, :] = (back * pre_b * sigma * (1.0 + pre_a * (1.0 - sigma))).astype(BF16)
        d_up[rows, :] = (back * gated).astype(BF16)
    grads[0] = dot_rows(k_all[...], d_gate[...])
    grads[1] = dot_rows(k_all[...], d_up[...])
    grads[2] = dot_rows(hid[...], gv[...])
    for m in range(3):
        own_out[m] = grads[m, pl.ds(row_start(s_ref, 4), 64), :]
        for j, out in enumerate(outs):
            out[m] = grads[m, pl.ds(row_start(s_ref, 5 + j), 64), :].astype(BF16)


def block_sum_kernel(s_ref, own, *rest):
    parts, outs, total = rest[:XY - 1], rest[XY - 1:XY - 1 + ZQ], rest[-1]
    acc = own[...]
    for part in parts:
        acc = acc + part[...].astype(F32)
    total[...] = acc
    for m in range(3):
        for k, out in enumerate(outs):
            out[m] = total[m, pl.ds(row_start(s_ref, 12 + k), 16), :].astype(out.dtype)


def update_kernel(s_ref, own, one, two, three, w_own, upd, upd_b):
    total = own[...] + one[...].astype(F32) + two[...].astype(F32) + three[...].astype(F32)
    total = total + w_own[...]
    upd[...] = total
    upd_b[...] = total.astype(BF16)


def apply_kernel(s_ref, q_prev, q_own, old_sq, upd, *rest):
    blocks, rest = rest[:XY], rest[XY:]
    f_prev, f_own, sq, new, u_rows = rest
    fill_rows(s_ref, blocks, u_rows)
    ratio = [
        jnp.sqrt(old_sq[m:m + 1, :]) / jnp.sqrt(columns_sq(u_rows, m) + EPS) for m in range(3)
    ]
    for m in range(3):
        new[m] = upd[m] * ratio[m]
    for part, (q, out) in enumerate(((q_prev, f_prev), (q_own, f_own))):
        pre_a = dot(q[...], u_rows[0]) * ratio[0]
        pre_b = dot(q[...], u_rows[1]) * ratio[1]
        hid = (pre_a * jax.nn.sigmoid(pre_a) * pre_b).astype(BF16)
        branch = dot(hid, u_rows[2]) * ratio[2]
        out[...] = branch.astype(BF16)
        squares = branch * branch
        lanes = sum(squares[:, c * 128:(c + 1) * 128] for c in range(HD // 128))
        sq[part:part + 1, :] = jnp.sum(lanes.T, axis=0, keepdims=True)


def attention_kernel(s_ref, q_ref, k_ref, v_ref, halo, out):
    scale = 1.0 / math.sqrt(HD)
    first = s_ref[2] == 0
    half = BLK // 2
    for part in range(2):
        base = part * half
        q = q_ref[base:base + half, :]
        own_len = base + half
        prev_len = BLK - base
        s_prev = dot_cols(q, halo[0, base:, :]) * scale
        s_own = dot_cols(q, k_ref[:own_len, :]) * scale
        row_p = lax.broadcasted_iota(jnp.int32, (half, prev_len), 0)
        col_p = lax.broadcasted_iota(jnp.int32, (half, prev_len), 1)
        keep_p = jnp.logical_and(col_p > row_p, jnp.logical_not(first))
        row_o = lax.broadcasted_iota(jnp.int32, (half, own_len), 0) + base
        col_o = lax.broadcasted_iota(jnp.int32, (half, own_len), 1)
        s_prev = jnp.where(keep_p, s_prev, NEG)
        s_own = jnp.where(col_o <= row_o, s_own, NEG)
        top = jnp.maximum(
            jnp.max(s_prev, axis=1, keepdims=True), jnp.max(s_own, axis=1, keepdims=True)
        )
        e_prev = jnp.exp(s_prev - top)
        e_own = jnp.exp(s_own - top)
        inv = 1.0 / (
            jnp.sum(e_prev, axis=1, keepdims=True) + jnp.sum(e_own, axis=1, keepdims=True)
        )
        p_prev = (e_prev * inv).astype(BF16)
        p_own = (e_own * inv).astype(BF16)
        out[base:base + half, :] = dot(p_prev, halo[1, base:, :]) + dot(p_own, v_ref[:own_len, :])


def mix_kernel(s_ref, f_own, f_back, attn_own, attn_other, sums, gain, out):
    inv = as_column(lax.rsqrt(sums[0:1, :] / (HEADS * HD) + EPS))
    for own_head in range(2):

        @pl.when(s_ref[0] == own_head)
        def _():
            for head in range(2):
                f, attn = (f_own, attn_own) if head == own_head else (f_back, attn_other)
                for c in range(HD // 128):
                    cols = slice(c * 128, (c + 1) * 128)
                    to = slice(head * HD + c * 128, head * HD + (c + 1) * 128)
                    branch = f[:, cols].astype(F32) * inv * gain[0:1, to]
                    out[:, to] = (attn[:, cols] + branch).astype(BF16)


def shape(dims, dtype):
    return jax.ShapeDtypeStruct(dims, dtype)


def local(queries, keys, values, rate, fast_gate, fast_up, fast_down, out_gain):
    seq_pos = lax.axis_index("seq").astype(jnp.int32)
    own = seq_pos & 1
    other = 1 - own
    zq = (seq_pos >> 1) & (ZQ - 1)
    xy = seq_pos >> 3
    scalars = jnp.stack(
        [own, other, seq_pos, seq_pos * 0]
        + [64 * (xy ^ j) for j in range(XY)]
        + [16 * (zq ^ k) for k in range(ZQ)]
    ).astype(jnp.int32)
    even = own == 0

    def head_of(array, want_own):
        flag = even if want_own else jnp.logical_not(even)
        return jnp.where(flag, array[:, :HD], array[:, HD:])

    fast = jnp.stack([fast_gate, fast_up, fast_down])
    mine = jnp.where(even, fast[:, 0], fast[:, 1])
    theirs = jnp.where(even, fast[:, 1], fast[:, 0])
    got = move_xor(theirs, 1)
    w_pair = jnp.where(
        even, jnp.concatenate([mine, got], axis=1), jnp.concatenate([got, mine], axis=1)
    )

    halo_send = jnp.stack([head_of(keys, False), head_of(values, False)])
    rate_send = jnp.where(even, rate[1:2], rate[0:1])
    rate_mine = jnp.where(even, rate[0:1], rate[1:2])

    def gather_blocks(chunk):
        block = jnp.stack([chunk] + [move_xor(chunk, k << 1) for k in range(1, ZQ)])
        return [block] + [move_xor(block, j << 3) for j in range(1, XY)]

    w_blocks = gather_blocks(w_pair.astype(BF16))
    halo = shift(halo_send, 1)
    rate_prev = shift(rate_send, 1)

    block_specs = [whole((ZQ, 3, 16, HD))] * XY
    grad_out = call(
        gradient_kernel,
        scalars,
        [halo, keys, values, rate_prev, rate_mine] + w_blocks,
        [whole((2, BLK, HD)), head_block(0), head_block(0), whole((1, BLK)), whole((1, BLK))]
        + block_specs,
        [shape((3, 64, HD), F32)] + [shape((3, 64, HD), BF16)] * (XY - 1) + [shape((3, HD), F32)],
        [pltpu.VMEM((3, HD, HD), BF16)]
        + [pltpu.VMEM((2 * BLK, HD), BF16)] * 5
        + [pltpu.VMEM((3, HD, HD), F32)],
        flops=12 * 2 * BLK * HD * HD,
    )
    old_sq = grad_out[XY]
    arrived = [move_xor(grad_out[j], j << 3) for j in range(1, XY)]
    chunks = call(
        block_sum_kernel,
        scalars,
        [grad_out[0]] + arrived,
        [whole((3, 64, HD))] * XY,
        [shape((3, 16, HD), F32)] + [shape((3, 16, HD), BF16)] * (ZQ - 1),
        [pltpu.VMEM((3, 64, HD), F32)],
    )
    arrived = [move_xor(chunks[k], k << 1) for k in range(1, ZQ)]
    upd, upd_b = call(
        update_kernel,
        scalars,
        [chunks[0]] + arrived + [w_pair],
        [whole((3, 16, HD))] * 5,
        [shape((3, 16, HD), F32), shape((3, 16, HD), BF16)],
    )
    u_blocks = gather_blocks(upd_b)

    halo_other = shift(jnp.stack([head_of(keys, True), head_of(values, True)]), 1)
    q_prev = shift(head_of(queries, False), 1)

    def attend(pick, prev):
        return call(
            attention_kernel,
            scalars,
            [queries, keys, values, prev],
            [head_block(pick)] * 3 + [whole((2, BLK, HD))],
            shape((BLK, HD), F32),
            flops=4 * BLK * 768 * HD,
        )

    attn_own = attend(0, halo)
    attn_other = attend(1, halo_other)

    f_prev, f_own, sq, new = call(
        apply_kernel,
        scalars,
        [q_prev, queries, old_sq, upd] + u_blocks,
        [whole((BLK, HD)), head_block(0), whole((3, HD)), whole((3, 16, HD))] + block_specs,
        [
            shape((BLK, HD), BF16),
            shape((BLK, HD), BF16),
            shape((2, BLK), F32),
            shape((3, 16, HD), F32),
        ],
        [pltpu.VMEM((3, HD, HD), BF16)],
        flops=6 * 2 * BLK * HD * HD,
    )
    f_back = shift(f_prev, -1)
    heads = lax.axis_size("head")
    totals = sq
    for k in range(1, heads):
        totals = totals + lax.ppermute(sq, "head", [(i, i ^ k) for i in range(heads)])
    sums = totals[1:2] + shift(totals[0:1], -1)
    new_mine = jnp.where(even, new[:, :8], new[:, 8:])
    new_theirs = move_xor(jnp.where(even, new[:, 8:], new[:, :8]), 1)
    new_all = jnp.where(
        even,
        jnp.stack([new_mine, new_theirs], axis=1),
        jnp.stack([new_theirs, new_mine], axis=1),
    )
    mixed = call(
        mix_kernel,
        scalars,
        [f_own, f_back, attn_own, attn_other, sums, out_gain.reshape(1, 2 * HD)],
        [whole((BLK, HD))] * 4 + [whole((1, BLK)), whole((1, 2 * HD))],
        shape((BLK, 2 * HD), BF16),
    )
    return mixed, new_all[0], new_all[1], new_all[2]


def solution(mesh):
    tokens = P("seq", "head")
    fast = P("head", "seq", None)
    return jax.shard_map(
        local,
        mesh=mesh,
        in_specs=(tokens, tokens, tokens, P("head", "seq"), fast, fast, fast, P("head")),
        out_specs=(tokens, fast, fast, fast),
        check_vma=False,
    )
```

time: 1580 us -> 220 us (0.14)
  waiting for transfers between devices: 1440 us -> 91.6 us
  starting transfers between devices: 5.95 us -> 82.2 us
  blocking collectives: 52.7 us -> 0 us
  Pallas kernels: 0 us -> 32.3 us
  matrix products: 26.6 us -> 0 us
  local copies, waits for them, and re-layouts: 28.4 us -> 6.84 us
    all_gather x3 -> x0, waiting for transfers between devices: 841 us -> none  [the longest x1 297 us: local(): lax.all_gather(fast_up, 'seq', axis=1, tiled=True)]
    psum x1 -> x0, waiting for transfers between devices: 583 us -> none  [local(): lax.psum((grad_one, grad_three, grad_two), 'seq')]
    ppermute x2 -> x41, waiting for transfers between devices: 13.6 us -> 91.6 us  [the longest x32 76.4 us: move_xor(): return lax.ppermute(value, 'seq', [(i, i ^ mask) for i in range(n)])]
    ppermute x2 -> x41, starting transfers between devices: 5.79 us -> 82.2 us  [the longest x32 49.9 us: move_xor(): return lax.ppermute(value, 'seq', [(i, i ^ mask) for i in range(n)])]
    psum x1 -> x0, blocking collectives: 52.7 us -> none  [local(): total_sq = lax.psum(local_sq, 'head')]
    pallas_call x0 -> x7, Pallas kernels: none -> 32.3 us  [call(): pl.pallas_call(kernel, out_shape=outs, grid_spec=pltpu.PrefetchScalarGrid...]
    dot_general x10 -> x0, matrix products: 26.6 us -> none  [the longest x1 5.39 us: local(): jnp.einsum('thf,hfd->thd', apply_h, use_two, preferred_element_type=jnp.f...]
  transfers between devices with their start and end apart: 6 -> 41, of which waited for: 6 -> 17; matrix products, arithmetic and copies ran while one was open for 2% -> 2% of each run, Pallas kernels for 0% -> 9%
where the time goes in v1:
time: 220 us; the launch traced here: 219 us
  waiting for transfers between devices  91.6 us (42%)
  starting transfers between devices  82.2 us (37%)
  Pallas kernels  32.3 us (15%)
  local copies, waits for them, and re-layouts  6.84 us (3%)
  other arithmetic  4.64 us (2%)
    ppermute x32, waiting for transfers between devices, move_xor(): return lax.ppermute(value, 'seq', [(i, i ^ mask) for i in range(n)])  76.4 us
    ppermute x32, starting transfers between devices, move_xor(): return lax.ppermute(value, 'seq', [(i, i ^ mask) for i in range(n)])  49.9 us
    pallas_call x7, Pallas kernels, call(): pl.pallas_call(kernel, out_shape=outs, grid_spec=pltpu.PrefetchScalarGrid...  32.3 us
    ppermute x3, starting transfers between devices, local(): lax.ppermute(sq, 'head', [(i, i ^ k) for i in range(heads)])  21.2 us
    ppermute x6, waiting for transfers between devices, shift(): return lax.ppermute(value, 'seq', [(i, (i + step) % n) for i in range(n)])  15.2 us
    ppermute x6, starting transfers between devices, shift(): return lax.ppermute(value, 'seq', [(i, (i + step) % n) for i in range(n)])  11 us
    unnamed x78, local copies, waits for them, and re-layouts  5.58 us
  transfers between devices with their start and end apart: 41, of which 17 were waited for; matrix products, arithmetic and copies ran while one was open for 2% of the time, Pallas kernels for 9%

profile of v1, /device:TPU:1, one launch (start us, length us, event | category | flops | bytes accessed | tf_op | source)
XLA Modules:
  0.0 218.6 jit_solution(17330032483030577735)
XLA Ops:
  2.4 2.5 %collective-permute-start.1 = (bf16[2,512,512]{2,1,0:T(8,128)(2,1)S(1)}, bf16[2,512,512]{2,1,0:T(8,128)(2,1)S(1)}, u32[]{:S(2)}, u32[]{:S(2)}) collective-permute-start(bf16[2,512,512]{2,1,0:T(8,128)(2,1)S(1)} %pad_maximum_fusion), channel_id=1, source_target_pairs={{0,1},{1,2},{2,3},{3,4},{4,5},{5,6},{6,7},{7,8},{8,9},{9,10},{10,1... | collective-permute-start | bytes 3145736 | tf_op jit(solution)/shard_map/ppermute | solution.py:30
  6.8 21.1 %collective-permute-done.3 = f32[3,8,512]{2,1,0:T(8,128)S(1)} collective-permute-done((f32[3,8,512]{2,1,0:T(8,128)S(1)}, f32[3,8,512]{2,1,0:T(8,128)S(1)}, u32[]{:S(2)}, u32[]{:S(2)}) %collective-permute-start.3) | collective-permute-done | bytes 49184 | tf_op jit(solution)/shard_map/ppermute | solution.py:25
  28.5 3.0 %collective-permute-start.4 = (bf16[3,16,512]{2,1,0:T(8,128)(2,1)S(1)}, bf16[3,16,512]{2,1,0:T(8,128)(2,1)S(1)}, u32[]{:S(2)}, u32[]{:S(2)}) collective-permute-start(bf16[3,16,512]{2,1,0:T(8,128)(2,1)S(1)} %get-tuple-element.42), channel_id=1, source_target_pairs={{0,2},{1,3},{2,0},{3,1},{4,6},{5,7},{6,4},{7,5},{8,10},{9,11},{10,... | collective-permute-start | bytes 147464 | tf_op jit(solution)/shard_map/ppermute | solution.py:25
  31.5 4.2 %collective-permute-start.5 = (bf16[3,16,512]{2,1,0:T(8,128)(2,1)S(1)}, bf16[3,16,512]{2,1,0:T(8,128)(2,1)S(1)}, u32[]{:S(2)}, u32[]{:S(2)}) collective-permute-start(bf16[3,16,512]{2,1,0:T(8,128)(2,1)S(1)} %get-tuple-element.42), channel_id=1, source_target_pairs={{0,4},{1,5},{2,6},{3,7},{4,0},{5,1},{6,2},{7,3},{8,12},{9,13},{10,... | collective-permute-start | bytes 147464 | tf_op jit(solution)/shard_map/ppermute | solution.py:25
  35.7 2.8 %collective-permute-done.5 = bf16[3,16,512]{2,1,0:T(8,128)(2,1)S(1)} collective-permute-done((bf16[3,16,512]{2,1,0:T(8,128)(2,1)S(1)}, bf16[3,16,512]{2,1,0:T(8,128)(2,1)S(1)}, u32[]{:S(2)}, u32[]{:S(2)}) %collective-permute-start.5) | collective-permute-done | bytes 49184 | tf_op jit(solution)/shard_map/ppermute | solution.py:25
  38.5 2.7 %collective-permute-done.6 = bf16[3,16,512]{2,1,0:T(8,128)(2,1)S(1)} collective-permute-done((bf16[3,16,512]{2,1,0:T(8,128)(2,1)S(1)}, bf16[3,16,512]{2,1,0:T(8,128)(2,1)S(1)}, u32[]{:S(2)}, u32[]{:S(2)}) %collective-permute-start.6) | collective-permute-done | bytes 49184 | tf_op jit(solution)/shard_map/ppermute | solution.py:25
  41.3 2.8 %collective-permute-start.10 = (bf16[4,3,16,512]{3,2,1,0:T(8,128)(2,1)S(1)}, bf16[4,3,16,512]{3,2,1,0:T(8,128)(2,1)S(1)}, u32[]{:S(2)}, u32[]{:S(2)}) collective-permute-start(bf16[4,3,16,512]{3,2,1,0:T(8,128)(2,1)S(1)} %pad_maximum_fusion.2.rest_0_), channel_id=1, source_target_pairs={{0,32},{1,33},{2,34},{3,35},{4,36},{5,37},{6,38},{7,39},{8,40},{9,... | collective-permute-start | bytes 589832 | tf_op jit(solution)/shard_map/ppermute | solution.py:25
  45.4 2.5 %collective-permute-start.12 = (bf16[4,3,16,512]{3,2,1,0:T(8,128)(2,1)S(1)}, bf16[4,3,16,512]{3,2,1,0:T(8,128)(2,1)S(1)}, u32[]{:S(2)}, u32[]{:S(2)}) collective-permute-start(bf16[4,3,16,512]{3,2,1,0:T(8,128)(2,1)S(1)} %pad_maximum_fusion.2.rest_0_), channel_id=1, source_target_pairs={{0,48},{1,49},{2,50},{3,51},{4,52},{5,53},{6,54},{7,55},{8,56},{9,... | collective-permute-start | bytes 589832 | tf_op jit(solution)/shard_map/ppermute | solution.py:25
  50.3 4.8 %collective-permute-done.2.rate_prev = f32[1,512]{1,0:T(1,128)S(1)} collective-permute-done((f32[1,512]{1,0:T(1,128)S(1)}, f32[1,512]{1,0:T(1,128)S(1)}, u32[]{:S(2)}, u32[]{:S(2)}) %collective-permute-start.2) | collective-permute-done | bytes 2080 | tf_op jit(solution)/shard_map/ppermute | solution.py:30
  55.4 3.8 %collective-permute-done.12.rest_6_ = bf16[4,3,16,512]{3,2,1,0:T(8,128)(2,1)S(1)} collective-permute-done((bf16[4,3,16,512]{3,2,1,0:T(8,128)(2,1)S(1)}, bf16[4,3,16,512]{3,2,1,0:T(8,128)(2,1)S(1)}, u32[]{:S(2)}, u32[]{:S(2)}) %collective-permute-start.12) | collective-permute-done | bytes 196640 | tf_op jit(solution)/shard_map/ppermute | solution.py:25
  62.0 5.2 %collective-permute-done.9.rest_3_ = bf16[4,3,16,512]{3,2,1,0:T(8,128)(2,1)} collective-permute-done((bf16[4,3,16,512]{3,2,1,0:T(8,128)(2,1)S(1)}, bf16[4,3,16,512]{3,2,1,0:T(8,128)(2,1)}, u32[]{:S(2)}, u32[]{:S(2)}) %collective-permute-start.9) | collective-permute-done | bytes 196640 | tf_op jit(solution)/shard_map/ppermute | solution.py:25
  68.2 8.2 %shard_map.111 = (f32[3,64,512]{2,1,0:T(8,128)}, bf16[3,64,512]{2,1,0:T(8,128)(2,1)}, bf16[3,64,512]{2,1,0:T(8,128)(2,1)}, bf16[3,64,512]{2,1,0:T(8,128)(2,1)}, ...) custom-call(s32[16]{0:T(128)} %stack.135.s_ref, ...), custom_call_target="tpu_custom_call" | custom-call | flops 3221225472 | bytes 4722688 | tf_op jit(solution)/shard_map/pallas_call | solution.py:59
  81.5 2.2 %collective-permute-start.17 = (bf16[3,64,512]{2,1,0:T(8,128)(2,1)S(1)}, bf16[3,64,512]{2,1,0:T(8,128)(2,1)S(1)}, u32[]{:S(2)}, u32[]{:S(2)}) collective-permute-start(bf16[3,64,512]{2,1,0:T(8,128)(2,1)S(1)} %copy-done.30), channel_id=1, source_target_pairs={{0,32},{1,33},{2,34},{3,35},{4,36},{5,37},{6,38},{7,39},{8,40},{9,... | collective-permute-start | bytes 589832 | tf_op jit(solution)/shard_map/ppermute | solution.py:25
  85.4 2.2 %collective-permute-start.19 = (bf16[3,64,512]{2,1,0:T(8,128)(2,1)S(1)}, bf16[3,64,512]{2,1,0:T(8,128)(2,1)S(1)}, u32[]{:S(2)}, u32[]{:S(2)}) collective-permute-start(bf16[3,64,512]{2,1,0:T(8,128)(2,1)S(1)} %copy-done.28), channel_id=1, source_target_pairs={{0,48},{1,49},{2,50},{3,51},{4,52},{5,53},{6,54},{7,55},{8,56},{9,... | collective-permute-start | bytes 589832 | tf_op jit(solution)/shard_map/ppermute | solution.py:25
  90.4 3.4 %collective-permute-start = (bf16[512,512]{1,0:T(8,128)(2,1)S(1)}, bf16[512,512]{1,0:T(8,128)(2,1)S(1)}, u32[]{:S(2)}, u32[]{:S(2)}) collective-permute-start(bf16[512,512]{1,0:T(8,128)(2,1)S(1)} %slice_select_fusion), channel_id=1, source_target_pairs={{0,1},{1,2},{2,3},{3,4},{4,5},{5,6},{6,7},{7,8},{8,9},{9,10},{10,1... | collective-permute-start | bytes 1572872 | tf_op jit(solution)/shard_map/ppermute | solution.py:30
  93.8 28.9 %collective-permute-done.18.rest_4_ = bf16[3,64,512]{2,1,0:T(8,128)(2,1)S(1)} collective-permute-done((bf16[3,64,512]{2,1,0:T(8,128)(2,1)S(1)}, bf16[3,64,512]{2,1,0:T(8,128)(2,1)S(1)}, u32[]{:S(2)}, u32[]{:S(2)}) %collective-permute-start.18) | collective-permute-done | bytes 196640 | tf_op jit(solution)/shard_map/ppermute | solution.py:25
  123.6 3.1 %shard_map.112 = (f32[3,16,512]{2,1,0:T(8,128)}, bf16[3,16,512]{2,1,0:T(8,128)(2,1)}, bf16[3,16,512]{2,1,0:T(8,128)(2,1)}, bf16[3,16,512]{2,1,0:T(8,128)(2,1)}) custom-call(s32[16]{0:T(128)} %stack.135.s_ref, f32[3,64,512]{2,1,0:T(8,128)} %get-tuple-element.24.own, bf16[3,64,512]{2,1,0:T(8,128)(2,1)} %copy-done.6, bf16[3,64,512]{2,1,0:T(8,128)(2,1)} %copy-done.7, ...), custom_call_target="tpu_custom_call" | custom-call | bytes 1769472 | tf_op jit(solution)/shard_map/pallas_call | solution.py:59
  126.8 5.6 %collective-permute-start.23 = (bf16[3,16,512]{2,1,0:T(8,128)(2,1)}, bf16[3,16,512]{2,1,0:T(8,128)(2,1)S(1)}, u32[]{:S(2)}, u32[]{:S(2)}) collective-permute-start(bf16[3,16,512]{2,1,0:T(8,128)(2,1)} %get-tuple-element.35), channel_id=1, source_target_pairs={{0,6},{1,7},{2,4},{3,5},{4,2},{5,3},{6,0},{7,1},{8,14},{9,15},{10,... | collective-permute-start | bytes 147464 | tf_op jit(solution)/shard_map/ppermute | solution.py:25
  132.4 2.2 %collective-permute-done.22.two = bf16[3,16,512]{2,1,0:T(8,128)(2,1)S(1)} collective-permute-done((bf16[3,16,512]{2,1,0:T(8,128)(2,1)}, bf16[3,16,512]{2,1,0:T(8,128)(2,1)S(1)}, u32[]{:S(2)}, u32[]{:S(2)}) %collective-permute-start.22) | collective-permute-done | bytes 49184 | tf_op jit(solution)/shard_map/ppermute | solution.py:25
  136.1 2.4 %shard_map.113 = (f32[3,16,512]{2,1,0:T(8,128)}, bf16[3,16,512]{2,1,0:T(8,128)(2,1)}) custom-call(s32[16]{0:T(128)} %stack.135.s_ref, f32[3,16,512]{2,1,0:T(8,128)} %get-tuple-element.32.own, bf16[3,16,512]{2,1,0:T(8,128)(2,1)} %copy-done.14, bf16[3,16,512]{2,1,0:T(8,128)(2,1)} %copy-done.15, bf16[3,16,512]{2,1,0:T(8,128)(2,1)} %copy-done.16, ...), custom_call_target="tpu_custom_call" | custom-call | bytes 344064 | tf_op jit(solution)/shard_map/pallas_call | solution.py:59
  139.9 2.9 %collective-permute-start.25 = (bf16[3,16,512]{2,1,0:T(8,128)(2,1)}, bf16[3,16,512]{2,1,0:T(8,128)(2,1)S(1)}, u32[]{:S(2)}, u32[]{:S(2)}) collective-permute-start(bf16[3,16,512]{2,1,0:T(8,128)(2,1)} %get-tuple-element.37), channel_id=1, source_target_pairs={{0,4},{1,5},{2,6},{3,7},{4,0},{5,1},{6,2},{7,3},{8,12},{9,13},{10,... | collective-permute-start | bytes 147464 | tf_op jit(solution)/shard_map/ppermute | solution.py:25
  144.1 2.9 %collective-permute-done.25 = bf16[3,16,512]{2,1,0:T(8,128)(2,1)S(1)} collective-permute-done((bf16[3,16,512]{2,1,0:T(8,128)(2,1)}, bf16[3,16,512]{2,1,0:T(8,128)(2,1)S(1)}, u32[]{:S(2)}, u32[]{:S(2)}) %collective-permute-start.25) | collective-permute-done | bytes 49184 | tf_op jit(solution)/shard_map/ppermute | solution.py:25
  149.3 2.5 %collective-permute-start.29 = (bf16[4,3,16,512]{3,2,1,0:T(8,128)(2,1)S(1)}, bf16[4,3,16,512]{3,2,1,0:T(8,128)(2,1)S(1)}, u32[]{:S(2)}, u32[]{:S(2)}) collective-permute-start(bf16[4,3,16,512]{3,2,1,0:T(8,128)(2,1)S(1)} %pad_maximum_fusion.3.rest_0_), channel_id=1, source_target_pairs={{0,24},{1,25},{2,26},{3,27},{4,28},{5,29},{6,30},{7,31},{8,16},{9,... | collective-permute-start | bytes 589832 | tf_op jit(solution)/shard_map/ppermute | solution.py:25
  151.8 2.6 %collective-permute-start.30 = (bf16[4,3,16,512]{3,2,1,0:T(8,128)(2,1)S(1)}, bf16[4,3,16,512]{3,2,1,0:T(8,128)(2,1)S(1)}, u32[]{:S(2)}, u32[]{:S(2)}) collective-permute-start(bf16[4,3,16,512]{3,2,1,0:T(8,128)(2,1)S(1)} %pad_maximum_fusion.3.rest_0_), channel_id=1, source_target_pairs={{0,32},{1,33},{2,34},{3,35},{4,36},{5,37},{6,38},{7,39},{8,40},{9,... | collective-permute-start | bytes 589832 | tf_op jit(solution)/shard_map/ppermute | solution.py:25
  157.0 2.9 %collective-permute-start.33 = (bf16[4,3,16,512]{3,2,1,0:T(8,128)(2,1)S(1)}, bf16[4,3,16,512]{3,2,1,0:T(8,128)(2,1)S(1)}, u32[]{:S(2)}, u32[]{:S(2)}) collective-permute-start(bf16[4,3,16,512]{3,2,1,0:T(8,128)(2,1)S(1)} %pad_maximum_fusion.3.rest_0_), channel_id=1, source_target_pairs={{0,56},{1,57},{2,58},{3,59},{4,60},{5,61},{6,62},{7,63},{8,48},{9,... | collective-permute-start | bytes 589832 | tf_op jit(solution)/shard_map/ppermute | solution.py:25
  159.9 4.7 %shard_map.115.attn_own = f32[512,512]{1,0:T(8,128)} custom-call(s32[16]{0:T(128)} %stack.135.s_ref, bf16[512,1024]{1,0:T(8,128)(2,1)} %q_ref.3, bf16[512,1024]{1,0:T(8,128)(2,1)} %k_ref.3, bf16[512,1024]{1,0:T(8,128)(2,1)} %v_ref.3, bf16[2,512,512]{2,1,0:T(8,128)(2,1)} %copy-done.1), custom_call_target="tpu_custom_call" | custom-call | flops 805306368 | bytes 4194304 | tf_op jit(solution)/shard_map/pallas_call | solution.py:59
  167.2 5.2 %shard_map.114 = (bf16[512,512]{1,0:T(8,128)(2,1)}, bf16[512,512]{1,0:T(8,128)(2,1)}, f32[2,512]{1,0:T(2,128)}, f32[3,16,512]{2,1,0:T(8,128)}) custom-call(s32[16]{0:T(128)} %stack.135.s_ref, bf16[512,512]{1,0:T(8,128)(2,1)} %copy-done.22, bf16[512,1024]{1,0:T(8,128)(2,1)} %q_ref.3, f32[3,512]{1,0:T(4,128)} %get-tuple-element.23.old_sq, ...), custom_call_target="tpu_custom_call" | custom-call | flops 1610612736 | bytes 3250176 | tf_op jit(solution)/shard_map/pallas_call | solution.py:59
  172.4 18.0 %collective-permute-start.36 = (f32[2,512]{1,0:T(2,128)}, f32[2,512]{1,0:T(2,128)S(1)}, u32[]{:S(2)}, u32[]{:S(2)}) collective-permute-start(f32[2,512]{1,0:T(2,128)} %get-tuple-element.40), channel_id=1, source_target_pairs={{0,64},{64,0},{128,192},{192,128},{1,65},{65,1},{129,193},{193,129... | collective-permute-start | bytes 12296 | tf_op jit(solution)/shard_map/ppermute | solution.py:321
  190.4 2.5 %collective-permute-start.37 = (f32[2,512]{1,0:T(2,128)}, f32[2,512]{1,0:T(2,128)S(1)}, u32[]{:S(2)}, u32[]{:S(2)}) collective-permute-start(f32[2,512]{1,0:T(2,128)} %get-tuple-element.40), channel_id=1, source_target_pairs={{0,128},{64,192},{128,0},{192,64},{1,129},{65,193},{129,1},{193,65... | collective-permute-start | bytes 12296 | tf_op jit(solution)/shard_map/ppermute | solution.py:321
  194.6 4.7 %shard_map.116.attn_other = f32[512,512]{1,0:T(8,128)} custom-call(s32[16]{0:T(128)} %stack.135.s_ref, bf16[512,1024]{1,0:T(8,128)(2,1)} %q_ref.3, bf16[512,1024]{1,0:T(8,128)(2,1)} %k_ref.3, bf16[512,1024]{1,0:T(8,128)(2,1)} %v_ref.3, bf16[2,512,512]{2,1,0:T(8,128)(2,1)} %copy-done.2), custom_call_target="tpu_custom_call" | custom-call | flops 805306368 | bytes 4194304 | tf_op jit(solution)/shard_map/pallas_call | solution.py:59
  203.4 10.3 %collective-permute-done.34.f_back = bf16[512,512]{1,0:T(8,128)(2,1)S(1)} collective-permute-done((bf16[512,512]{1,0:T(8,128)(2,1)S(1)}, bf16[512,512]{1,0:T(8,128)(2,1)S(1)}, u32[]{:S(2)}, u32[]{:S(2)}) %collective-permute-start.34) | collective-permute-done | bytes 524320 | tf_op jit(solution)/shard_map/ppermute | solution.py:30
  214.5 4.0 %shard_map.117 = bf16[512,1024]{1,0:T(8,128)(2,1)} custom-call(s32[16]{0:T(128)} %stack.135.s_ref, bf16[512,512]{1,0:T(8,128)(2,1)} %get-tuple-element.38.f_own, bf16[512,512]{1,0:T(8,128)(2,1)} %copy-done.3, f32[512,512]{1,0:T(8,128)} %shard_map.115.attn_own, f32[512,512]{1,0:T(8,128)} %shard_map.116.attn_other, f32[1,512]{1,0:T(1,128)} %slice_add_fusion.sums, ...), custom_call_target="tpu_custom_call" | custom-call | bytes 3151872 | tf_op jit(solution)/shard_map/pallas_call | solution.py:59
  (154 shorter events, 40.4 us)
Async XLA Ops:
  2.4 64.8 %collective-permute-start.1 = (bf16[2,512,512]{2,1,0:T(8,128)(2,1)S(1)}, bf16[2,512,512]{2,1,0:T(8,128)(2,1)S(1)}, u32[]{:S(2)}, u32[]{:S(2)}) collective-permute-start(bf16[2,512,512]{2,1,0:T(8,128)(2,1)S(1)} %pad_maximum_fusion), channel_id=1, source_target_pairs={{0,1},{1,2},{2,3},{3,4},{4,5},{5,6},{6,7},{7,8},{8,9},{9,10},{10,1... | collective-permute-start | bytes 3145736 | tf_op jit(solution)/shard_map/ppermute | solution.py:30
  5.0 22.8 %collective-permute-start.3 = (f32[3,8,512]{2,1,0:T(8,128)S(1)}, f32[3,8,512]{2,1,0:T(8,128)S(1)}, u32[]{:S(2)}, u32[]{:S(2)}) collective-permute-start(f32[3,8,512]{2,1,0:T(8,128)S(1)} %get-tuple-element.53), channel_id=1, source_target_pairs={{0,1},{1,0},{2,3},{3,2},{4,5},{5,4},{6,7},{7,6},{8,9},{9,8},{10,11... | collective-permute-start | bytes 147464 | tf_op jit(solution)/shard_map/ppermute | solution.py:25
  28.5 7.2 %collective-permute-start.4 = (bf16[3,16,512]{2,1,0:T(8,128)(2,1)S(1)}, bf16[3,16,512]{2,1,0:T(8,128)(2,1)S(1)}, u32[]{:S(2)}, u32[]{:S(2)}) collective-permute-start(bf16[3,16,512]{2,1,0:T(8,128)(2,1)S(1)} %get-tuple-element.42), channel_id=1, source_target_pairs={{0,2},{1,3},{2,0},{3,1},{4,6},{5,7},{6,4},{7,5},{8,10},{9,11},{10,... | collective-permute-start | bytes 147464 | tf_op jit(solution)/shard_map/ppermute | solution.py:25
  31.5 7.0 %collective-permute-start.5 = (bf16[3,16,512]{2,1,0:T(8,128)(2,1)S(1)}, bf16[3,16,512]{2,1,0:T(8,128)(2,1)S(1)}, u32[]{:S(2)}, u32[]{:S(2)}) collective-permute-start(bf16[3,16,512]{2,1,0:T(8,128)(2,1)S(1)} %get-tuple-element.42), channel_id=1, source_target_pairs={{0,4},{1,5},{2,6},{3,7},{4,0},{5,1},{6,2},{7,3},{8,12},{9,13},{10,... | collective-permute-start | bytes 147464 | tf_op jit(solution)/shard_map/ppermute | solution.py:25
  41.3 13.9 %collective-permute-start.10 = (bf16[4,3,16,512]{3,2,1,0:T(8,128)(2,1)S(1)}, bf16[4,3,16,512]{3,2,1,0:T(8,128)(2,1)S(1)}, u32[]{:S(2)}, u32[]{:S(2)}) collective-permute-start(bf16[4,3,16,512]{3,2,1,0:T(8,128)(2,1)S(1)} %pad_maximum_fusion.2.rest_0_), channel_id=1, source_target_pairs={{0,32},{1,33},{2,34},{3,35},{4,36},{5,37},{6,38},{7,39},{8,40},{9,... | collective-permute-start | bytes 589832 | tf_op jit(solution)/shard_map/ppermute | solution.py:25
  44.1 11.2 %collective-permute-start.11 = (bf16[4,3,16,512]{3,2,1,0:T(8,128)(2,1)S(1)}, bf16[4,3,16,512]{3,2,1,0:T(8,128)(2,1)S(1)}, u32[]{:S(2)}, u32[]{:S(2)}) collective-permute-start(bf16[4,3,16,512]{3,2,1,0:T(8,128)(2,1)S(1)} %pad_maximum_fusion.2.rest_0_), channel_id=1, source_target_pairs={{0,40},{1,41},{2,42},{3,43},{4,44},{5,45},{6,46},{7,47},{8,32},{9,... | collective-permute-start | bytes 589832 | tf_op jit(solution)/shard_map/ppermute | solution.py:25
  45.4 13.9 %collective-permute-start.12 = (bf16[4,3,16,512]{3,2,1,0:T(8,128)(2,1)S(1)}, bf16[4,3,16,512]{3,2,1,0:T(8,128)(2,1)S(1)}, u32[]{:S(2)}, u32[]{:S(2)}) collective-permute-start(bf16[4,3,16,512]{3,2,1,0:T(8,128)(2,1)S(1)} %pad_maximum_fusion.2.rest_0_), channel_id=1, source_target_pairs={{0,48},{1,49},{2,50},{3,51},{4,52},{5,53},{6,54},{7,55},{8,56},{9,... | collective-permute-start | bytes 589832 | tf_op jit(solution)/shard_map/ppermute | solution.py:25
  48.4 6.7 %collective-permute-start.2 = (f32[1,512]{1,0:T(1,128)S(1)}, f32[1,512]{1,0:T(1,128)S(1)}, u32[]{:S(2)}, u32[]{:S(2)}) collective-permute-start(f32[1,512]{1,0:T(1,128)S(1)} %get-tuple-element.56), channel_id=1, source_target_pairs={{0,1},{1,2},{2,3},{3,4},{4,5},{5,6},{6,7},{7,8},{8,9},{9,10},{10,1... | collective-permute-start | bytes 6152 | tf_op jit(solution)/shard_map/ppermute | solution.py:30
  55.2 6.8 %collective-permute-start.13 = (bf16[4,3,16,512]{3,2,1,0:T(8,128)(2,1)S(1)}, bf16[4,3,16,512]{3,2,1,0:T(8,128)(2,1)}, u32[]{:S(2)}, u32[]{:S(2)}) collective-permute-start(bf16[4,3,16,512]{3,2,1,0:T(8,128)(2,1)S(1)} %pad_maximum_fusion.2.rest_0_), channel_id=1, source_target_pairs={{0,56},{1,57},{2,58},{3,59},{4,60},{5,61},{6,62},{7,63},{8,48},{9,... | collective-permute-start | bytes 589832 | tf_op jit(solution)/shard_map/ppermute | solution.py:25
  55.2 6.8 %collective-permute-start.7 = (bf16[4,3,16,512]{3,2,1,0:T(8,128)(2,1)S(1)}, bf16[4,3,16,512]{3,2,1,0:T(8,128)(2,1)}, u32[]{:S(2)}, u32[]{:S(2)}) collective-permute-start(bf16[4,3,16,512]{3,2,1,0:T(8,128)(2,1)S(1)} %pad_maximum_fusion.2.rest_0_), channel_id=1, source_target_pairs={{0,8},{1,9},{2,10},{3,11},{4,12},{5,13},{6,14},{7,15},{8,0},{9,1},... | collective-permute-start | bytes 589832 | tf_op jit(solution)/shard_map/ppermute | solution.py:25
  59.9 7.3 %collective-permute-start.9 = (bf16[4,3,16,512]{3,2,1,0:T(8,128)(2,1)S(1)}, bf16[4,3,16,512]{3,2,1,0:T(8,128)(2,1)}, u32[]{:S(2)}, u32[]{:S(2)}) collective-permute-start(bf16[4,3,16,512]{3,2,1,0:T(8,128)(2,1)S(1)} %pad_maximum_fusion.2.rest_0_), channel_id=1, source_target_pairs={{0,24},{1,25},{2,26},{3,27},{4,28},{5,29},{6,30},{7,31},{8,16},{9,... | collective-permute-start | bytes 589832 | tf_op jit(solution)/shard_map/ppermute | solution.py:25
  76.4 7.2 %collective-permute-start.14 = (bf16[3,64,512]{2,1,0:T(8,128)(2,1)}, bf16[3,64,512]{2,1,0:T(8,128)(2,1)S(1)}, u32[]{:S(2)}, u32[]{:S(2)}) collective-permute-start(bf16[3,64,512]{2,1,0:T(8,128)(2,1)} %get-tuple-element.25), channel_id=1, source_target_pairs={{0,8},{1,9},{2,10},{3,11},{4,12},{5,13},{6,14},{7,15},{8,0},{9,1},... | collective-permute-start | bytes 589832 | tf_op jit(solution)/shard_map/ppermute | solution.py:25
  76.9 8.5 %collective-permute-start.15 = (bf16[3,64,512]{2,1,0:T(8,128)(2,1)}, bf16[3,64,512]{2,1,0:T(8,128)(2,1)S(1)}, u32[]{:S(2)}, u32[]{:S(2)}) collective-permute-start(bf16[3,64,512]{2,1,0:T(8,128)(2,1)} %get-tuple-element.26), channel_id=1, source_target_pairs={{0,16},{1,17},{2,18},{3,19},{4,20},{5,21},{6,22},{7,23},{8,24},{9,... | collective-permute-start | bytes 589832 | tf_op jit(solution)/shard_map/ppermute | solution.py:25
  78.3 9.3 %collective-permute-start.16 = (bf16[3,64,512]{2,1,0:T(8,128)(2,1)}, bf16[3,64,512]{2,1,0:T(8,128)(2,1)S(1)}, u32[]{:S(2)}, u32[]{:S(2)}) collective-permute-start(bf16[3,64,512]{2,1,0:T(8,128)(2,1)} %get-tuple-element.27), channel_id=1, source_target_pairs={{0,24},{1,25},{2,26},{3,27},{4,28},{5,29},{6,30},{7,31},{8,16},{9,... | collective-permute-start | bytes 589832 | tf_op jit(solution)/shard_map/ppermute | solution.py:25
  79.5 114.2 %collective-permute-start.35 = (bf16[2,512,512]{2,1,0:T(8,128)(2,1)S(1)}, bf16[2,512,512]{2,1,0:T(8,128)(2,1)S(1)}, u32[]{:S(2)}, u32[]{:S(2)}) collective-permute-start(bf16[2,512,512]{2,1,0:T(8,128)(2,1)S(1)} %pad_maximum_fusion.1), channel_id=1, source_target_pairs={{0,1},{1,2},{2,3},{3,4},{4,5},{5,6},{6,7},{7,8},{8,9},{9,10},{10,1... | collective-permute-start | bytes 3145736 | tf_op jit(solution)/shard_map/ppermute | solution.py:30
  81.5 9.0 %collective-permute-start.17 = (bf16[3,64,512]{2,1,0:T(8,128)(2,1)S(1)}, bf16[3,64,512]{2,1,0:T(8,128)(2,1)S(1)}, u32[]{:S(2)}, u32[]{:S(2)}) collective-permute-start(bf16[3,64,512]{2,1,0:T(8,128)(2,1)S(1)} %copy-done.30), channel_id=1, source_target_pairs={{0,32},{1,33},{2,34},{3,35},{4,36},{5,37},{6,38},{7,39},{8,40},{9,... | collective-permute-start | bytes 589832 | tf_op jit(solution)/shard_map/ppermute | solution.py:25
  83.7 39.1 %collective-permute-start.18 = (bf16[3,64,512]{2,1,0:T(8,128)(2,1)S(1)}, bf16[3,64,512]{2,1,0:T(8,128)(2,1)S(1)}, u32[]{:S(2)}, u32[]{:S(2)}) collective-permute-start(bf16[3,64,512]{2,1,0:T(8,128)(2,1)S(1)} %copy-done.29), channel_id=1, source_target_pairs={{0,40},{1,41},{2,42},{3,43},{4,44},{5,45},{6,46},{7,47},{8,32},{9,... | collective-permute-start | bytes 589832 | tf_op jit(solution)/shard_map/ppermute | solution.py:25
  85.4 37.3 %collective-permute-start.19 = (bf16[3,64,512]{2,1,0:T(8,128)(2,1)S(1)}, bf16[3,64,512]{2,1,0:T(8,128)(2,1)S(1)}, u32[]{:S(2)}, u32[]{:S(2)}) collective-permute-start(bf16[3,64,512]{2,1,0:T(8,128)(2,1)S(1)} %copy-done.28), channel_id=1, source_target_pairs={{0,48},{1,49},{2,50},{3,51},{4,52},{5,53},{6,54},{7,55},{8,56},{9,... | collective-permute-start | bytes 589832 | tf_op jit(solution)/shard_map/ppermute | solution.py:25
  87.7 35.1 %collective-permute-start.20 = (bf16[3,64,512]{2,1,0:T(8,128)(2,1)S(1)}, bf16[3,64,512]{2,1,0:T(8,128)(2,1)S(1)}, u32[]{:S(2)}, u32[]{:S(2)}) collective-permute-start(bf16[3,64,512]{2,1,0:T(8,128)(2,1)S(1)} %copy-done.27), channel_id=1, source_target_pairs={{0,56},{1,57},{2,58},{3,59},{4,60},{5,61},{6,62},{7,63},{8,48},{9,... | collective-permute-start | bytes 589832 | tf_op jit(solution)/shard_map/ppermute | solution.py:25
  90.4 61.4 %collective-permute-start = (bf16[512,512]{1,0:T(8,128)(2,1)S(1)}, bf16[512,512]{1,0:T(8,128)(2,1)S(1)}, u32[]{:S(2)}, u32[]{:S(2)}) collective-permute-start(bf16[512,512]{1,0:T(8,128)(2,1)S(1)} %slice_select_fusion), channel_id=1, source_target_pairs={{0,1},{1,2},{2,3},{3,4},{4,5},{5,6},{6,7},{7,8},{8,9},{9,10},{10,1... | collective-permute-start | bytes 1572872 | tf_op jit(solution)/shard_map/ppermute | solution.py:30
  126.7 7.9 %collective-permute-start.22 = (bf16[3,16,512]{2,1,0:T(8,128)(2,1)}, bf16[3,16,512]{2,1,0:T(8,128)(2,1)S(1)}, u32[]{:S(2)}, u32[]{:S(2)}) collective-permute-start(bf16[3,16,512]{2,1,0:T(8,128)(2,1)} %get-tuple-element.34), channel_id=1, source_target_pairs={{0,4},{1,5},{2,6},{3,7},{4,0},{5,1},{6,2},{7,3},{8,12},{9,13},{10,... | collective-permute-start | bytes 147464 | tf_op jit(solution)/shard_map/ppermute | solution.py:25
  126.8 8.6 %collective-permute-start.23 = (bf16[3,16,512]{2,1,0:T(8,128)(2,1)}, bf16[3,16,512]{2,1,0:T(8,128)(2,1)S(1)}, u32[]{:S(2)}, u32[]{:S(2)}) collective-permute-start(bf16[3,16,512]{2,1,0:T(8,128)(2,1)} %get-tuple-element.35), channel_id=1, source_target_pairs={{0,6},{1,7},{2,4},{3,5},{4,2},{5,3},{6,0},{7,1},{8,14},{9,15},{10,... | collective-permute-start | bytes 147464 | tf_op jit(solution)/shard_map/ppermute | solution.py:25
  139.9 7.2 %collective-permute-start.25 = (bf16[3,16,512]{2,1,0:T(8,128)(2,1)}, bf16[3,16,512]{2,1,0:T(8,128)(2,1)S(1)}, u32[]{:S(2)}, u32[]{:S(2)}) collective-permute-start(bf16[3,16,512]{2,1,0:T(8,128)(2,1)} %get-tuple-element.37), channel_id=1, source_target_pairs={{0,4},{1,5},{2,6},{3,7},{4,0},{5,1},{6,2},{7,3},{8,12},{9,13},{10,... | collective-permute-start | bytes 147464 | tf_op jit(solution)/shard_map/ppermute | solution.py:25
  149.2 6.8 %collective-permute-start.28 = (bf16[4,3,16,512]{3,2,1,0:T(8,128)(2,1)S(1)}, bf16[4,3,16,512]{3,2,1,0:T(8,128)(2,1)S(1)}, u32[]{:S(2)}, u32[]{:S(2)}) collective-permute-start(bf16[4,3,16,512]{3,2,1,0:T(8,128)(2,1)S(1)} %pad_maximum_fusion.3.rest_0_), channel_id=1, source_target_pairs={{0,16},{1,17},{2,18},{3,19},{4,20},{5,21},{6,22},{7,23},{8,24},{9,... | collective-permute-start | bytes 589832 | tf_op jit(solution)/shard_map/ppermute | solution.py:25
  149.3 7.7 %collective-permute-start.29 = (bf16[4,3,16,512]{3,2,1,0:T(8,128)(2,1)S(1)}, bf16[4,3,16,512]{3,2,1,0:T(8,128)(2,1)S(1)}, u32[]{:S(2)}, u32[]{:S(2)}) collective-permute-start(bf16[4,3,16,512]{3,2,1,0:T(8,128)(2,1)S(1)} %pad_maximum_fusion.3.rest_0_), channel_id=1, source_target_pairs={{0,24},{1,25},{2,26},{3,27},{4,28},{5,29},{6,30},{7,31},{8,16},{9,... | collective-permute-start | bytes 589832 | tf_op jit(solution)/shard_map/ppermute | solution.py:25
  151.8 12.7 %collective-permute-start.30 = (bf16[4,3,16,512]{3,2,1,0:T(8,128)(2,1)S(1)}, bf16[4,3,16,512]{3,2,1,0:T(8,128)(2,1)S(1)}, u32[]{:S(2)}, u32[]{:S(2)}) collective-permute-start(bf16[4,3,16,512]{3,2,1,0:T(8,128)(2,1)S(1)} %pad_maximum_fusion.3.rest_0_), channel_id=1, source_target_pairs={{0,32},{1,33},{2,34},{3,35},{4,36},{5,37},{6,38},{7,39},{8,40},{9,... | collective-permute-start | bytes 589832 | tf_op jit(solution)/shard_map/ppermute | solution.py:25
  154.4 10.2 %collective-permute-start.31 = (bf16[4,3,16,512]{3,2,1,0:T(8,128)(2,1)S(1)}, bf16[4,3,16,512]{3,2,1,0:T(8,128)(2,1)S(1)}, u32[]{:S(2)}, u32[]{:S(2)}) collective-permute-start(bf16[4,3,16,512]{3,2,1,0:T(8,128)(2,1)S(1)} %pad_maximum_fusion.3.rest_0_), channel_id=1, source_target_pairs={{0,40},{1,41},{2,42},{3,43},{4,44},{5,45},{6,46},{7,47},{8,32},{9,... | collective-permute-start | bytes 589832 | tf_op jit(solution)/shard_map/ppermute | solution.py:25
  156.0 8.6 %collective-permute-start.32 = (bf16[4,3,16,512]{3,2,1,0:T(8,128)(2,1)S(1)}, bf16[4,3,16,512]{3,2,1,0:T(8,128)(2,1)S(1)}, u32[]{:S(2)}, u32[]{:S(2)}) collective-permute-start(bf16[4,3,16,512]{3,2,1,0:T(8,128)(2,1)S(1)} %pad_maximum_fusion.3.rest_0_), channel_id=1, source_target_pairs={{0,48},{1,49},{2,50},{3,51},{4,52},{5,53},{6,54},{7,55},{8,56},{9,... | collective-permute-start | bytes 589832 | tf_op jit(solution)/shard_map/ppermute | solution.py:25
  157.0 9.6 %collective-permute-start.33 = (bf16[4,3,16,512]{3,2,1,0:T(8,128)(2,1)S(1)}, bf16[4,3,16,512]{3,2,1,0:T(8,128)(2,1)S(1)}, u32[]{:S(2)}, u32[]{:S(2)}) collective-permute-start(bf16[4,3,16,512]{3,2,1,0:T(8,128)(2,1)S(1)} %pad_maximum_fusion.3.rest_0_), channel_id=1, source_target_pairs={{0,56},{1,57},{2,58},{3,59},{4,60},{5,61},{6,62},{7,63},{8,48},{9,... | collective-permute-start | bytes 589832 | tf_op jit(solution)/shard_map/ppermute | solution.py:25
  172.4 26.9 %collective-permute-start.36 = (f32[2,512]{1,0:T(2,128)}, f32[2,512]{1,0:T(2,128)S(1)}, u32[]{:S(2)}, u32[]{:S(2)}) collective-permute-start(f32[2,512]{1,0:T(2,128)} %get-tuple-element.40), channel_id=1, source_target_pairs={{0,64},{64,0},{128,192},{192,128},{1,65},{65,1},{129,193},{193,129... | collective-permute-start | bytes 12296 | tf_op jit(solution)/shard_map/ppermute | solution.py:321
  190.4 8.9 %collective-permute-start.37 = (f32[2,512]{1,0:T(2,128)}, f32[2,512]{1,0:T(2,128)S(1)}, u32[]{:S(2)}, u32[]{:S(2)}) collective-permute-start(f32[2,512]{1,0:T(2,128)} %get-tuple-element.40), channel_id=1, source_target_pairs={{0,128},{64,192},{128,0},{192,64},{1,129},{65,193},{129,1},{193,65... | collective-permute-start | bytes 12296 | tf_op jit(solution)/shard_map/ppermute | solution.py:321
  201.0 12.7 %collective-permute-start.34 = (bf16[512,512]{1,0:T(8,128)(2,1)S(1)}, bf16[512,512]{1,0:T(8,128)(2,1)S(1)}, u32[]{:S(2)}, u32[]{:S(2)}) collective-permute-start(bf16[512,512]{1,0:T(8,128)(2,1)S(1)} %copy-done.23), channel_id=1, source_target_pairs={{0,63},{1,0},{2,1},{3,2},{4,3},{5,4},{6,5},{7,6},{8,7},{9,8},{10,9... | collective-permute-start | bytes 1572872 | tf_op jit(solution)/shard_map/ppermute | solution.py:30
  (48 other events, 335.4 us)

commit v2 on v1

--- a/solution.py
+++ b/solution.py
@@ -17,7 +17,7 @@
 F32 = jnp.float32
 BF16 = jnp.bfloat16
 
-ZQ, XY = 4, 8
+ZQ, XY, RING = 4, 8, 8
 
 
 def move_xor(value, mask):
@@ -25,9 +25,24 @@
     return lax.ppermute(value, "seq", [(i, i ^ mask) for i in range(n)])
 
 
-def shift(value, step):
+def ring(value, step):
     n = lax.axis_size("seq")
-    return lax.ppermute(value, "seq", [(i, (i + step) % n) for i in range(n)])
+    pairs = [(i, i - i % RING + (i + step) % RING) for i in range(n)]
+    return lax.ppermute(value, "seq", pairs)
+
+
+def to_next_plane(value):
+    n = lax.axis_size("seq")
+    return lax.ppermute(value, "seq", [(i, i + RING) for i in range(RING - 1, n - RING, RING)])
+
+
+def close_ring(value):
+    n = lax.axis_size("seq")
+    return lax.ppermute(value, "seq", [(i, i - RING + 1) for i in range(RING - 1, n, RING)])
+
+
+def after(value, other):
+    return lax.optimization_barrier((value, other))[0]
 
 
 def dot(a, b):
@@ -77,10 +92,12 @@
 
 def fill_rows(s_ref, blocks, rows_ref):
     for j, block in enumerate(blocks):
-        for k in range(ZQ):
-            at = pl.multiple_of(row_start(s_ref, 4 + j) + row_start(s_ref, 12 + k), 16)
-            for m in range(3):
-                rows_ref[m, pl.ds(at, 16), :] = block[k, m]
+        for t in range(2):
+            for k in range(ZQ):
+                at = row_start(s_ref, 4 + 2 * j + t) + row_start(s_ref, 12 + k)
+                at = pl.multiple_of(at, 16)
+                for m in range(3):
+                    rows_ref[m, pl.ds(at, 16), :] = block[t, k, m]
 
 
 def columns_sq(rows_ref, m):
@@ -93,7 +110,7 @@
 
 
 def gradient_kernel(s_ref, halo, k_own, v_own, rate_prev, rate_own, *rest):
-    blocks, rest = rest[:XY], rest[XY:]
+    blocks, rest = rest[:XY // 2], rest[XY // 2:]
     own_out, outs, old_sq = rest[0], rest[1:XY], rest[XY]
     w_rows, k_all, gv, hid, d_gate, d_up, grads = rest[XY + 1:]
     fill_rows(s_ref, blocks, w_rows)
@@ -144,36 +161,44 @@
     upd_b[...] = total.astype(BF16)
 
 
+def branch_of(q, u_rows, ratio):
+    pre_a = dot(q, u_rows[0]) * ratio[0]
+    pre_b = dot(q, u_rows[1]) * ratio[1]
+    hid = (pre_a * jax.nn.sigmoid(pre_a) * pre_b).astype(BF16)
+    branch = dot(hid, u_rows[2]) * ratio[2]
+    squares = branch * branch
+    lanes = sum(squares[:, c * 128:(c + 1) * 128] for c in range(HD // 128))
+    return branch.astype(BF16), jnp.sum(lanes.T, axis=0, keepdims=True)
+
+
 def apply_kernel(s_ref, q_prev, q_own, old_sq, upd, *rest):
-    blocks, rest = rest[:XY], rest[XY:]
-    f_prev, f_own, sq, new, u_rows = rest
+    blocks, (f_prev, f_own, sq, new, u_rows) = rest[:XY // 2], rest[XY // 2:]
     fill_rows(s_ref, blocks, u_rows)
     ratio = [
         jnp.sqrt(old_sq[m:m + 1, :]) / jnp.sqrt(columns_sq(u_rows, m) + EPS) for m in range(3)
     ]
     for m in range(3):
         new[m] = upd[m] * ratio[m]
-    for part, (q, out) in enumerate(((q_prev, f_prev), (q_own, f_own))):
-        pre_a = dot(q[...], u_rows[0]) * ratio[0]
-        pre_b = dot(q[...], u_rows[1]) * ratio[1]
-        hid = (pre_a * jax.nn.sigmoid(pre_a) * pre_b).astype(BF16)
-        branch = dot(hid, u_rows[2]) * ratio[2]
-        out[...] = branch.astype(BF16)
-        squares = branch * branch
-        lanes = sum(squares[:, c * 128:(c + 1) * 128] for c in range(HD // 128))
-        sq[part:part + 1, :] = jnp.sum(lanes.T, axis=0, keepdims=True)
-
-
-def attention_kernel(s_ref, q_ref, k_ref, v_ref, halo, out):
+    f_prev[...], sq[0:1, :] = branch_of(q_prev[...], u_rows, ratio)
+    f_own[...], sq[1:2, :] = branch_of(q_own[...], u_rows, ratio)
+
+
+def attention_kernel(s_ref, q_ref, k_ref, v_ref, halo, *rest):
     scale = 1.0 / math.sqrt(HD)
     first = s_ref[2] == 0
+    crossing = s_ref[3] == 0
+    close, out = rest[:-1], rest[-1]
     half = BLK // 2
     for part in range(2):
         base = part * half
         q = q_ref[base:base + half, :]
         own_len = base + half
         prev_len = BLK - base
-        s_prev = dot_cols(q, halo[0, base:, :]) * scale
+        k_prev, v_prev = halo[0, base:, :], halo[1, base:, :]
+        if close:
+            k_prev = jnp.where(crossing, close[0][0, base:, :], k_prev)
+            v_prev = jnp.where(crossing, close[0][1, base:, :], v_prev)
+        s_prev = dot_cols(q, k_prev) * scale
         s_own = dot_cols(q, k_ref[:own_len, :]) * scale
         row_p = lax.broadcasted_iota(jnp.int32, (half, prev_len), 0)
         col_p = lax.broadcasted_iota(jnp.int32, (half, prev_len), 1)
@@ -192,7 +217,7 @@
         )
         p_prev = (e_prev * inv).astype(BF16)
         p_own = (e_own * inv).astype(BF16)
-        out[base:base + half, :] = dot(p_prev, halo[1, base:, :]) + dot(p_own, v_ref[:own_len, :])
+        out[base:base + half, :] = dot(p_prev, v_prev) + dot(p_own, v_ref[:own_len, :])
 
 
 def mix_kernel(s_ref, f_own, f_back, attn_own, attn_other, sums, gain, out):
@@ -221,7 +246,7 @@
     zq = (seq_pos >> 1) & (ZQ - 1)
     xy = seq_pos >> 3
     scalars = jnp.stack(
-        [own, other, seq_pos, seq_pos * 0]
+        [own, other, seq_pos, seq_pos & (RING - 1)]
         + [64 * (xy ^ j) for j in range(XY)]
         + [16 * (zq ^ k) for k in range(ZQ)]
     ).astype(jnp.int32)
@@ -239,19 +264,38 @@
         even, jnp.concatenate([mine, got], axis=1), jnp.concatenate([got, mine], axis=1)
     )
 
-    halo_send = jnp.stack([head_of(keys, False), head_of(values, False)])
     rate_send = jnp.where(even, rate[1:2], rate[0:1])
     rate_mine = jnp.where(even, rate[0:1], rate[1:2])
 
-    def gather_blocks(chunk):
-        block = jnp.stack([chunk] + [move_xor(chunk, k << 1) for k in range(1, ZQ)])
-        return [block] + [move_xor(block, j << 3) for j in range(1, XY)]
-
-    w_blocks = gather_blocks(w_pair.astype(BF16))
-    halo = shift(halo_send, 1)
-    rate_prev = shift(rate_send, 1)
-
-    block_specs = [whole((ZQ, 3, 16, HD))] * XY
+    def gather_zq(chunk):
+        return jnp.stack([chunk] + [move_xor(chunk, k << 1) for k in range(1, ZQ)])
+
+    def gather_xy(block):
+        pair = jnp.stack([block, move_xor(block, 1 << 3)])
+        return [pair] + [move_xor(pair, j << 4) for j in range(1, XY // 2)]
+
+    send_other = jnp.stack([head_of(keys, False), head_of(values, False)])
+    send_own = jnp.stack([head_of(keys, True), head_of(values, True)])
+    plane_k = to_next_plane(keys[:, HD:])
+    rate_prev = ring(rate_send, 1)
+    w_block = after(gather_zq(after(w_pair.astype(BF16), rate_prev)), plane_k)
+    w_blocks = gather_xy(w_block)
+    halo = ring(after(send_other, w_block), 1)
+    last = (seq_pos & (RING - 1)) == RING - 1
+    plane_v = to_next_plane(after(values[:, HD:], w_blocks[-1]))
+    q_prev = ring(after(head_of(queries, False), halo), 1)
+
+    def attend(pick, prev):
+        return call(
+            attention_kernel,
+            scalars,
+            [queries, keys, values] + prev,
+            [head_block(pick)] * 3 + [whole((2, BLK, HD))] * len(prev),
+            shape((BLK, HD), F32),
+            flops=4 * BLK * 768 * HD,
+        )
+
+    block_specs = [whole((2, ZQ, 3, 16, HD))] * (XY // 2)
     grad_out = call(
         gradient_kernel,
         scalars,
@@ -266,6 +310,8 @@
     )
     old_sq = grad_out[XY]
     arrived = [move_xor(grad_out[j], j << 3) for j in range(1, XY)]
+    plane_own = jnp.stack([plane_k, after(plane_v, old_sq)])
+    halo_other = ring(jnp.where(last, plane_own, after(send_own, q_prev)), 1)
     chunks = call(
         block_sum_kernel,
         scalars,
@@ -278,32 +324,20 @@
     upd, upd_b = call(
         update_kernel,
         scalars,
-        [chunks[0]] + arrived + [w_pair],
+        [after(chunks[0], halo_other)] + arrived + [w_pair],
         [whole((3, 16, HD))] * 5,
         [shape((3, 16, HD), F32), shape((3, 16, HD), BF16)],
     )
-    u_blocks = gather_blocks(upd_b)
-
-    halo_other = shift(jnp.stack([head_of(keys, True), head_of(values, True)]), 1)
-    q_prev = shift(head_of(queries, False), 1)
-
-    def attend(pick, prev):
-        return call(
-            attention_kernel,
-            scalars,
-            [queries, keys, values, prev],
-            [head_block(pick)] * 3 + [whole((2, BLK, HD))],
-            shape((BLK, HD), F32),
-            flops=4 * BLK * 768 * HD,
-        )
-
-    attn_own = attend(0, halo)
-    attn_other = attend(1, halo_other)
-
+    plane_other = to_next_plane(after(send_other, chunks[0]))
+    u_block = after(gather_zq(upd_b), plane_other)
+    u_blocks = gather_xy(u_block)
+    closing = close_ring(after(plane_other, u_block))
+    attn_other = attend(1, [halo_other])
+    attn_own = attend(0, [halo, closing])
     f_prev, f_own, sq, new = call(
         apply_kernel,
         scalars,
-        [q_prev, queries, old_sq, upd] + u_blocks,
+        [after(after(q_prev, attn_other), attn_own), queries, old_sq, upd] + u_blocks,
         [whole((BLK, HD)), head_block(0), whole((3, HD)), whole((3, 16, HD))] + block_specs,
         [
             shape((BLK, HD), BF16),
@@ -314,14 +348,14 @@
         [pltpu.VMEM((3, HD, HD), BF16)],
         flops=6 * 2 * BLK * HD * HD,
     )
-    f_back = shift(f_prev, -1)
+    f_back = ring(f_prev, -1)
     heads = lax.axis_size("head")
     totals = sq
     for k in range(1, heads):
         totals = totals + lax.ppermute(sq, "head", [(i, i ^ k) for i in range(heads)])
-    sums = totals[1:2] + shift(totals[0:1], -1)
+    sums = totals[1:2] + ring(totals[0:1], -1)
     new_mine = jnp.where(even, new[:, :8], new[:, 8:])
-    new_theirs = move_xor(jnp.where(even, new[:, 8:], new[:, :8]), 1)
+    new_theirs = after(move_xor(jnp.where(even, new[:, 8:], new[:, :8]), 1), f_back)
     new_all = jnp.where(
         even,
         jnp.stack([new_mine, new_theirs], axis=1),

time: 220 us -> 175 us (0.80)
  waiting for transfers between devices: 91.6 us -> 63.4 us
  starting transfers between devices: 82.2 us -> 61.5 us
  other arithmetic: 4.64 us -> 9.6 us
    ppermute x32 -> x26, waiting for transfers between devices: 76.4 us -> 39.8 us  [move_xor(): return lax.ppermute(value, 'seq', [(i, i ^ mask) for i in range(n)])]
    ppermute x3, starting transfers between devices: 21.2 us -> 10.3 us  [local(): lax.ppermute(sq, 'head', [(i, i ^ k) for i in range(heads)])]
    ppermute x32 -> x26, starting transfers between devices: 49.9 us -> 43.1 us  [move_xor(): return lax.ppermute(value, 'seq', [(i, i ^ mask) for i in range(n)])]
    ppermute x3, waiting for transfers between devices: 0.01 us -> 4.41 us  [local(): lax.ppermute(sq, 'head', [(i, i ^ k) for i in range(heads)])]
    ppermute x6 -> x10, waiting for transfers between devices: 15.2 us -> 19.2 us  [the longest x6 13.3 us: ring(): return lax.ppermute(value, 'seq', pairs)]
    ppermute x6 -> x10, starting transfers between devices: 11 us -> 8.06 us  [the longest x6 3.91 us: ring(): return lax.ppermute(value, 'seq', pairs)]
    unnamed x78 -> x68, local copies, waits for them, and re-layouts: 5.58 us -> 4.25 us
  transfers between devices with their start and end apart: 41 -> 39, of which waited for: 17 -> 19; matrix products, arithmetic and copies ran while one was open for 2% -> 5% of each run, Pallas kernels for 9% -> 13%
where the time goes in v2:
time: 175 us; the launch traced here: 174 us
  waiting for transfers between devices  63.4 us (36%)
  starting transfers between devices  61.5 us (35%)
  Pallas kernels  32.6 us (19%)
  other arithmetic  9.6 us (5%)
  local copies, waits for them, and re-layouts  5.65 us (3%)
    ppermute x26, starting transfers between devices, move_xor(): return lax.ppermute(value, 'seq', [(i, i ^ mask) for i in range(n)])  43.1 us
    ppermute x26, waiting for transfers between devices, move_xor(): return lax.ppermute(value, 'seq', [(i, i ^ mask) for i in range(n)])  39.8 us
    pallas_call x7, Pallas kernels, call(): pl.pallas_call(kernel, out_shape=outs, grid_spec=pltpu.PrefetchScalarGrid...  32.6 us
    ppermute x6, waiting for transfers between devices, ring(): return lax.ppermute(value, 'seq', pairs)  13.3 us
    ppermute x3, starting transfers between devices, local(): lax.ppermute(sq, 'head', [(i, i ^ k) for i in range(heads)])  10.3 us
    ppermute x1, waiting for transfers between devices, close_ring(): lax.ppermute(value, 'seq', [(i, i - RING + 1) for i in range(RING - 1, n,...  5.84 us
    ppermute x3, waiting for transfers between devices, local(): lax.ppermute(sq, 'head', [(i, i ^ k) for i in range(heads)])  4.41 us
    unnamed x68, local copies, waits for them, and re-layouts  4.25 us
  transfers between devices with their start and end apart: 39, of which 19 were waited for; matrix products, arithmetic and copies ran while one was open for 5% of the time, Pallas kernels for 13%

profile of v2, /device:TPU:1, one launch (start us, length us, event | category | flops | bytes accessed | tf_op | source)
XLA Modules:
  0.0 173.8 jit_solution(12936063368815739358)
XLA Ops:
  1.5 2.6 %collective-permute-start = (f32[3,8,512]{2,1,0:T(8,128)S(1)}, f32[3,8,512]{2,1,0:T(8,128)S(1)}, u32[]{:S(2)}, u32[]{:S(2)}) collective-permute-start(f32[3,8,512]{2,1,0:T(8,128)S(1)} %get-tuple-element.83), channel_id=1, source_target_pairs={{0,1},{1,0},{2,3},{3,2},{4,5},{5,4},{6,7},{7,6},{8,9},{9,8},{10,11... | collective-permute-start | bytes 147464 | tf_op jit(solution)/shard_map/ppermute | solution.py:25
  11.8 4.4 %collective-permute-start.3 = (bf16[3,16,512]{2,1,0:T(8,128)(2,1)S(1)}, bf16[3,16,512]{2,1,0:T(8,128)(2,1)S(1)}, u32[]{:S(2)}, u32[]{:S(2)}) collective-permute-start(bf16[3,16,512]{2,1,0:T(8,128)(2,1)S(1)} %get-tuple-element.37), channel_id=1, source_target_pairs={{0,4},{1,5},{2,6},{3,7},{4,0},{5,1},{6,2},{7,3},{8,12},{9,13},{10,... | collective-permute-start | bytes 147464 | tf_op jit(solution)/shard_map/ppermute | solution.py:25
  16.3 2.4 %collective-permute-done.3 = bf16[3,16,512]{2,1,0:T(8,128)(2,1)S(1)} collective-permute-done((bf16[3,16,512]{2,1,0:T(8,128)(2,1)S(1)}, bf16[3,16,512]{2,1,0:T(8,128)(2,1)S(1)}, u32[]{:S(2)}, u32[]{:S(2)}) %collective-permute-start.3) | collective-permute-done | bytes 49184 | tf_op jit(solution)/shard_map/ppermute | solution.py:25
  18.7 3.1 %collective-permute-done.4 = bf16[3,16,512]{2,1,0:T(8,128)(2,1)S(1)} collective-permute-done((bf16[3,16,512]{2,1,0:T(8,128)(2,1)S(1)}, bf16[3,16,512]{2,1,0:T(8,128)(2,1)S(1)}, u32[]{:S(2)}, u32[]{:S(2)}) %collective-permute-start.4) | collective-permute-done | bytes 49184 | tf_op jit(solution)/shard_map/ppermute | solution.py:25
  21.9 2.3 %collective-permute-start.6 = (bf16[2,512,512]{2,1,0:T(8,128)(2,1)S(1)}, bf16[2,512,512]{2,1,0:T(8,128)(2,1)S(1)}, u32[]{:S(2)}, u32[]{:S(2)}) collective-permute-start(bf16[2,512,512]{2,1,0:T(8,128)(2,1)S(1)} %pad_maximum_fusion), channel_id=1, source_target_pairs={{0,1},{1,2},{2,3},{3,4},{4,5},{5,6},{6,7},{7,0},{8,9},{9,10},{10,1... | collective-permute-start | bytes 3145736 | tf_op jit(solution)/shard_map/ppermute | solution.py:31
  25.3 3.7 %collective-permute-done.8 = bf16[4,3,16,512]{3,2,1,0:T(8,128)(2,1)S(1)} collective-permute-done((bf16[4,3,16,512]{3,2,1,0:T(8,128)(2,1)S(1)}, bf16[4,3,16,512]{3,2,1,0:T(8,128)(2,1)S(1)}, u32[]{:S(2)}, u32[]{:S(2)}) %collective-permute-start.8) | collective-permute-done | bytes 196640 | tf_op jit(solution)/shard_map/ppermute | solution.py:25
  29.1 2.2 %collective-permute-start.9 = (bf16[2,4,3,16,512]{4,3,2,1,0:T(8,128)(2,1)S(1)}, bf16[2,4,3,16,512]{4,3,2,1,0:T(8,128)(2,1)S(1)}, u32[]{:S(2)}, u32[]{:S(2)}) collective-permute-start(bf16[2,4,3,16,512]{4,3,2,1,0:T(8,128)(2,1)S(1)} %pad_maximum_fusion.2.rest_0_), channel_id=1, source_target_pairs={{0,48},{1,49},{2,50},{3,51},{4,52},{5,53},{6,54},{7,55},{8,56},{9,... | collective-permute-start | bytes 1179656 | tf_op jit(solution)/shard_map/ppermute | solution.py:25
  33.0 4.3 %collective-permute-done.9.rest_3_ = bf16[2,4,3,16,512]{4,3,2,1,0:T(8,128)(2,1)S(1)} collective-permute-done((bf16[2,4,3,16,512]{4,3,2,1,0:T(8,128)(2,1)S(1)}, bf16[2,4,3,16,512]{4,3,2,1,0:T(8,128)(2,1)S(1)}, u32[]{:S(2)}, u32[]{:S(2)}) %collective-permute-start.9) | collective-permute-done | bytes 393248 | tf_op jit(solution)/shard_map/ppermute | solution.py:25
  39.6 5.9 %collective-permute-done.6.halo = bf16[2,512,512]{2,1,0:T(8,128)(2,1)S(1)} collective-permute-done((bf16[2,512,512]{2,1,0:T(8,128)(2,1)S(1)}, bf16[2,512,512]{2,1,0:T(8,128)(2,1)S(1)}, u32[]{:S(2)}, u32[]{:S(2)}) %collective-permute-start.6) | collective-permute-done | bytes 1048608 | tf_op jit(solution)/shard_map/ppermute | solution.py:31
  47.0 8.3 %shard_map.111 = (f32[3,64,512]{2,1,0:T(8,128)}, bf16[3,64,512]{2,1,0:T(8,128)(2,1)}, bf16[3,64,512]{2,1,0:T(8,128)(2,1)}, bf16[3,64,512]{2,1,0:T(8,128)(2,1)}, ...) custom-call(s32[16]{0:T(128)} %stack.168.s_ref, ...), custom_call_target="tpu_custom_call" | custom-call | flops 3221225472 | bytes 4722688 | tf_op jit(solution)/shard_map/pallas_call | solution.py:74
  60.1 3.0 %collective-permute-start.17 = (bf16[3,64,512]{2,1,0:T(8,128)(2,1)S(1)}, bf16[3,64,512]{2,1,0:T(8,128)(2,1)S(1)}, u32[]{:S(2)}, u32[]{:S(2)}) collective-permute-start(bf16[3,64,512]{2,1,0:T(8,128)(2,1)S(1)} %copy-done.31), channel_id=1, source_target_pairs={{0,32},{1,33},{2,34},{3,35},{4,36},{5,37},{6,38},{7,39},{8,40},{9,... | collective-permute-start | bytes 589832 | tf_op jit(solution)/shard_map/ppermute | solution.py:25
  63.3 2.8 %collective-permute-start.19 = (bf16[3,64,512]{2,1,0:T(8,128)(2,1)S(1)}, bf16[3,64,512]{2,1,0:T(8,128)(2,1)S(1)}, u32[]{:S(2)}, u32[]{:S(2)}) collective-permute-start(bf16[3,64,512]{2,1,0:T(8,128)(2,1)S(1)} %copy-done.29), channel_id=1, source_target_pairs={{0,48},{1,49},{2,50},{3,51},{4,52},{5,53},{6,54},{7,55},{8,56},{9,... | collective-permute-start | bytes 589832 | tf_op jit(solution)/shard_map/ppermute | solution.py:25
  68.5 2.6 %collective-permute-done.17.rest_3_ = bf16[3,64,512]{2,1,0:T(8,128)(2,1)S(1)} collective-permute-done((bf16[3,64,512]{2,1,0:T(8,128)(2,1)S(1)}, bf16[3,64,512]{2,1,0:T(8,128)(2,1)S(1)}, u32[]{:S(2)}, u32[]{:S(2)}) %collective-permute-start.17) | collective-permute-done | bytes 196640 | tf_op jit(solution)/shard_map/ppermute | solution.py:25
  71.1 5.3 %collective-permute-done.18.rest_4_ = bf16[3,64,512]{2,1,0:T(8,128)(2,1)S(1)} collective-permute-done((bf16[3,64,512]{2,1,0:T(8,128)(2,1)S(1)}, bf16[3,64,512]{2,1,0:T(8,128)(2,1)S(1)}, u32[]{:S(2)}, u32[]{:S(2)}) %collective-permute-start.18) | collective-permute-done | bytes 196640 | tf_op jit(solution)/shard_map/ppermute | solution.py:25
  76.5 5.7 %collective-permute-done.20.rest_6_ = bf16[3,64,512]{2,1,0:T(8,128)(2,1)S(1)} collective-permute-done((bf16[3,64,512]{2,1,0:T(8,128)(2,1)S(1)}, bf16[3,64,512]{2,1,0:T(8,128)(2,1)S(1)}, u32[]{:S(2)}, u32[]{:S(2)}) %collective-permute-start.20) | collective-permute-done | bytes 196640 | tf_op jit(solution)/shard_map/ppermute | solution.py:25
  82.9 3.2 %shard_map.113 = (f32[3,16,512]{2,1,0:T(8,128)}, bf16[3,16,512]{2,1,0:T(8,128)(2,1)}, bf16[3,16,512]{2,1,0:T(8,128)(2,1)}, bf16[3,16,512]{2,1,0:T(8,128)(2,1)}) custom-call(s32[16]{0:T(128)} %stack.168.s_ref, f32[3,64,512]{2,1,0:T(8,128)} %get-tuple-element.46.own, bf16[3,64,512]{2,1,0:T(8,128)(2,1)} %copy-done.12, bf16[3,64,512]{2,1,0:T(8,128)(2,1)} %copy-done.13, ...), custom_call_target="tpu_custom_call" | custom-call | bytes 1769472 | tf_op jit(solution)/shard_map/pallas_call | solution.py:74
  86.9 3.5 %collective-permute-start.23 = (bf16[3,16,512]{2,1,0:T(8,128)(2,1)}, bf16[3,16,512]{2,1,0:T(8,128)(2,1)S(1)}, u32[]{:S(2)}, u32[]{:S(2)}) collective-permute-start(bf16[3,16,512]{2,1,0:T(8,128)(2,1)} %get-tuple-element.58), channel_id=1, source_target_pairs={{0,4},{1,5},{2,6},{3,7},{4,0},{5,1},{6,2},{7,3},{8,12},{9,13},{10,... | collective-permute-start | bytes 147464 | tf_op jit(solution)/shard_map/ppermute | solution.py:25
  94.6 2.1 %collective-permute-done.24.three = bf16[3,16,512]{2,1,0:T(8,128)(2,1)S(1)} collective-permute-done((bf16[3,16,512]{2,1,0:T(8,128)(2,1)}, bf16[3,16,512]{2,1,0:T(8,128)(2,1)S(1)}, u32[]{:S(2)}, u32[]{:S(2)}) %collective-permute-start.24) | collective-permute-done | bytes 49184 | tf_op jit(solution)/shard_map/ppermute | solution.py:25
  97.3 2.4 %shard_map.114 = (f32[3,16,512]{2,1,0:T(8,128)}, bf16[3,16,512]{2,1,0:T(8,128)(2,1)}) custom-call(s32[16]{0:T(128)} %stack.168.s_ref, f32[3,16,512]{2,1,0:T(8,128)} %get-tuple-element.56.own, bf16[3,16,512]{2,1,0:T(8,128)(2,1)} %copy-done.19, bf16[3,16,512]{2,1,0:T(8,128)(2,1)} %copy-done.20, bf16[3,16,512]{2,1,0:T(8,128)(2,1)} %copy-done.21, ...), custom_call_target="tpu_custom_call" | custom-call | bytes 344064 | tf_op jit(solution)/shard_map/pallas_call | solution.py:74
  100.9 3.1 %collective-permute-start.26 = (bf16[3,16,512]{2,1,0:T(8,128)(2,1)}, bf16[3,16,512]{2,1,0:T(8,128)(2,1)S(1)}, u32[]{:S(2)}, u32[]{:S(2)}) collective-permute-start(bf16[3,16,512]{2,1,0:T(8,128)(2,1)} %get-tuple-element.60), channel_id=1, source_target_pairs={{0,4},{1,5},{2,6},{3,7},{4,0},{5,1},{6,2},{7,3},{8,12},{9,13},{10,... | collective-permute-start | bytes 147464 | tf_op jit(solution)/shard_map/ppermute | solution.py:25
  105.4 2.6 %collective-permute-done.26 = bf16[3,16,512]{2,1,0:T(8,128)(2,1)S(1)} collective-permute-done((bf16[3,16,512]{2,1,0:T(8,128)(2,1)}, bf16[3,16,512]{2,1,0:T(8,128)(2,1)S(1)}, u32[]{:S(2)}, u32[]{:S(2)}) %collective-permute-start.26) | collective-permute-done | bytes 49184 | tf_op jit(solution)/shard_map/ppermute | solution.py:25
  112.2 3.9 %collective-permute-done.29 = bf16[4,3,16,512]{3,2,1,0:T(8,128)(2,1)S(1)} collective-permute-done((bf16[4,3,16,512]{3,2,1,0:T(8,128)(2,1)S(1)}, bf16[4,3,16,512]{3,2,1,0:T(8,128)(2,1)S(1)}, u32[]{:S(2)}, u32[]{:S(2)}) %collective-permute-start.29) | collective-permute-done | bytes 196640 | tf_op jit(solution)/shard_map/ppermute | solution.py:25
  116.1 2.6 %collective-permute-start.30 = (bf16[2,4,3,16,512]{4,3,2,1,0:T(8,128)(2,1)S(1)}, bf16[2,4,3,16,512]{4,3,2,1,0:T(8,128)(2,1)S(1)}, u32[]{:S(2)}, u32[]{:S(2)}) collective-permute-start(bf16[2,4,3,16,512]{4,3,2,1,0:T(8,128)(2,1)S(1)} %pad_maximum_fusion.3.rest_0_), channel_id=1, source_target_pairs={{0,16},{1,17},{2,18},{3,19},{4,20},{5,21},{6,22},{7,23},{8,24},{9,... | collective-permute-start | bytes 1179656 | tf_op jit(solution)/shard_map/ppermute | solution.py:25
  121.3 4.7 %shard_map.112.attn_other = f32[512,512]{1,0:T(8,128)} custom-call(s32[16]{0:T(128)} %stack.168.s_ref, bf16[512,1024]{1,0:T(8,128)(2,1)} %q_own.1, bf16[512,1024]{1,0:T(8,128)(2,1)} %k_ref.3, bf16[512,1024]{1,0:T(8,128)(2,1)} %v_ref.3, bf16[2,512,512]{2,1,0:T(8,128)(2,1)} %copy-done.6), custom_call_target="tpu_custom_call" | custom-call | flops 805306368 | bytes 4194304 | tf_op jit(solution)/shard_map/pallas_call | solution.py:74
  126.0 5.8 %collective-permute-done.28.rest_0_ = bf16[2,512,512]{2,1,0:T(8,128)(2,1)S(1)} collective-permute-done((bf16[2,512,512]{2,1,0:T(8,128)(2,1)S(1)}, bf16[2,512,512]{2,1,0:T(8,128)(2,1)S(1)}, u32[]{:S(2)}, u32[]{:S(2)}) %collective-permute-start.28) | collective-permute-done | bytes 1048608 | tf_op jit(solution)/shard_map/ppermute | solution.py:41
  132.8 5.0 %shard_map.115.attn_own = f32[512,512]{1,0:T(8,128)} custom-call(s32[16]{0:T(128)} %stack.168.s_ref, bf16[512,1024]{1,0:T(8,128)(2,1)} %q_own.1, bf16[512,1024]{1,0:T(8,128)(2,1)} %k_ref.3, bf16[512,1024]{1,0:T(8,128)(2,1)} %v_ref.3, bf16[2,512,512]{2,1,0:T(8,128)(2,1)} %copy-done.2, bf16[2,512,512]{2,1,0:T(8,128)(2,1)} %copy-done.3), custom_call_target="tpu_custom_call" | custom-call | flops 805306368 | bytes 5242880 | tf_op jit(solution)/shard_map/pallas_call | solution.py:74
  138.8 5.1 %shard_map.116 = (bf16[512,512]{1,0:T(8,128)(2,1)}, bf16[512,512]{1,0:T(8,128)(2,1)}, f32[2,512]{1,0:T(2,128)}, f32[3,16,512]{2,1,0:T(8,128)}) custom-call(s32[16]{0:T(128)} %stack.168.s_ref, bf16[512,512]{1,0:T(8,128)(2,1)} %copy-done.23, bf16[512,1024]{1,0:T(8,128)(2,1)} %q_own.1, f32[3,512]{1,0:T(4,128)} %get-tuple-element.42.old_sq, ...), custom_call_target="tpu_custom_call" | custom-call | flops 1610612736 | bytes 3250176 | tf_op jit(solution)/shard_map/pallas_call | solution.py:74
  143.9 7.1 %collective-permute-start.34 = (f32[2,512]{1,0:T(2,128)}, f32[2,512]{1,0:T(2,128)S(1)}, u32[]{:S(2)}, u32[]{:S(2)}) collective-permute-start(f32[2,512]{1,0:T(2,128)} %get-tuple-element.67), channel_id=1, source_target_pairs={{0,64},{64,0},{128,192},{192,128},{1,65},{65,1},{129,193},{193,129... | collective-permute-start | bytes 12296 | tf_op jit(solution)/shard_map/ppermute | solution.py:355
  151.0 2.9 %collective-permute-start.35 = (f32[2,512]{1,0:T(2,128)}, f32[2,512]{1,0:T(2,128)S(1)}, u32[]{:S(2)}, u32[]{:S(2)}) collective-permute-start(f32[2,512]{1,0:T(2,128)} %get-tuple-element.67), channel_id=1, source_target_pairs={{0,128},{64,192},{128,0},{192,64},{1,129},{65,193},{129,1},{193,65... | collective-permute-start | bytes 12296 | tf_op jit(solution)/shard_map/ppermute | solution.py:355
  155.2 3.4 %collective-permute-done.36 = f32[2,512]{1,0:T(2,128)S(1)} collective-permute-done((f32[2,512]{1,0:T(2,128)}, f32[2,512]{1,0:T(2,128)S(1)}, u32[]{:S(2)}, u32[]{:S(2)}) %collective-permute-start.36) | collective-permute-done | bytes 4128 | tf_op jit(solution)/shard_map/ppermute | solution.py:355
  161.8 6.0 %collective-permute-done.37 = f32[1,512]{1,0:T(1,128)S(1)} collective-permute-done((f32[1,512]{1,0:T(1,128)S(1)}, f32[1,512]{1,0:T(1,128)S(1)}, u32[]{:S(2)}, u32[]{:S(2)}) %collective-permute-start.37) | collective-permute-done | bytes 2080 | tf_op jit(solution)/shard_map/ppermute | solution.py:31
  169.7 4.0 %shard_map.117 = bf16[512,1024]{1,0:T(8,128)(2,1)} custom-call(s32[16]{0:T(128)} %stack.168.s_ref, bf16[512,512]{1,0:T(8,128)(2,1)} %get-tuple-element.65.f_own, bf16[512,512]{1,0:T(8,128)(2,1)} %copy-done.7, f32[512,512]{1,0:T(8,128)} %shard_map.115.attn_own, f32[512,512]{1,0:T(8,128)} %shard_map.112.attn_other, f32[1,512]{1,0:T(1,128)} %slice_add_fusion.sums, ...), custom_call_target="tpu_custom_call" | custom-call | bytes 3151872 | tf_op jit(solution)/shard_map/pallas_call | solution.py:74
  (142 shorter events, 46.6 us)
Async XLA Ops:
  1.5 6.7 %collective-permute-start = (f32[3,8,512]{2,1,0:T(8,128)S(1)}, f32[3,8,512]{2,1,0:T(8,128)S(1)}, u32[]{:S(2)}, u32[]{:S(2)}) collective-permute-start(f32[3,8,512]{2,1,0:T(8,128)S(1)} %get-tuple-element.83), channel_id=1, source_target_pairs={{0,1},{1,0},{2,3},{3,2},{4,5},{5,4},{6,7},{7,6},{8,9},{9,8},{10,11... | collective-permute-start | bytes 147464 | tf_op jit(solution)/shard_map/ppermute | solution.py:25
  6.6 15.3 %collective-permute-start.5 = (bf16[512,512]{1,0:T(8,128)(2,1)S(1)}, bf16[512,512]{1,0:T(8,128)(2,1)S(1)}, u32[]{:S(2)}, u32[]{:S(2)}) collective-permute-start(bf16[512,512]{1,0:T(8,128)(2,1)S(1)} %get-tuple-element.76), channel_id=1, source_target_pairs={{7,15},{15,23},{23,31},{31,39},{39,47},{47,55},{55,63},{71,79},{79... | collective-permute-start | bytes 1572872 | tf_op jit(solution)/shard_map/ppermute | solution.py:36
  10.2 6.1 %collective-permute-start.2 = (bf16[3,16,512]{2,1,0:T(8,128)(2,1)S(1)}, bf16[3,16,512]{2,1,0:T(8,128)(2,1)S(1)}, u32[]{:S(2)}, u32[]{:S(2)}) collective-permute-start(bf16[3,16,512]{2,1,0:T(8,128)(2,1)S(1)} %get-tuple-element.37), channel_id=1, source_target_pairs={{0,2},{1,3},{2,0},{3,1},{4,6},{5,7},{6,4},{7,5},{8,10},{9,11},{10,... | collective-permute-start | bytes 147464 | tf_op jit(solution)/shard_map/ppermute | solution.py:25
  11.8 6.9 %collective-permute-start.3 = (bf16[3,16,512]{2,1,0:T(8,128)(2,1)S(1)}, bf16[3,16,512]{2,1,0:T(8,128)(2,1)S(1)}, u32[]{:S(2)}, u32[]{:S(2)}) collective-permute-start(bf16[3,16,512]{2,1,0:T(8,128)(2,1)S(1)} %get-tuple-element.37), channel_id=1, source_target_pairs={{0,4},{1,5},{2,6},{3,7},{4,0},{5,1},{6,2},{7,3},{8,12},{9,13},{10,... | collective-permute-start | bytes 147464 | tf_op jit(solution)/shard_map/ppermute | solution.py:25
  21.9 23.6 %collective-permute-start.6 = (bf16[2,512,512]{2,1,0:T(8,128)(2,1)S(1)}, bf16[2,512,512]{2,1,0:T(8,128)(2,1)S(1)}, u32[]{:S(2)}, u32[]{:S(2)}) collective-permute-start(bf16[2,512,512]{2,1,0:T(8,128)(2,1)S(1)} %pad_maximum_fusion), channel_id=1, source_target_pairs={{0,1},{1,2},{2,3},{3,4},{4,5},{5,6},{6,7},{7,0},{8,9},{9,10},{10,1... | collective-permute-start | bytes 3145736 | tf_op jit(solution)/shard_map/ppermute | solution.py:31
  29.1 8.2 %collective-permute-start.9 = (bf16[2,4,3,16,512]{4,3,2,1,0:T(8,128)(2,1)S(1)}, bf16[2,4,3,16,512]{4,3,2,1,0:T(8,128)(2,1)S(1)}, u32[]{:S(2)}, u32[]{:S(2)}) collective-permute-start(bf16[2,4,3,16,512]{4,3,2,1,0:T(8,128)(2,1)S(1)} %pad_maximum_fusion.2.rest_0_), channel_id=1, source_target_pairs={{0,48},{1,49},{2,50},{3,51},{4,52},{5,53},{6,54},{7,55},{8,56},{9,... | collective-permute-start | bytes 1179656 | tf_op jit(solution)/shard_map/ppermute | solution.py:25
  31.3 15.7 %collective-permute-start.11 = (bf16[2,4,3,16,512]{4,3,2,1,0:T(8,128)(2,1)S(1)}, bf16[2,4,3,16,512]{4,3,2,1,0:T(8,128)(2,1)}, u32[]{:S(2)}, u32[]{:S(2)}) collective-permute-start(bf16[2,4,3,16,512]{4,3,2,1,0:T(8,128)(2,1)S(1)} %pad_maximum_fusion.2.rest_0_), channel_id=1, source_target_pairs={{0,16},{1,17},{2,18},{3,19},{4,20},{5,21},{6,22},{7,23},{8,24},{9,... | collective-permute-start | bytes 1179656 | tf_op jit(solution)/shard_map/ppermute | solution.py:25
  31.3 15.7 %collective-permute-start.12 = (bf16[2,4,3,16,512]{4,3,2,1,0:T(8,128)(2,1)S(1)}, bf16[2,4,3,16,512]{4,3,2,1,0:T(8,128)(2,1)}, u32[]{:S(2)}, u32[]{:S(2)}) collective-permute-start(bf16[2,4,3,16,512]{4,3,2,1,0:T(8,128)(2,1)S(1)} %pad_maximum_fusion.2.rest_0_), channel_id=1, source_target_pairs={{0,32},{1,33},{2,34},{3,35},{4,36},{5,37},{6,38},{7,39},{8,40},{9,... | collective-permute-start | bytes 1179656 | tf_op jit(solution)/shard_map/ppermute | solution.py:25
  37.3 22.8 %collective-permute-start.10 = (bf16[512,512]{1,0:T(8,128)(2,1)}, bf16[512,512]{1,0:T(8,128)(2,1)}, u32[]{:S(2)}, u32[]{:S(2)}) collective-permute-start(bf16[512,512]{1,0:T(8,128)(2,1)} %get-tuple-element.41), channel_id=1, source_target_pairs={{7,15},{15,23},{23,31},{31,39},{39,47},{47,55},{55,63},{71,79},{79... | collective-permute-start | bytes 1572872 | tf_op jit(solution)/shard_map/ppermute | solution.py:36
  45.5 17.6 %collective-permute-start.7 = (bf16[512,512]{1,0:T(8,128)(2,1)}, bf16[512,512]{1,0:T(8,128)(2,1)S(1)}, u32[]{:S(2)}, u32[]{:S(2)}) collective-permute-start(bf16[512,512]{1,0:T(8,128)(2,1)} %slice_select_fusion), channel_id=1, source_target_pairs={{0,1},{1,2},{2,3},{3,4},{4,5},{5,6},{6,7},{7,0},{8,9},{9,10},{10,1... | collective-permute-start | bytes 1572872 | tf_op jit(solution)/shard_map/ppermute | solution.py:31
  55.3 8.0 %collective-permute-start.14 = (bf16[3,64,512]{2,1,0:T(8,128)(2,1)}, bf16[3,64,512]{2,1,0:T(8,128)(2,1)S(1)}, u32[]{:S(2)}, u32[]{:S(2)}) collective-permute-start(bf16[3,64,512]{2,1,0:T(8,128)(2,1)} %get-tuple-element.47), channel_id=1, source_target_pairs={{0,8},{1,9},{2,10},{3,11},{4,12},{5,13},{6,14},{7,15},{8,0},{9,1},... | collective-permute-start | bytes 589832 | tf_op jit(solution)/shard_map/ppermute | solution.py:25
  56.8 9.3 %collective-permute-start.15 = (bf16[3,64,512]{2,1,0:T(8,128)(2,1)}, bf16[3,64,512]{2,1,0:T(8,128)(2,1)S(1)}, u32[]{:S(2)}, u32[]{:S(2)}) collective-permute-start(bf16[3,64,512]{2,1,0:T(8,128)(2,1)} %get-tuple-element.48), channel_id=1, source_target_pairs={{0,16},{1,17},{2,18},{3,19},{4,20},{5,21},{6,22},{7,23},{8,24},{9,... | collective-permute-start | bytes 589832 | tf_op jit(solution)/shard_map/ppermute | solution.py:25
  59.2 9.2 %collective-permute-start.16 = (bf16[3,64,512]{2,1,0:T(8,128)(2,1)S(1)}, bf16[3,64,512]{2,1,0:T(8,128)(2,1)S(1)}, u32[]{:S(2)}, u32[]{:S(2)}) collective-permute-start(bf16[3,64,512]{2,1,0:T(8,128)(2,1)S(1)} %copy-done.32), channel_id=1, source_target_pairs={{0,24},{1,25},{2,26},{3,27},{4,28},{5,29},{6,30},{7,31},{8,16},{9,... | collective-permute-start | bytes 589832 | tf_op jit(solution)/shard_map/ppermute | solution.py:25
  60.1 11.0 %collective-permute-start.17 = (bf16[3,64,512]{2,1,0:T(8,128)(2,1)S(1)}, bf16[3,64,512]{2,1,0:T(8,128)(2,1)S(1)}, u32[]{:S(2)}, u32[]{:S(2)}) collective-permute-start(bf16[3,64,512]{2,1,0:T(8,128)(2,1)S(1)} %copy-done.31), channel_id=1, source_target_pairs={{0,32},{1,33},{2,34},{3,35},{4,36},{5,37},{6,38},{7,39},{8,40},{9,... | collective-permute-start | bytes 589832 | tf_op jit(solution)/shard_map/ppermute | solution.py:25
  63.1 13.3 %collective-permute-start.18 = (bf16[3,64,512]{2,1,0:T(8,128)(2,1)S(1)}, bf16[3,64,512]{2,1,0:T(8,128)(2,1)S(1)}, u32[]{:S(2)}, u32[]{:S(2)}) collective-permute-start(bf16[3,64,512]{2,1,0:T(8,128)(2,1)S(1)} %copy-done.30), channel_id=1, source_target_pairs={{0,40},{1,41},{2,42},{3,43},{4,44},{5,45},{6,46},{7,47},{8,32},{9,... | collective-permute-start | bytes 589832 | tf_op jit(solution)/shard_map/ppermute | solution.py:25
  63.3 13.2 %collective-permute-start.19 = (bf16[3,64,512]{2,1,0:T(8,128)(2,1)S(1)}, bf16[3,64,512]{2,1,0:T(8,128)(2,1)S(1)}, u32[]{:S(2)}, u32[]{:S(2)}) collective-permute-start(bf16[3,64,512]{2,1,0:T(8,128)(2,1)S(1)} %copy-done.29), channel_id=1, source_target_pairs={{0,48},{1,49},{2,50},{3,51},{4,52},{5,53},{6,54},{7,55},{8,56},{9,... | collective-permute-start | bytes 589832 | tf_op jit(solution)/shard_map/ppermute | solution.py:25
  66.1 16.1 %collective-permute-start.20 = (bf16[3,64,512]{2,1,0:T(8,128)(2,1)S(1)}, bf16[3,64,512]{2,1,0:T(8,128)(2,1)S(1)}, u32[]{:S(2)}, u32[]{:S(2)}) collective-permute-start(bf16[3,64,512]{2,1,0:T(8,128)(2,1)S(1)} %copy-done.28), channel_id=1, source_target_pairs={{0,56},{1,57},{2,58},{3,59},{4,60},{5,61},{6,62},{7,63},{8,48},{9,... | collective-permute-start | bytes 589832 | tf_op jit(solution)/shard_map/ppermute | solution.py:25
  68.4 24.1 %collective-permute-start.13 = (bf16[2,512,512]{2,1,0:T(8,128)(2,1)S(1)}, bf16[2,512,512]{2,1,0:T(8,128)(2,1)S(1)}, u32[]{:S(2)}, u32[]{:S(2)}) collective-permute-start(bf16[2,512,512]{2,1,0:T(8,128)(2,1)S(1)} %maximum_select_fusion), channel_id=1, source_target_pairs={{0,1},{1,2},{2,3},{3,4},{4,5},{5,6},{6,7},{7,0},{8,9},{9,10},{10,1... | collective-permute-start | bytes 3145736 | tf_op jit(solution)/shard_map/ppermute | solution.py:31
  86.0 24.1 %collective-permute-start.21 = (bf16[2,512,512]{2,1,0:T(8,128)(2,1)S(1)}, bf16[2,512,512]{2,1,0:T(8,128)(2,1)S(1)}, u32[]{:S(2)}, u32[]{:S(2)}) collective-permute-start(bf16[2,512,512]{2,1,0:T(8,128)(2,1)S(1)} %copy-done.5), channel_id=1, source_target_pairs={{7,15},{15,23},{23,31},{31,39},{39,47},{47,55},{55,63},{71,79},{79... | collective-permute-start | bytes 3145736 | tf_op jit(solution)/shard_map/ppermute | solution.py:36
  86.8 5.8 %collective-permute-start.22 = (bf16[3,16,512]{2,1,0:T(8,128)(2,1)}, bf16[3,16,512]{2,1,0:T(8,128)(2,1)S(1)}, u32[]{:S(2)}, u32[]{:S(2)}) collective-permute-start(bf16[3,16,512]{2,1,0:T(8,128)(2,1)} %get-tuple-element.57), channel_id=1, source_target_pairs={{0,2},{1,3},{2,0},{3,1},{4,6},{5,7},{6,4},{7,5},{8,10},{9,11},{10,... | collective-permute-start | bytes 147464 | tf_op jit(solution)/shard_map/ppermute | solution.py:25
  86.9 7.7 %collective-permute-start.23 = (bf16[3,16,512]{2,1,0:T(8,128)(2,1)}, bf16[3,16,512]{2,1,0:T(8,128)(2,1)S(1)}, u32[]{:S(2)}, u32[]{:S(2)}) collective-permute-start(bf16[3,16,512]{2,1,0:T(8,128)(2,1)} %get-tuple-element.58), channel_id=1, source_target_pairs={{0,4},{1,5},{2,6},{3,7},{4,0},{5,1},{6,2},{7,3},{8,12},{9,13},{10,... | collective-permute-start | bytes 147464 | tf_op jit(solution)/shard_map/ppermute | solution.py:25
  90.4 6.3 %collective-permute-start.24 = (bf16[3,16,512]{2,1,0:T(8,128)(2,1)}, bf16[3,16,512]{2,1,0:T(8,128)(2,1)S(1)}, u32[]{:S(2)}, u32[]{:S(2)}) collective-permute-start(bf16[3,16,512]{2,1,0:T(8,128)(2,1)} %get-tuple-element.59), channel_id=1, source_target_pairs={{0,6},{1,7},{2,4},{3,5},{4,2},{5,3},{6,0},{7,1},{8,14},{9,15},{10,... | collective-permute-start | bytes 147464 | tf_op jit(solution)/shard_map/ppermute | solution.py:25
  99.7 5.7 %collective-permute-start.25 = (bf16[3,16,512]{2,1,0:T(8,128)(2,1)}, bf16[3,16,512]{2,1,0:T(8,128)(2,1)S(1)}, u32[]{:S(2)}, u32[]{:S(2)}) collective-permute-start(bf16[3,16,512]{2,1,0:T(8,128)(2,1)} %get-tuple-element.60), channel_id=1, source_target_pairs={{0,2},{1,3},{2,0},{3,1},{4,6},{5,7},{6,4},{7,5},{8,10},{9,11},{10,... | collective-permute-start | bytes 147464 | tf_op jit(solution)/shard_map/ppermute | solution.py:25
  100.9 7.1 %collective-permute-start.26 = (bf16[3,16,512]{2,1,0:T(8,128)(2,1)}, bf16[3,16,512]{2,1,0:T(8,128)(2,1)S(1)}, u32[]{:S(2)}, u32[]{:S(2)}) collective-permute-start(bf16[3,16,512]{2,1,0:T(8,128)(2,1)} %get-tuple-element.60), channel_id=1, source_target_pairs={{0,4},{1,5},{2,6},{3,7},{4,0},{5,1},{6,2},{7,3},{8,12},{9,13},{10,... | collective-permute-start | bytes 147464 | tf_op jit(solution)/shard_map/ppermute | solution.py:25
  110.2 21.6 %collective-permute-start.28 = (bf16[2,512,512]{2,1,0:T(8,128)(2,1)S(1)}, bf16[2,512,512]{2,1,0:T(8,128)(2,1)S(1)}, u32[]{:S(2)}, u32[]{:S(2)}) collective-permute-start(bf16[2,512,512]{2,1,0:T(8,128)(2,1)S(1)} %collective-permute-done.21), channel_id=1, source_target_pairs={{7,0},{15,8},{23,16},{31,24},{39,32},{47,40},{55,48},{63,56},{71,6... | collective-permute-start | bytes 3145736 | tf_op jit(solution)/shard_map/ppermute | solution.py:41
  116.1 21.6 %collective-permute-start.30 = (bf16[2,4,3,16,512]{4,3,2,1,0:T(8,128)(2,1)S(1)}, bf16[2,4,3,16,512]{4,3,2,1,0:T(8,128)(2,1)S(1)}, u32[]{:S(2)}, u32[]{:S(2)}) collective-permute-start(bf16[2,4,3,16,512]{4,3,2,1,0:T(8,128)(2,1)S(1)} %pad_maximum_fusion.3.rest_0_), channel_id=1, source_target_pairs={{0,16},{1,17},{2,18},{3,19},{4,20},{5,21},{6,22},{7,23},{8,24},{9,... | collective-permute-start | bytes 1179656 | tf_op jit(solution)/shard_map/ppermute | solution.py:25
  118.8 19.0 %collective-permute-start.31 = (bf16[2,4,3,16,512]{4,3,2,1,0:T(8,128)(2,1)S(1)}, bf16[2,4,3,16,512]{4,3,2,1,0:T(8,128)(2,1)S(1)}, u32[]{:S(2)}, u32[]{:S(2)}) collective-permute-start(bf16[2,4,3,16,512]{4,3,2,1,0:T(8,128)(2,1)S(1)} %pad_maximum_fusion.3.rest_0_), channel_id=1, source_target_pairs={{0,32},{1,33},{2,34},{3,35},{4,36},{5,37},{6,38},{7,39},{8,40},{9,... | collective-permute-start | bytes 1179656 | tf_op jit(solution)/shard_map/ppermute | solution.py:25
  119.4 18.4 %collective-permute-start.32 = (bf16[2,4,3,16,512]{4,3,2,1,0:T(8,128)(2,1)S(1)}, bf16[2,4,3,16,512]{4,3,2,1,0:T(8,128)(2,1)S(1)}, u32[]{:S(2)}, u32[]{:S(2)}) collective-permute-start(bf16[2,4,3,16,512]{4,3,2,1,0:T(8,128)(2,1)S(1)} %pad_maximum_fusion.3.rest_0_), channel_id=1, source_target_pairs={{0,48},{1,49},{2,50},{3,51},{4,52},{5,53},{6,54},{7,55},{8,56},{9,... | collective-permute-start | bytes 1179656 | tf_op jit(solution)/shard_map/ppermute | solution.py:25
  143.9 10.3 %collective-permute-start.34 = (f32[2,512]{1,0:T(2,128)}, f32[2,512]{1,0:T(2,128)S(1)}, u32[]{:S(2)}, u32[]{:S(2)}) collective-permute-start(f32[2,512]{1,0:T(2,128)} %get-tuple-element.67), channel_id=1, source_target_pairs={{0,64},{64,0},{128,192},{192,128},{1,65},{65,1},{129,193},{193,129... | collective-permute-start | bytes 12296 | tf_op jit(solution)/shard_map/ppermute | solution.py:355
  154.2 14.7 %collective-permute-start.33 = (bf16[512,512]{1,0:T(8,128)(2,1)}, bf16[512,512]{1,0:T(8,128)(2,1)S(1)}, u32[]{:S(2)}, u32[]{:S(2)}) collective-permute-start(bf16[512,512]{1,0:T(8,128)(2,1)} %get-tuple-element.66), channel_id=1, source_target_pairs={{0,7},{1,0},{2,1},{3,2},{4,3},{5,4},{6,5},{7,6},{8,15},{9,8},{10,9... | collective-permute-start | bytes 1572872 | tf_op jit(solution)/shard_map/ppermute | solution.py:31
  159.4 8.5 %collective-permute-start.37 = (f32[1,512]{1,0:T(1,128)S(1)}, f32[1,512]{1,0:T(1,128)S(1)}, u32[]{:S(2)}, u32[]{:S(2)}) collective-permute-start(f32[1,512]{1,0:T(1,128)S(1)} %slice.83), channel_id=1, source_target_pairs={{0,7},{1,0},{2,1},{3,2},{4,3},{5,4},{6,5},{7,6},{8,15},{9,8},{10,9... | collective-permute-start | bytes 6152 | tf_op jit(solution)/shard_map/ppermute | solution.py:31
  160.3 8.6 %collective-permute-start.38 = (f32[3,8,512]{2,1,0:T(8,128)S(1)}, f32[3,8,512]{2,1,0:T(8,128)S(1)}, u32[]{:S(2)}, u32[]{:S(2)}) collective-permute-start(f32[3,8,512]{2,1,0:T(8,128)S(1)} %get-tuple-element.82), channel_id=1, source_target_pairs={{0,1},{1,0},{2,3},{3,2},{4,5},{5,4},{6,7},{7,6},{8,9},{9,8},{10,11... | collective-permute-start | bytes 147464 | tf_op jit(solution)/shard_map/ppermute | solution.py:25
  (41 other events, 270.2 us)

commit v3 on v2

--- a/solution.py
+++ b/solution.py
@@ -11,6 +11,7 @@
 HEADS = 8
 HD = 512
 BLK = 512
+TILE = 512
 EPS = 1e-06
 NEG = -1e30
 VMEM_LIMIT = 56 * 1024 * 1024
@@ -112,53 +113,41 @@
 def gradient_kernel(s_ref, halo, k_own, v_own, rate_prev, rate_own, *rest):
     blocks, rest = rest[:XY // 2], rest[XY // 2:]
     own_out, outs, old_sq = rest[0], rest[1:XY], rest[XY]
-    w_rows, k_all, gv, hid, d_gate, d_up, grads = rest[XY + 1:]
+    w_rows, k_all, gv, hid, d_both, grads = rest[XY + 1:]
     fill_rows(s_ref, blocks, w_rows)
     for m in range(3):
         old_sq[m:m + 1, :] = columns_sq(w_rows, m)
     for part in range(2):
-        rows = slice(part * BLK, (part + 1) * BLK)
-        k = halo[0] if part == 0 else k_own[...]
-        v = (halo[1] if part == 0 else v_own[...]).astype(F32)
-        eta = as_column((rate_prev if part == 0 else rate_own)[0:1, :])
-        scaled = jnp.concatenate(
-            [eta * v[:, c * 128:(c + 1) * 128] for c in range(HD // 128)], axis=1
-        ).astype(BF16)
-        k_all[rows, :] = k
-        gv[rows, :] = scaled
-        pre_a = dot(k, w_rows[0])
-        pre_b = dot(k, w_rows[1])
-        back = dot_cols(scaled, w_rows[2])
-        sigma = jax.nn.sigmoid(pre_a)
-        gated = pre_a * sigma
-        hid[rows, :] = (gated * pre_b).astype(BF16)
-        d_gate[rows, :] = (back * pre_b * sigma * (1.0 + pre_a * (1.0 - sigma))).astype(BF16)
-        d_up[rows, :] = (back * gated).astype(BF16)
-    grads[0] = dot_rows(k_all[...], d_gate[...])
-    grads[1] = dot_rows(k_all[...], d_up[...])
+        eta_all = as_column((rate_prev if part == 0 else rate_own)[0:1, :])
+        for at in range(0, BLK, TILE):
+            rows = slice(part * BLK + at, part * BLK + at + TILE)
+            here = slice(at, at + TILE)
+            k = halo[0, here, :] if part == 0 else k_own[here, :]
+            v = (halo[1, here, :] if part == 0 else v_own[here, :]).astype(F32)
+            eta = eta_all[here, :]
+            scaled = jnp.concatenate(
+                [eta * v[:, c * 128:(c + 1) * 128] for c in range(HD // 128)], axis=1
+            ).astype(BF16)
+            k_all[rows, :] = k
+            gv[rows, :] = scaled
+            pre_a = dot(k, w_rows[0])
+            pre_b = dot(k, w_rows[1])
+            back = dot_cols(scaled, w_rows[2])
+            sigma = jax.nn.sigmoid(pre_a)
+            gated = pre_a * sigma
+            hid[rows, :] = (gated * pre_b).astype(BF16)
+            gate = back * pre_b * sigma * (1.0 + pre_a * (1.0 - sigma))
+            d_both[rows, :HD] = gate.astype(BF16)
+            d_both[rows, HD:] = (back * gated).astype(BF16)
+    both = dot_rows(k_all[...], d_both[...])
+    grads[0] = both[:, :HD]
+    grads[1] = both[:, HD:]
     grads[2] = dot_rows(hid[...], gv[...])
-    for m in range(3):
-        own_out[m] = grads[m, pl.ds(row_start(s_ref, 4), 64), :]
-        for j, out in enumerate(outs):
-            out[m] = grads[m, pl.ds(row_start(s_ref, 5 + j), 64), :].astype(BF16)
-
-
-def block_sum_kernel(s_ref, own, *rest):
-    parts, outs, total = rest[:XY - 1], rest[XY - 1:XY - 1 + ZQ], rest[-1]
-    acc = own[...]
-    for part in parts:
-        acc = acc + part[...].astype(F32)
-    total[...] = acc
-    for m in range(3):
-        for k, out in enumerate(outs):
-            out[m] = total[m, pl.ds(row_start(s_ref, 12 + k), 16), :].astype(out.dtype)
-
-
-def update_kernel(s_ref, own, one, two, three, w_own, upd, upd_b):
-    total = own[...] + one[...].astype(F32) + two[...].astype(F32) + three[...].astype(F32)
-    total = total + w_own[...]
-    upd[...] = total
-    upd_b[...] = total.astype(BF16)
+    for j, out in enumerate((own_out,) + tuple(outs)):
+        for k in range(ZQ):
+            at = pl.multiple_of(row_start(s_ref, 4 + j) + row_start(s_ref, 12 + k), 16)
+            for m in range(3):
+                out[k, m] = grads[m, pl.ds(at, 16), :].astype(out.dtype)
 
 
 def branch_of(q, u_rows, ratio):
@@ -268,7 +257,7 @@
     rate_mine = jnp.where(even, rate[0:1], rate[1:2])
 
     def gather_zq(chunk):
-        return jnp.stack([chunk] + [move_xor(chunk, k << 1) for k in range(1, ZQ)])
+        return [chunk] + [move_xor(chunk, k << 1) for k in range(1, ZQ)]
 
     def gather_xy(block):
         pair = jnp.stack([block, move_xor(block, 1 << 3)])
@@ -278,9 +267,10 @@
     send_own = jnp.stack([head_of(keys, True), head_of(values, True)])
     plane_k = to_next_plane(keys[:, HD:])
     rate_prev = ring(rate_send, 1)
-    w_block = after(gather_zq(after(w_pair.astype(BF16), rate_prev)), plane_k)
+    w_parts = gather_zq(after(w_pair.astype(BF16), rate_prev))
+    w_block = after(jnp.stack(w_parts), plane_k)
     w_blocks = gather_xy(w_block)
-    halo = ring(after(send_other, w_block), 1)
+    halo = ring(after(send_other, w_parts[1]), 1)
     last = (seq_pos & (RING - 1)) == RING - 1
     plane_v = to_next_plane(after(values[:, HD:], w_blocks[-1]))
     q_prev = ring(after(head_of(queries, False), halo), 1)
@@ -302,9 +292,10 @@
         [halo, keys, values, rate_prev, rate_mine] + w_blocks,
         [whole((2, BLK, HD)), head_block(0), head_block(0), whole((1, BLK)), whole((1, BLK))]
         + block_specs,
-        [shape((3, 64, HD), F32)] + [shape((3, 64, HD), BF16)] * (XY - 1) + [shape((3, HD), F32)],
+        [shape((ZQ, 3, 16, HD), F32)] + [shape((ZQ, 3, 16, HD), BF16)] * (XY - 1) + [shape((3, HD), F32)],
         [pltpu.VMEM((3, HD, HD), BF16)]
-        + [pltpu.VMEM((2 * BLK, HD), BF16)] * 5
+        + [pltpu.VMEM((2 * BLK, HD), BF16)] * 3
+        + [pltpu.VMEM((2 * BLK, 2 * HD), BF16)]
         + [pltpu.VMEM((3, HD, HD), F32)],
         flops=12 * 2 * BLK * HD * HD,
     )
@@ -312,32 +303,23 @@
     arrived = [move_xor(grad_out[j], j << 3) for j in range(1, XY)]
     plane_own = jnp.stack([plane_k, after(plane_v, old_sq)])
     halo_other = ring(jnp.where(last, plane_own, after(send_own, q_prev)), 1)
-    chunks = call(
-        block_sum_kernel,
-        scalars,
-        [grad_out[0]] + arrived,
-        [whole((3, 64, HD))] * XY,
-        [shape((3, 16, HD), F32)] + [shape((3, 16, HD), BF16)] * (ZQ - 1),
-        [pltpu.VMEM((3, 64, HD), F32)],
-    )
-    arrived = [move_xor(chunks[k], k << 1) for k in range(1, ZQ)]
-    upd, upd_b = call(
-        update_kernel,
-        scalars,
-        [after(chunks[0], halo_other)] + arrived + [w_pair],
-        [whole((3, 16, HD))] * 5,
-        [shape((3, 16, HD), F32), shape((3, 16, HD), BF16)],
-    )
-    plane_other = to_next_plane(after(send_other, chunks[0]))
-    u_block = after(gather_zq(upd_b), plane_other)
+    chunks = []
+    for k in range(ZQ):
+        total = grad_out[0][k] + sum(part[k].astype(F32) for part in arrived)
+        chunks.append(total if k == 0 else total.astype(BF16))
+    parts = [move_xor(chunks[k], k << 1) for k in range(1, ZQ)]
+    parts[0] = after(parts[0], halo_other)
+    upd = w_pair + chunks[0] + sum(part.astype(F32) for part in parts)
+    upd_b = upd.astype(BF16)
+    plane_other = to_next_plane(after(send_other, chunks[1]))
+    u_block = after(jnp.stack(gather_zq(upd_b)), plane_other)
     u_blocks = gather_xy(u_block)
     closing = close_ring(after(plane_other, u_block))
     attn_other = attend(1, [halo_other])
-    attn_own = attend(0, [halo, closing])
     f_prev, f_own, sq, new = call(
         apply_kernel,
         scalars,
-        [after(after(q_prev, attn_other), attn_own), queries, old_sq, upd] + u_blocks,
+        [after(q_prev, attn_other), queries, old_sq, upd] + u_blocks,
         [whole((BLK, HD)), head_block(0), whole((3, HD)), whole((3, 16, HD))] + block_specs,
         [
             shape((BLK, HD), BF16),
@@ -353,7 +335,8 @@
     totals = sq
     for k in range(1, heads):
         totals = totals + lax.ppermute(sq, "head", [(i, i ^ k) for i in range(heads)])
-    sums = totals[1:2] + ring(totals[0:1], -1)
+    attn_own = attend(0, [halo, after(closing, totals)])
+    sums = totals[1:2] + after(ring(totals[0:1], -1), attn_own)
     new_mine = jnp.where(even, new[:, :8], new[:, 8:])
     new_theirs = after(move_xor(jnp.where(even, new[:, 8:], new[:, :8]), 1), f_back)
     new_all = jnp.where(
@@ -361,10 +344,11 @@
         jnp.stack([new_mine, new_theirs], axis=1),
         jnp.stack([new_theirs, new_mine], axis=1),
     )
+    gain = out_gain.reshape(1, 2 * HD)
     mixed = call(
         mix_kernel,
         scalars,
-        [f_own, f_back, attn_own, attn_other, sums, out_gain.reshape(1, 2 * HD)],
+        [f_own, f_back, attn_own, attn_other, sums, gain],
         [whole((BLK, HD))] * 4 + [whole((1, BLK)), whole((1, 2 * HD))],
         shape((BLK, 2 * HD), BF16),
     )

time: 175 us -> 166 us (0.949)
  waiting for transfers between devices: 63.4 us -> 52.3 us
  starting transfers between devices: 61.5 us -> 71.3 us
  Pallas kernels: 32.6 us -> 27.1 us
    ppermute x3, starting transfers between devices: 10.3 us -> 16.7 us  [local(): lax.ppermute(sq, 'head', [(i, i ^ k) for i in range(heads)])]
    ppermute x1, waiting for transfers between devices: 5.84 us -> 0.01 us  [close_ring(): lax.ppermute(value, 'seq', [(i, i - RING + 1) for i in range(RING - 1, n,...]
    pallas_call x7 -> x5, Pallas kernels: 32.6 us -> 27.1 us  [call(): pl.pallas_call(kernel, out_shape=outs, grid_spec=pltpu.PrefetchScalarGrid...]
    ppermute x26, starting transfers between devices: 43.1 us -> 45.7 us  [move_xor(): return lax.ppermute(value, 'seq', [(i, i ^ mask) for i in range(n)])]
    ppermute x3, waiting for transfers between devices: 4.41 us -> 2.08 us  [local(): lax.ppermute(sq, 'head', [(i, i ^ k) for i in range(heads)])]
    ppermute x26, waiting for transfers between devices: 39.8 us -> 37.8 us  [move_xor(): return lax.ppermute(value, 'seq', [(i, i ^ mask) for i in range(n)])]
    unnamed x68 -> x50, local copies, waits for them, and re-layouts: 4.25 us -> 2.71 us
  transfers between devices with their start and end apart: 39 -> 39, of which waited for: 19 -> 18; matrix products, arithmetic and copies ran while one was open for 5% -> 6% of each run, Pallas kernels for 13% -> 14%
where the time goes in v3:
time: 166 us; the launch traced here: 165 us
  starting transfers between devices  71.3 us (43%)
  waiting for transfers between devices  52.3 us (32%)
  Pallas kernels  27.1 us (16%)
  other arithmetic  9.24 us (6%)
  local copies, waits for them, and re-layouts  4.17 us (3%)
    ppermute x26, starting transfers between devices, move_xor(): return lax.ppermute(value, 'seq', [(i, i ^ mask) for i in range(n)])  45.7 us
    ppermute x26, waiting for transfers between devices, move_xor(): return lax.ppermute(value, 'seq', [(i, i ^ mask) for i in range(n)])  37.8 us
    pallas_call x5, Pallas kernels, call(): pl.pallas_call(kernel, out_shape=outs, grid_spec=pltpu.PrefetchScalarGrid...  27.1 us
    ppermute x3, starting transfers between devices, local(): lax.ppermute(sq, 'head', [(i, i ^ k) for i in range(heads)])  16.7 us
    ppermute x6, waiting for transfers between devices, ring(): return lax.ppermute(value, 'seq', pairs)  12.3 us
    ppermute x6, starting transfers between devices, ring(): return lax.ppermute(value, 'seq', pairs)  4.77 us
  transfers between devices with their start and end apart: 39, of which 18 were waited for; matrix products, arithmetic and copies ran while one was open for 6% of the time, Pallas kernels for 14%

profile of v3, /device:TPU:1, one launch (start us, length us, event | category | flops | bytes accessed | tf_op | source)
XLA Modules:
  0.0 165.0 jit_solution(3841209603112320876)
XLA Ops:
  1.5 2.6 %collective-permute-start = (f32[3,8,512]{2,1,0:T(8,128)S(1)}, f32[3,8,512]{2,1,0:T(8,128)S(1)}, u32[]{:S(2)}, u32[]{:S(2)}) collective-permute-start(f32[3,8,512]{2,1,0:T(8,128)S(1)} %get-tuple-element.75), channel_id=1, source_target_pairs={{0,1},{1,0},{2,3},{3,2},{4,5},{5,4},{6,7},{7,6},{8,9},{9,8},{10,11... | collective-permute-start | bytes 147464 | tf_op jit(solution)/shard_map/ppermute | solution.py:26
  8.2 2.0 %collective-permute-done.1.rate_prev = f32[1,512]{1,0:T(1,128)S(1)} collective-permute-done((f32[1,512]{1,0:T(1,128)S(1)}, f32[1,512]{1,0:T(1,128)S(1)}, u32[]{:S(2)}, u32[]{:S(2)}) %collective-permute-start.1) | collective-permute-done | bytes 2080 | tf_op jit(solution)/shard_map/ppermute | solution.py:32
  11.3 4.4 %collective-permute-start.6 = (bf16[3,16,512]{2,1,0:T(8,128)(2,1)S(1)}, bf16[3,16,512]{2,1,0:T(8,128)(2,1)S(1)}, u32[]{:S(2)}, u32[]{:S(2)}) collective-permute-start(bf16[3,16,512]{2,1,0:T(8,128)(2,1)S(1)} %fusion.1), channel_id=1, source_target_pairs={{0,4},{1,5},{2,6},{3,7},{4,0},{5,1},{6,2},{7,3},{8,12},{9,13},{10,... | collective-permute-start | bytes 147464 | tf_op jit(solution)/shard_map/ppermute | solution.py:26
  16.0 2.4 %collective-permute-start.3 = (bf16[2,512,512]{2,1,0:T(8,128)(2,1)S(1)}, bf16[2,512,512]{2,1,0:T(8,128)(2,1)S(1)}, u32[]{:S(2)}, u32[]{:S(2)}) collective-permute-start(bf16[2,512,512]{2,1,0:T(8,128)(2,1)S(1)} %pad_maximum_fusion), channel_id=1, source_target_pairs={{0,1},{1,2},{2,3},{3,4},{4,5},{5,6},{6,7},{7,0},{8,9},{9,10},{10,1... | collective-permute-start | bytes 3145736 | tf_op jit(solution)/shard_map/ppermute | solution.py:32
  18.4 3.0 %collective-permute-done.7 = bf16[3,16,512]{2,1,0:T(8,128)(2,1)S(1)} collective-permute-done((bf16[3,16,512]{2,1,0:T(8,128)(2,1)S(1)}, bf16[3,16,512]{2,1,0:T(8,128)(2,1)S(1)}, u32[]{:S(2)}, u32[]{:S(2)}) %collective-permute-start.7) | collective-permute-done | bytes 49184 | tf_op jit(solution)/shard_map/ppermute | solution.py:26
  22.9 3.5 %collective-permute-done.8 = bf16[4,3,16,512]{3,2,1,0:T(8,128)(2,1)S(1)} collective-permute-done((bf16[4,3,16,512]{3,2,1,0:T(8,128)(2,1)S(1)}, bf16[4,3,16,512]{3,2,1,0:T(8,128)(2,1)S(1)}, u32[]{:S(2)}, u32[]{:S(2)}) %collective-permute-start.8) | collective-permute-done | bytes 196640 | tf_op jit(solution)/shard_map/ppermute | solution.py:26
  27.2 2.5 %collective-permute-start.9 = (bf16[2,4,3,16,512]{4,3,2,1,0:T(8,128)(2,1)}, bf16[2,4,3,16,512]{4,3,2,1,0:T(8,128)(2,1)S(1)}, u32[]{:S(2)}, u32[]{:S(2)}) collective-permute-start(bf16[2,4,3,16,512]{4,3,2,1,0:T(8,128)(2,1)} %pad_maximum_fusion.2.rest_0_), channel_id=1, source_target_pairs={{0,48},{1,49},{2,50},{3,51},{4,52},{5,53},{6,54},{7,55},{8,56},{9,... | collective-permute-start | bytes 1179656 | tf_op jit(solution)/shard_map/ppermute | solution.py:26
  31.0 5.0 %collective-permute-done.9.rest_3_ = bf16[2,4,3,16,512]{4,3,2,1,0:T(8,128)(2,1)S(1)} collective-permute-done((bf16[2,4,3,16,512]{4,3,2,1,0:T(8,128)(2,1)}, bf16[2,4,3,16,512]{4,3,2,1,0:T(8,128)(2,1)S(1)}, u32[]{:S(2)}, u32[]{:S(2)}) %collective-permute-start.9) | collective-permute-done | bytes 393248 | tf_op jit(solution)/shard_map/ppermute | solution.py:26
  38.3 5.8 %collective-permute-done.3.halo = bf16[2,512,512]{2,1,0:T(8,128)(2,1)S(1)} collective-permute-done((bf16[2,512,512]{2,1,0:T(8,128)(2,1)S(1)}, bf16[2,512,512]{2,1,0:T(8,128)(2,1)S(1)}, u32[]{:S(2)}, u32[]{:S(2)}) %collective-permute-start.3) | collective-permute-done | bytes 1048608 | tf_op jit(solution)/shard_map/ppermute | solution.py:32
  45.4 8.2 %shard_map.111 = (f32[4,3,16,512]{3,2,1,0:T(8,128)}, bf16[4,3,16,512]{3,2,1,0:T(8,128)(2,1)}, bf16[4,3,16,512]{3,2,1,0:T(8,128)(2,1)}, bf16[4,3,16,512]{3,2,1,0:...) custom-call(s32[16]{0:T(128)} %stack.168.s_ref, ...), custom_call_target="tpu_custom_call" | custom-call | flops 3221225472 | bytes 4722688 | tf_op jit(solution)/shard_map/pallas_call | solution.py:75
  57.4 2.4 %collective-permute-start.17 = (bf16[4,3,16,512]{3,2,1,0:T(8,128)(2,1)S(1)}, bf16[4,3,16,512]{3,2,1,0:T(8,128)(2,1)S(1)}, u32[]{:S(2)}, u32[]{:S(2)}) collective-permute-start(bf16[4,3,16,512]{3,2,1,0:T(8,128)(2,1)S(1)} %copy-done.22), channel_id=1, source_target_pairs={{0,32},{1,33},{2,34},{3,35},{4,36},{5,37},{6,38},{7,39},{8,40},{9,... | collective-permute-start | bytes 589832 | tf_op jit(solution)/shard_map/ppermute | solution.py:26
  61.3 2.6 %collective-permute-start.19 = (bf16[4,3,16,512]{3,2,1,0:T(8,128)(2,1)S(1)}, bf16[4,3,16,512]{3,2,1,0:T(8,128)(2,1)S(1)}, u32[]{:S(2)}, u32[]{:S(2)}) collective-permute-start(bf16[4,3,16,512]{3,2,1,0:T(8,128)(2,1)S(1)} %copy-done.20), channel_id=1, source_target_pairs={{0,48},{1,49},{2,50},{3,51},{4,52},{5,53},{6,54},{7,55},{8,56},{9,... | collective-permute-start | bytes 589832 | tf_op jit(solution)/shard_map/ppermute | solution.py:26
  67.8 4.4 %collective-permute-done.18 = bf16[4,3,16,512]{3,2,1,0:T(8,128)(2,1)S(1)} collective-permute-done((bf16[4,3,16,512]{3,2,1,0:T(8,128)(2,1)S(1)}, bf16[4,3,16,512]{3,2,1,0:T(8,128)(2,1)S(1)}, u32[]{:S(2)}, u32[]{:S(2)}) %collective-permute-start.18) | collective-permute-done | bytes 196640 | tf_op jit(solution)/shard_map/ppermute | solution.py:26
  72.2 5.4 %collective-permute-done.20 = bf16[4,3,16,512]{3,2,1,0:T(8,128)(2,1)S(1)} collective-permute-done((bf16[4,3,16,512]{3,2,1,0:T(8,128)(2,1)S(1)}, bf16[4,3,16,512]{3,2,1,0:T(8,128)(2,1)S(1)}, u32[]{:S(2)}, u32[]{:S(2)}) %collective-permute-start.20) | collective-permute-done | bytes 196640 | tf_op jit(solution)/shard_map/ppermute | solution.py:26
  78.4 3.4 %collective-permute-start.21 = (bf16[3,16,512]{2,1,0:T(8,128)(2,1)S(1)}, bf16[3,16,512]{2,1,0:T(8,128)(2,1)S(1)}, u32[]{:S(2)}, u32[]{:S(2)}) collective-permute-start(bf16[3,16,512]{2,1,0:T(8,128)(2,1)S(1)} %get-tuple-element.62), channel_id=1, source_target_pairs={{0,2},{1,3},{2,0},{3,1},{4,6},{5,7},{6,4},{7,5},{8,10},{9,11},{10,... | collective-permute-start | bytes 147464 | tf_op jit(solution)/shard_map/ppermute | solution.py:26
  82.5 2.8 %collective-permute-start.23 = (bf16[3,16,512]{2,1,0:T(8,128)(2,1)S(1)}, bf16[3,16,512]{2,1,0:T(8,128)(2,1)S(1)}, u32[]{:S(2)}, u32[]{:S(2)}) collective-permute-start(bf16[3,16,512]{2,1,0:T(8,128)(2,1)S(1)} %get-tuple-element.63), channel_id=1, source_target_pairs={{0,6},{1,7},{2,4},{3,5},{4,2},{5,3},{6,0},{7,1},{8,14},{9,15},{10,... | collective-permute-start | bytes 147464 | tf_op jit(solution)/shard_map/ppermute | solution.py:26
  85.8 3.9 %collective-permute-done.22 = bf16[3,16,512]{2,1,0:T(8,128)(2,1)S(1)} collective-permute-done((bf16[3,16,512]{2,1,0:T(8,128)(2,1)S(1)}, bf16[3,16,512]{2,1,0:T(8,128)(2,1)S(1)}, u32[]{:S(2)}, u32[]{:S(2)}) %collective-permute-start.22) | collective-permute-done | bytes 49184 | tf_op jit(solution)/shard_map/ppermute | solution.py:26
  91.4 2.4 %collective-permute-start.25 = (bf16[3,16,512]{2,1,0:T(8,128)(2,1)S(1)}, bf16[3,16,512]{2,1,0:T(8,128)(2,1)S(1)}, u32[]{:S(2)}, u32[]{:S(2)}) collective-permute-start(bf16[3,16,512]{2,1,0:T(8,128)(2,1)S(1)} %get-tuple-element.60), channel_id=1, source_target_pairs={{0,4},{1,5},{2,6},{3,7},{4,0},{5,1},{6,2},{7,3},{8,12},{9,13},{10,... | collective-permute-start | bytes 147464 | tf_op jit(solution)/shard_map/ppermute | solution.py:26
  93.7 2.3 %collective-permute-start.26 = (bf16[3,16,512]{2,1,0:T(8,128)(2,1)S(1)}, bf16[3,16,512]{2,1,0:T(8,128)(2,1)S(1)}, u32[]{:S(2)}, u32[]{:S(2)}) collective-permute-start(bf16[3,16,512]{2,1,0:T(8,128)(2,1)S(1)} %get-tuple-element.60), channel_id=1, source_target_pairs={{0,6},{1,7},{2,4},{3,5},{4,2},{5,3},{6,0},{7,1},{8,14},{9,15},{10,... | collective-permute-start | bytes 147464 | tf_op jit(solution)/shard_map/ppermute | solution.py:26
  96.0 2.4 %collective-permute-done.25 = bf16[3,16,512]{2,1,0:T(8,128)(2,1)S(1)} collective-permute-done((bf16[3,16,512]{2,1,0:T(8,128)(2,1)S(1)}, bf16[3,16,512]{2,1,0:T(8,128)(2,1)S(1)}, u32[]{:S(2)}, u32[]{:S(2)}) %collective-permute-start.25) | collective-permute-done | bytes 49184 | tf_op jit(solution)/shard_map/ppermute | solution.py:26
  102.9 1.9 %collective-permute-done.28 = bf16[4,3,16,512]{3,2,1,0:T(8,128)(2,1)S(1)} collective-permute-done((bf16[4,3,16,512]{3,2,1,0:T(8,128)(2,1)S(1)}, bf16[4,3,16,512]{3,2,1,0:T(8,128)(2,1)S(1)}, u32[]{:S(2)}, u32[]{:S(2)}) %collective-permute-start.28) | collective-permute-done | bytes 196640 | tf_op jit(solution)/shard_map/ppermute | solution.py:26
  104.9 5.1 %collective-permute-start.29 = (bf16[2,4,3,16,512]{4,3,2,1,0:T(8,128)(2,1)S(1)}, bf16[2,4,3,16,512]{4,3,2,1,0:T(8,128)(2,1)S(1)}, u32[]{:S(2)}, u32[]{:S(2)}) collective-permute-start(bf16[2,4,3,16,512]{4,3,2,1,0:T(8,128)(2,1)S(1)} %pad_maximum_fusion.3.rest_0_), channel_id=1, source_target_pairs={{0,16},{1,17},{2,18},{3,19},{4,20},{5,21},{6,22},{7,23},{8,24},{9,... | collective-permute-start | bytes 1179656 | tf_op jit(solution)/shard_map/ppermute | solution.py:26
  110.0 2.5 %collective-permute-start.31 = (bf16[2,4,3,16,512]{4,3,2,1,0:T(8,128)(2,1)S(1)}, bf16[2,4,3,16,512]{4,3,2,1,0:T(8,128)(2,1)S(1)}, u32[]{:S(2)}, u32[]{:S(2)}) collective-permute-start(bf16[2,4,3,16,512]{4,3,2,1,0:T(8,128)(2,1)S(1)} %pad_maximum_fusion.3.rest_0_), channel_id=1, source_target_pairs={{0,48},{1,49},{2,50},{3,51},{4,52},{5,53},{6,54},{7,55},{8,56},{9,... | collective-permute-start | bytes 1179656 | tf_op jit(solution)/shard_map/ppermute | solution.py:26
  112.4 4.7 %shard_map.112.attn_other = f32[512,512]{1,0:T(8,128)} custom-call(s32[16]{0:T(128)} %stack.168.s_ref, bf16[512,1024]{1,0:T(8,128)(2,1)} %q_ref.3, bf16[512,1024]{1,0:T(8,128)(2,1)} %k_ref.3, bf16[512,1024]{1,0:T(8,128)(2,1)} %v_ref.3, bf16[2,512,512]{2,1,0:T(8,128)(2,1)} %copy-done.6), custom_call_target="tpu_custom_call" | custom-call | flops 805306368 | bytes 4194304 | tf_op jit(solution)/shard_map/pallas_call | solution.py:75
  118.9 3.4 %collective-permute-done.31.rest_3_ = bf16[2,4,3,16,512]{4,3,2,1,0:T(8,128)(2,1)S(1)} collective-permute-done((bf16[2,4,3,16,512]{4,3,2,1,0:T(8,128)(2,1)S(1)}, bf16[2,4,3,16,512]{4,3,2,1,0:T(8,128)(2,1)S(1)}, u32[]{:S(2)}, u32[]{:S(2)}) %collective-permute-start.31) | collective-permute-done | bytes 393248 | tf_op jit(solution)/shard_map/ppermute | solution.py:26
  123.1 5.2 %shard_map.113 = (bf16[512,512]{1,0:T(8,128)(2,1)}, bf16[512,512]{1,0:T(8,128)(2,1)}, f32[2,512]{1,0:T(2,128)}, f32[3,16,512]{2,1,0:T(8,128)}) custom-call(s32[16]{0:T(128)} %stack.168.s_ref, bf16[512,512]{1,0:T(8,128)(2,1)} %copy-done.14, bf16[512,1024]{1,0:T(8,128)(2,1)} %q_ref.3, f32[3,512]{1,0:T(4,128)} %get-tuple-element.37.old_sq, ...), custom_call_target="tpu_custom_call" | custom-call | flops 1610612736 | bytes 3250176 | tf_op jit(solution)/shard_map/pallas_call | solution.py:75
  128.3 13.5 %collective-permute-start.34 = (f32[2,512]{1,0:T(2,128)}, f32[2,512]{1,0:T(2,128)S(1)}, u32[]{:S(2)}, u32[]{:S(2)}) collective-permute-start(f32[2,512]{1,0:T(2,128)} %get-tuple-element.55), channel_id=1, source_target_pairs={{0,64},{64,0},{128,192},{192,128},{1,65},{65,1},{129,193},{193,129... | collective-permute-start | bytes 12296 | tf_op jit(solution)/shard_map/ppermute | solution.py:337
  141.7 2.9 %collective-permute-start.35 = (f32[2,512]{1,0:T(2,128)}, f32[2,512]{1,0:T(2,128)S(1)}, u32[]{:S(2)}, u32[]{:S(2)}) collective-permute-start(f32[2,512]{1,0:T(2,128)} %get-tuple-element.55), channel_id=1, source_target_pairs={{0,128},{64,192},{128,0},{192,64},{1,129},{65,193},{129,1},{193,65... | collective-permute-start | bytes 12296 | tf_op jit(solution)/shard_map/ppermute | solution.py:337
  147.3 2.1 %collective-permute-done.36 = f32[2,512]{1,0:T(2,128)S(1)} collective-permute-done((f32[2,512]{1,0:T(2,128)}, f32[2,512]{1,0:T(2,128)S(1)}, u32[]{:S(2)}, u32[]{:S(2)}) %collective-permute-start.36) | collective-permute-done | bytes 4128 | tf_op jit(solution)/shard_map/ppermute | solution.py:337
  150.5 5.0 %shard_map.114.attn_own = f32[512,512]{1,0:T(8,128)} custom-call(s32[16]{0:T(128)} %stack.168.s_ref, bf16[512,1024]{1,0:T(8,128)(2,1)} %q_ref.3, bf16[512,1024]{1,0:T(8,128)(2,1)} %k_ref.3, bf16[512,1024]{1,0:T(8,128)(2,1)} %v_ref.3, bf16[2,512,512]{2,1,0:T(8,128)(2,1)} %copy-done.2, bf16[2,512,512]{2,1,0:T(8,128)(2,1)} %copy-done.3), custom_call_target="tpu_custom_call" | custom-call | flops 805306368 | bytes 5242880 | tf_op jit(solution)/shard_map/pallas_call | solution.py:75
  155.5 4.1 %collective-permute-done.37 = f32[1,512]{1,0:T(1,128)S(1)} collective-permute-done((f32[1,512]{1,0:T(1,128)S(1)}, f32[1,512]{1,0:T(1,128)S(1)}, u32[]{:S(2)}, u32[]{:S(2)}) %collective-permute-start.37) | collective-permute-done | bytes 2080 | tf_op jit(solution)/shard_map/ppermute | solution.py:32
  161.0 4.0 %shard_map.115 = bf16[512,1024]{1,0:T(8,128)(2,1)} custom-call(s32[16]{0:T(128)} %stack.168.s_ref, bf16[512,512]{1,0:T(8,128)(2,1)} %get-tuple-element.52.f_own, bf16[512,512]{1,0:T(8,128)(2,1)} %copy-done.7, f32[512,512]{1,0:T(8,128)} %shard_map.114.attn_own, f32[512,512]{1,0:T(8,128)} %shard_map.112.attn_other, f32[1,512]{1,0:T(1,128)} %slice_add_fusion.sums, ...), custom_call_target="tpu_custom_call" | custom-call | bytes 3151872 | tf_op jit(solution)/shard_map/pallas_call | solution.py:75
  (125 shorter events, 38.5 us)
Async XLA Ops:
  1.5 6.7 %collective-permute-start = (f32[3,8,512]{2,1,0:T(8,128)S(1)}, f32[3,8,512]{2,1,0:T(8,128)S(1)}, u32[]{:S(2)}, u32[]{:S(2)}) collective-permute-start(f32[3,8,512]{2,1,0:T(8,128)S(1)} %get-tuple-element.75), channel_id=1, source_target_pairs={{0,1},{1,0},{2,3},{3,2},{4,5},{5,4},{6,7},{7,6},{8,9},{9,8},{10,11... | collective-permute-start | bytes 147464 | tf_op jit(solution)/shard_map/ppermute | solution.py:26
  6.6 14.9 %collective-permute-start.5 = (bf16[512,512]{1,0:T(8,128)(2,1)S(1)}, bf16[512,512]{1,0:T(8,128)(2,1)S(1)}, u32[]{:S(2)}, u32[]{:S(2)}) collective-permute-start(bf16[512,512]{1,0:T(8,128)(2,1)S(1)} %get-tuple-element.64), channel_id=1, source_target_pairs={{7,15},{15,23},{23,31},{31,39},{39,47},{47,55},{55,63},{71,79},{79... | collective-permute-start | bytes 1572872 | tf_op jit(solution)/shard_map/ppermute | solution.py:37
  10.2 5.8 %collective-permute-start.2 = (bf16[3,16,512]{2,1,0:T(8,128)(2,1)S(1)}, bf16[3,16,512]{2,1,0:T(8,128)(2,1)S(1)}, u32[]{:S(2)}, u32[]{:S(2)}) collective-permute-start(bf16[3,16,512]{2,1,0:T(8,128)(2,1)S(1)} %fusion.1), channel_id=1, source_target_pairs={{0,2},{1,3},{2,0},{3,1},{4,6},{5,7},{6,4},{7,5},{8,10},{9,11},{10,... | collective-permute-start | bytes 147464 | tf_op jit(solution)/shard_map/ppermute | solution.py:26
  11.3 7.1 %collective-permute-start.6 = (bf16[3,16,512]{2,1,0:T(8,128)(2,1)S(1)}, bf16[3,16,512]{2,1,0:T(8,128)(2,1)S(1)}, u32[]{:S(2)}, u32[]{:S(2)}) collective-permute-start(bf16[3,16,512]{2,1,0:T(8,128)(2,1)S(1)} %fusion.1), channel_id=1, source_target_pairs={{0,4},{1,5},{2,6},{3,7},{4,0},{5,1},{6,2},{7,3},{8,12},{9,13},{10,... | collective-permute-start | bytes 147464 | tf_op jit(solution)/shard_map/ppermute | solution.py:26
  16.0 28.1 %collective-permute-start.3 = (bf16[2,512,512]{2,1,0:T(8,128)(2,1)S(1)}, bf16[2,512,512]{2,1,0:T(8,128)(2,1)S(1)}, u32[]{:S(2)}, u32[]{:S(2)}) collective-permute-start(bf16[2,512,512]{2,1,0:T(8,128)(2,1)S(1)} %pad_maximum_fusion), channel_id=1, source_target_pairs={{0,1},{1,2},{2,3},{3,4},{4,5},{5,6},{6,7},{7,0},{8,9},{9,10},{10,1... | collective-permute-start | bytes 3145736 | tf_op jit(solution)/shard_map/ppermute | solution.py:32
  27.2 8.8 %collective-permute-start.9 = (bf16[2,4,3,16,512]{4,3,2,1,0:T(8,128)(2,1)}, bf16[2,4,3,16,512]{4,3,2,1,0:T(8,128)(2,1)S(1)}, u32[]{:S(2)}, u32[]{:S(2)}) collective-permute-start(bf16[2,4,3,16,512]{4,3,2,1,0:T(8,128)(2,1)} %pad_maximum_fusion.2.rest_0_), channel_id=1, source_target_pairs={{0,48},{1,49},{2,50},{3,51},{4,52},{5,53},{6,54},{7,55},{8,56},{9,... | collective-permute-start | bytes 1179656 | tf_op jit(solution)/shard_map/ppermute | solution.py:26
  29.6 15.2 %collective-permute-start.11 = (bf16[2,4,3,16,512]{4,3,2,1,0:T(8,128)(2,1)}, bf16[2,4,3,16,512]{4,3,2,1,0:T(8,128)(2,1)}, u32[]{:S(2)}, u32[]{:S(2)}) collective-permute-start(bf16[2,4,3,16,512]{4,3,2,1,0:T(8,128)(2,1)} %pad_maximum_fusion.2.rest_0_), channel_id=1, source_target_pairs={{0,16},{1,17},{2,18},{3,19},{4,20},{5,21},{6,22},{7,23},{8,24},{9,... | collective-permute-start | bytes 1179656 | tf_op jit(solution)/shard_map/ppermute | solution.py:26
  29.6 15.8 %collective-permute-start.12 = (bf16[2,4,3,16,512]{4,3,2,1,0:T(8,128)(2,1)}, bf16[2,4,3,16,512]{4,3,2,1,0:T(8,128)(2,1)}, u32[]{:S(2)}, u32[]{:S(2)}) collective-permute-start(bf16[2,4,3,16,512]{4,3,2,1,0:T(8,128)(2,1)} %pad_maximum_fusion.2.rest_0_), channel_id=1, source_target_pairs={{0,32},{1,33},{2,34},{3,35},{4,36},{5,37},{6,38},{7,39},{8,40},{9,... | collective-permute-start | bytes 1179656 | tf_op jit(solution)/shard_map/ppermute | solution.py:26
  36.0 21.4 %collective-permute-start.10 = (bf16[512,512]{1,0:T(8,128)(2,1)}, bf16[512,512]{1,0:T(8,128)(2,1)}, u32[]{:S(2)}, u32[]{:S(2)}) collective-permute-start(bf16[512,512]{1,0:T(8,128)(2,1)} %get-tuple-element.36), channel_id=1, source_target_pairs={{7,15},{15,23},{23,31},{31,39},{39,47},{47,55},{55,63},{71,79},{79... | collective-permute-start | bytes 1572872 | tf_op jit(solution)/shard_map/ppermute | solution.py:37
  44.1 15.7 %collective-permute-start.4 = (bf16[512,512]{1,0:T(8,128)(2,1)}, bf16[512,512]{1,0:T(8,128)(2,1)S(1)}, u32[]{:S(2)}, u32[]{:S(2)}) collective-permute-start(bf16[512,512]{1,0:T(8,128)(2,1)} %slice_select_fusion), channel_id=1, source_target_pairs={{0,1},{1,2},{2,3},{3,4},{4,5},{5,6},{6,7},{7,0},{8,9},{9,10},{10,1... | collective-permute-start | bytes 1572872 | tf_op jit(solution)/shard_map/ppermute | solution.py:32
  53.6 7.7 %collective-permute-start.14 = (bf16[4,3,16,512]{3,2,1,0:T(8,128)(2,1)}, bf16[4,3,16,512]{3,2,1,0:T(8,128)(2,1)S(1)}, u32[]{:S(2)}, u32[]{:S(2)}) collective-permute-start(bf16[4,3,16,512]{3,2,1,0:T(8,128)(2,1)} %get-tuple-element.42), channel_id=1, source_target_pairs={{0,8},{1,9},{2,10},{3,11},{4,12},{5,13},{6,14},{7,15},{8,0},{9,1},... | collective-permute-start | bytes 589832 | tf_op jit(solution)/shard_map/ppermute | solution.py:26
  55.0 9.0 %collective-permute-start.15 = (bf16[4,3,16,512]{3,2,1,0:T(8,128)(2,1)}, bf16[4,3,16,512]{3,2,1,0:T(8,128)(2,1)S(1)}, u32[]{:S(2)}, u32[]{:S(2)}) collective-permute-start(bf16[4,3,16,512]{3,2,1,0:T(8,128)(2,1)} %get-tuple-element.43), channel_id=1, source_target_pairs={{0,16},{1,17},{2,18},{3,19},{4,20},{5,21},{6,22},{7,23},{8,24},{9,... | collective-permute-start | bytes 589832 | tf_op jit(solution)/shard_map/ppermute | solution.py:26
  56.8 8.5 %collective-permute-start.16 = (bf16[4,3,16,512]{3,2,1,0:T(8,128)(2,1)S(1)}, bf16[4,3,16,512]{3,2,1,0:T(8,128)(2,1)S(1)}, u32[]{:S(2)}, u32[]{:S(2)}) collective-permute-start(bf16[4,3,16,512]{3,2,1,0:T(8,128)(2,1)S(1)} %copy-done.23), channel_id=1, source_target_pairs={{0,24},{1,25},{2,26},{3,27},{4,28},{5,29},{6,30},{7,31},{8,16},{9,... | collective-permute-start | bytes 589832 | tf_op jit(solution)/shard_map/ppermute | solution.py:26
  57.4 10.5 %collective-permute-start.17 = (bf16[4,3,16,512]{3,2,1,0:T(8,128)(2,1)S(1)}, bf16[4,3,16,512]{3,2,1,0:T(8,128)(2,1)S(1)}, u32[]{:S(2)}, u32[]{:S(2)}) collective-permute-start(bf16[4,3,16,512]{3,2,1,0:T(8,128)(2,1)S(1)} %copy-done.22), channel_id=1, source_target_pairs={{0,32},{1,33},{2,34},{3,35},{4,36},{5,37},{6,38},{7,39},{8,40},{9,... | collective-permute-start | bytes 589832 | tf_op jit(solution)/shard_map/ppermute | solution.py:26
  59.8 12.4 %collective-permute-start.18 = (bf16[4,3,16,512]{3,2,1,0:T(8,128)(2,1)S(1)}, bf16[4,3,16,512]{3,2,1,0:T(8,128)(2,1)S(1)}, u32[]{:S(2)}, u32[]{:S(2)}) collective-permute-start(bf16[4,3,16,512]{3,2,1,0:T(8,128)(2,1)S(1)} %copy-done.21), channel_id=1, source_target_pairs={{0,40},{1,41},{2,42},{3,43},{4,44},{5,45},{6,46},{7,47},{8,32},{9,... | collective-permute-start | bytes 589832 | tf_op jit(solution)/shard_map/ppermute | solution.py:26
  61.3 10.9 %collective-permute-start.19 = (bf16[4,3,16,512]{3,2,1,0:T(8,128)(2,1)S(1)}, bf16[4,3,16,512]{3,2,1,0:T(8,128)(2,1)S(1)}, u32[]{:S(2)}, u32[]{:S(2)}) collective-permute-start(bf16[4,3,16,512]{3,2,1,0:T(8,128)(2,1)S(1)} %copy-done.20), channel_id=1, source_target_pairs={{0,48},{1,49},{2,50},{3,51},{4,52},{5,53},{6,54},{7,55},{8,56},{9,... | collective-permute-start | bytes 589832 | tf_op jit(solution)/shard_map/ppermute | solution.py:26
  64.0 13.6 %collective-permute-start.20 = (bf16[4,3,16,512]{3,2,1,0:T(8,128)(2,1)S(1)}, bf16[4,3,16,512]{3,2,1,0:T(8,128)(2,1)S(1)}, u32[]{:S(2)}, u32[]{:S(2)}) collective-permute-start(bf16[4,3,16,512]{3,2,1,0:T(8,128)(2,1)S(1)} %copy-done.19), channel_id=1, source_target_pairs={{0,56},{1,57},{2,58},{3,59},{4,60},{5,61},{6,62},{7,63},{8,48},{9,... | collective-permute-start | bytes 589832 | tf_op jit(solution)/shard_map/ppermute | solution.py:26
  65.3 20.4 %collective-permute-start.13 = (bf16[2,512,512]{2,1,0:T(8,128)(2,1)S(1)}, bf16[2,512,512]{2,1,0:T(8,128)(2,1)S(1)}, u32[]{:S(2)}, u32[]{:S(2)}) collective-permute-start(bf16[2,512,512]{2,1,0:T(8,128)(2,1)S(1)} %maximum_select_fusion), channel_id=1, source_target_pairs={{0,1},{1,2},{2,3},{3,4},{4,5},{5,6},{6,7},{7,0},{8,9},{9,10},{10,1... | collective-permute-start | bytes 3145736 | tf_op jit(solution)/shard_map/ppermute | solution.py:32
  77.7 22.5 %collective-permute-start.27 = (bf16[2,512,512]{2,1,0:T(8,128)(2,1)S(1)}, bf16[2,512,512]{2,1,0:T(8,128)(2,1)S(1)}, u32[]{:S(2)}, u32[]{:S(2)}) collective-permute-start(bf16[2,512,512]{2,1,0:T(8,128)(2,1)S(1)} %copy-done.5), channel_id=1, source_target_pairs={{7,15},{15,23},{23,31},{31,39},{39,47},{47,55},{55,63},{71,79},{79... | collective-permute-start | bytes 3145736 | tf_op jit(solution)/shard_map/ppermute | solution.py:37
  78.4 6.9 %collective-permute-start.21 = (bf16[3,16,512]{2,1,0:T(8,128)(2,1)S(1)}, bf16[3,16,512]{2,1,0:T(8,128)(2,1)S(1)}, u32[]{:S(2)}, u32[]{:S(2)}) collective-permute-start(bf16[3,16,512]{2,1,0:T(8,128)(2,1)S(1)} %get-tuple-element.62), channel_id=1, source_target_pairs={{0,2},{1,3},{2,0},{3,1},{4,6},{5,7},{6,4},{7,5},{8,10},{9,11},{10,... | collective-permute-start | bytes 147464 | tf_op jit(solution)/shard_map/ppermute | solution.py:26
  81.9 7.7 %collective-permute-start.22 = (bf16[3,16,512]{2,1,0:T(8,128)(2,1)S(1)}, bf16[3,16,512]{2,1,0:T(8,128)(2,1)S(1)}, u32[]{:S(2)}, u32[]{:S(2)}) collective-permute-start(bf16[3,16,512]{2,1,0:T(8,128)(2,1)S(1)} %fusion.3), channel_id=1, source_target_pairs={{0,4},{1,5},{2,6},{3,7},{4,0},{5,1},{6,2},{7,3},{8,12},{9,13},{10,... | collective-permute-start | bytes 147464 | tf_op jit(solution)/shard_map/ppermute | solution.py:26
  82.5 7.1 %collective-permute-start.23 = (bf16[3,16,512]{2,1,0:T(8,128)(2,1)S(1)}, bf16[3,16,512]{2,1,0:T(8,128)(2,1)S(1)}, u32[]{:S(2)}, u32[]{:S(2)}) collective-permute-start(bf16[3,16,512]{2,1,0:T(8,128)(2,1)S(1)} %get-tuple-element.63), channel_id=1, source_target_pairs={{0,6},{1,7},{2,4},{3,5},{4,2},{5,3},{6,0},{7,1},{8,14},{9,15},{10,... | collective-permute-start | bytes 147464 | tf_op jit(solution)/shard_map/ppermute | solution.py:26
  91.4 7.1 %collective-permute-start.25 = (bf16[3,16,512]{2,1,0:T(8,128)(2,1)S(1)}, bf16[3,16,512]{2,1,0:T(8,128)(2,1)S(1)}, u32[]{:S(2)}, u32[]{:S(2)}) collective-permute-start(bf16[3,16,512]{2,1,0:T(8,128)(2,1)S(1)} %get-tuple-element.60), channel_id=1, source_target_pairs={{0,4},{1,5},{2,6},{3,7},{4,0},{5,1},{6,2},{7,3},{8,12},{9,13},{10,... | collective-permute-start | bytes 147464 | tf_op jit(solution)/shard_map/ppermute | solution.py:26
  93.7 6.5 %collective-permute-start.26 = (bf16[3,16,512]{2,1,0:T(8,128)(2,1)S(1)}, bf16[3,16,512]{2,1,0:T(8,128)(2,1)S(1)}, u32[]{:S(2)}, u32[]{:S(2)}) collective-permute-start(bf16[3,16,512]{2,1,0:T(8,128)(2,1)S(1)} %get-tuple-element.60), channel_id=1, source_target_pairs={{0,6},{1,7},{2,4},{3,5},{4,2},{5,3},{6,0},{7,1},{8,14},{9,15},{10,... | collective-permute-start | bytes 147464 | tf_op jit(solution)/shard_map/ppermute | solution.py:26
  101.6 47.9 %collective-permute-start.33 = (bf16[2,512,512]{2,1,0:T(8,128)(2,1)S(1)}, bf16[2,512,512]{2,1,0:T(8,128)(2,1)S(1)}, u32[]{:S(2)}, u32[]{:S(2)}) collective-permute-start(bf16[2,512,512]{2,1,0:T(8,128)(2,1)S(1)} %collective-permute-done.27), channel_id=1, source_target_pairs={{7,0},{15,8},{23,16},{31,24},{39,32},{47,40},{55,48},{63,56},{71,6... | collective-permute-start | bytes 3145736 | tf_op jit(solution)/shard_map/ppermute | solution.py:42
  104.9 12.3 %collective-permute-start.29 = (bf16[2,4,3,16,512]{4,3,2,1,0:T(8,128)(2,1)S(1)}, bf16[2,4,3,16,512]{4,3,2,1,0:T(8,128)(2,1)S(1)}, u32[]{:S(2)}, u32[]{:S(2)}) collective-permute-start(bf16[2,4,3,16,512]{4,3,2,1,0:T(8,128)(2,1)S(1)} %pad_maximum_fusion.3.rest_0_), channel_id=1, source_target_pairs={{0,16},{1,17},{2,18},{3,19},{4,20},{5,21},{6,22},{7,23},{8,24},{9,... | collective-permute-start | bytes 1179656 | tf_op jit(solution)/shard_map/ppermute | solution.py:26
  110.0 9.0 %collective-permute-start.30 = (bf16[2,4,3,16,512]{4,3,2,1,0:T(8,128)(2,1)S(1)}, bf16[2,4,3,16,512]{4,3,2,1,0:T(8,128)(2,1)S(1)}, u32[]{:S(2)}, u32[]{:S(2)}) collective-permute-start(bf16[2,4,3,16,512]{4,3,2,1,0:T(8,128)(2,1)S(1)} %pad_maximum_fusion.3.rest_0_), channel_id=1, source_target_pairs={{0,32},{1,33},{2,34},{3,35},{4,36},{5,37},{6,38},{7,39},{8,40},{9,... | collective-permute-start | bytes 1179656 | tf_op jit(solution)/shard_map/ppermute | solution.py:26
  110.0 12.3 %collective-permute-start.31 = (bf16[2,4,3,16,512]{4,3,2,1,0:T(8,128)(2,1)S(1)}, bf16[2,4,3,16,512]{4,3,2,1,0:T(8,128)(2,1)S(1)}, u32[]{:S(2)}, u32[]{:S(2)}) collective-permute-start(bf16[2,4,3,16,512]{4,3,2,1,0:T(8,128)(2,1)S(1)} %pad_maximum_fusion.3.rest_0_), channel_id=1, source_target_pairs={{0,48},{1,49},{2,50},{3,51},{4,52},{5,53},{6,54},{7,55},{8,56},{9,... | collective-permute-start | bytes 1179656 | tf_op jit(solution)/shard_map/ppermute | solution.py:26
  128.3 17.7 %collective-permute-start.34 = (f32[2,512]{1,0:T(2,128)}, f32[2,512]{1,0:T(2,128)S(1)}, u32[]{:S(2)}, u32[]{:S(2)}) collective-permute-start(f32[2,512]{1,0:T(2,128)} %get-tuple-element.55), channel_id=1, source_target_pairs={{0,64},{64,0},{128,192},{192,128},{1,65},{65,1},{129,193},{193,129... | collective-permute-start | bytes 12296 | tf_op jit(solution)/shard_map/ppermute | solution.py:337
  144.9 15.3 %collective-permute-start.32 = (bf16[512,512]{1,0:T(8,128)(2,1)}, bf16[512,512]{1,0:T(8,128)(2,1)S(1)}, u32[]{:S(2)}, u32[]{:S(2)}) collective-permute-start(bf16[512,512]{1,0:T(8,128)(2,1)} %get-tuple-element.53), channel_id=1, source_target_pairs={{0,7},{1,0},{2,1},{3,2},{4,3},{5,4},{6,5},{7,6},{8,15},{9,8},{10,9... | collective-permute-start | bytes 1572872 | tf_op jit(solution)/shard_map/ppermute | solution.py:32
  145.9 14.2 %collective-permute-start.38 = (f32[3,8,512]{2,1,0:T(8,128)S(1)}, f32[3,8,512]{2,1,0:T(8,128)S(1)}, u32[]{:S(2)}, u32[]{:S(2)}) collective-permute-start(f32[3,8,512]{2,1,0:T(8,128)S(1)} %get-tuple-element.74), channel_id=1, source_target_pairs={{0,1},{1,0},{2,3},{3,2},{4,5},{5,4},{6,7},{7,6},{8,9},{9,8},{10,11... | collective-permute-start | bytes 147464 | tf_op jit(solution)/shard_map/ppermute | solution.py:26
  149.4 10.1 %collective-permute-start.37 = (f32[1,512]{1,0:T(1,128)S(1)}, f32[1,512]{1,0:T(1,128)S(1)}, u32[]{:S(2)}, u32[]{:S(2)}) collective-permute-start(f32[1,512]{1,0:T(1,128)S(1)} %slice.239), channel_id=1, source_target_pairs={{0,7},{1,0},{2,1},{3,2},{4,3},{5,4},{6,5},{7,6},{8,15},{9,8},{10,9... | collective-permute-start | bytes 6152 | tf_op jit(solution)/shard_map/ppermute | solution.py:32
  (32 other events, 226.5 us)

commit v4 on v3

--- a/solution.py
+++ b/solution.py
@@ -270,7 +270,7 @@
     w_parts = gather_zq(after(w_pair.astype(BF16), rate_prev))
     w_block = after(jnp.stack(w_parts), plane_k)
     w_blocks = gather_xy(w_block)
-    halo = ring(after(send_other, w_parts[1]), 1)
+    halo = ring(after(send_other, w_block), 1)
     last = (seq_pos & (RING - 1)) == RING - 1
     plane_v = to_next_plane(after(values[:, HD:], w_blocks[-1]))
     q_prev = ring(after(head_of(queries, False), halo), 1)
@@ -307,8 +307,7 @@
     for k in range(ZQ):
         total = grad_out[0][k] + sum(part[k].astype(F32) for part in arrived)
         chunks.append(total if k == 0 else total.astype(BF16))
-    parts = [move_xor(chunks[k], k << 1) for k in range(1, ZQ)]
-    parts[0] = after(parts[0], halo_other)
+    parts = [move_xor(after(chunks[k], halo_other), k << 1) for k in range(1, ZQ)]
     upd = w_pair + chunks[0] + sum(part.astype(F32) for part in parts)
     upd_b = upd.astype(BF16)
     plane_other = to_next_plane(after(send_other, chunks[1]))
@@ -345,12 +344,14 @@
         jnp.stack([new_theirs, new_mine], axis=1),
     )
     gain = out_gain.reshape(1, 2 * HD)
-    mixed = call(
-        mix_kernel,
-        scalars,
-        [f_own, f_back, attn_own, attn_other, sums, gain],
-        [whole((BLK, HD))] * 4 + [whole((1, BLK)), whole((1, 2 * HD))],
-        shape((BLK, 2 * HD), BF16),
+    inv = lax.rsqrt(sums[0] / (HEADS * HD) + EPS)[:, None]
+    gains = jnp.where(even, gain, jnp.roll(gain, HD, axis=1))
+    mixed_own = (attn_own + f_own.astype(F32) * inv * gains[:, :HD]).astype(BF16)
+    mixed_other = (attn_other + f_back.astype(F32) * inv * gains[:, HD:]).astype(BF16)
+    mixed = jnp.where(
+        even,
+        jnp.concatenate([mixed_own, mixed_other], axis=1),
+        jnp.concatenate([mixed_other, mixed_own], axis=1),
     )
     return mixed, new_all[0], new_all[1], new_all[2]
 

time: 166 us -> 162 us (0.976)
  Pallas kernels: 27.1 us -> 23.4 us
  other arithmetic: 9.24 us -> 11.8 us
  starting transfers between devices: 71.3 us -> 69.1 us
    ppermute x6, starting transfers between devices: 4.77 us -> 10.2 us  [ring(): return lax.ppermute(value, 'seq', pairs)]
    ppermute x26, waiting for transfers between devices: 37.8 us -> 42.7 us  [move_xor(): return lax.ppermute(value, 'seq', [(i, i ^ mask) for i in range(n)])]
    pallas_call x5 -> x4, Pallas kernels: 27.1 us -> 23.4 us  [call(): pl.pallas_call(kernel, out_shape=outs, grid_spec=pltpu.PrefetchScalarGrid...]
    ppermute x3, starting transfers between devices: 16.7 us -> 13 us  [local(): lax.ppermute(sq, 'head', [(i, i ^ k) for i in range(heads)])]
    ppermute x26, starting transfers between devices: 45.7 us -> 42.5 us  [move_xor(): return lax.ppermute(value, 'seq', [(i, i ^ mask) for i in range(n)])]
    ppermute x6, waiting for transfers between devices: 12.3 us -> 9.86 us  [ring(): return lax.ppermute(value, 'seq', pairs)]
    ppermute x3, waiting for transfers between devices: 2.08 us -> 0.01 us  [local(): lax.ppermute(sq, 'head', [(i, i ^ k) for i in range(heads)])]
  transfers between devices with their start and end apart: 39 -> 39, of which waited for: 18 -> 18; matrix products, arithmetic and copies ran while one was open for 6% -> 5% of each run, Pallas kernels for 14% -> 14%
where the time goes in v4:
time: 162 us
  starting transfers between devices  69.1 us (43%)
  waiting for transfers between devices  52.6 us (32%)
  Pallas kernels  23.4 us (14%)
  other arithmetic  11.8 us (7%)
  local copies, waits for them, and re-layouts  3.81 us (2%)
    ppermute x26, waiting for transfers between devices, move_xor(): return lax.ppermute(value, 'seq', [(i, i ^ mask) for i in range(n)])  42.7 us
    ppermute x26, starting transfers between devices, move_xor(): return lax.ppermute(value, 'seq', [(i, i ^ mask) for i in range(n)])  42.5 us
    pallas_call x4, Pallas kernels, call(): pl.pallas_call(kernel, out_shape=outs, grid_spec=pltpu.PrefetchScalarGrid...  23.4 us
    ppermute x3, starting transfers between devices, local(): lax.ppermute(sq, 'head', [(i, i ^ k) for i in range(heads)])  13 us
    ppermute x6, starting transfers between devices, ring(): return lax.ppermute(value, 'seq', pairs)  10.2 us
    ppermute x6, waiting for transfers between devices, ring(): return lax.ppermute(value, 'seq', pairs)  9.86 us
  transfers between devices with their start and end apart: 39, of which 18 were waited for; matrix products, arithmetic and copies ran while one was open for 5% of the time, Pallas kernels for 14%

profile of v4, /device:TPU:1, one launch (start us, length us, event | category | flops | bytes accessed | tf_op | source)
XLA Modules:
  0.0 161.8 jit_solution(16610556282904079681)
XLA Ops:
  1.5 2.6 %collective-permute-start = (f32[3,8,512]{2,1,0:T(8,128)S(1)}, f32[3,8,512]{2,1,0:T(8,128)S(1)}, u32[]{:S(2)}, u32[]{:S(2)}) collective-permute-start(f32[3,8,512]{2,1,0:T(8,128)S(1)} %get-tuple-element.79), channel_id=1, source_target_pairs={{0,1},{1,0},{2,3},{3,2},{4,5},{5,4},{6,7},{7,6},{8,9},{9,8},{10,11... | collective-permute-start | bytes 147464 | tf_op jit(solution)/shard_map/ppermute | solution.py:26
  8.4 2.6 %collective-permute-done.1.rate_prev = f32[1,512]{1,0:T(1,128)S(1)} collective-permute-done((f32[1,512]{1,0:T(1,128)S(1)}, f32[1,512]{1,0:T(1,128)S(1)}, u32[]{:S(2)}, u32[]{:S(2)}) %collective-permute-start.1) | collective-permute-done | bytes 2080 | tf_op jit(solution)/shard_map/ppermute | solution.py:32
  11.5 4.9 %collective-permute-start.3 = (bf16[3,16,512]{2,1,0:T(8,128)(2,1)S(1)}, bf16[3,16,512]{2,1,0:T(8,128)(2,1)S(1)}, u32[]{:S(2)}, u32[]{:S(2)}) collective-permute-start(bf16[3,16,512]{2,1,0:T(8,128)(2,1)S(1)} %fusion.1), channel_id=1, source_target_pairs={{0,4},{1,5},{2,6},{3,7},{4,0},{5,1},{6,2},{7,3},{8,12},{9,13},{10,... | collective-permute-start | bytes 147464 | tf_op jit(solution)/shard_map/ppermute | solution.py:26
  18.5 3.5 %collective-permute-done.4 = bf16[3,16,512]{2,1,0:T(8,128)(2,1)S(1)} collective-permute-done((bf16[3,16,512]{2,1,0:T(8,128)(2,1)S(1)}, bf16[3,16,512]{2,1,0:T(8,128)(2,1)S(1)}, u32[]{:S(2)}, u32[]{:S(2)}) %collective-permute-start.4) | collective-permute-done | bytes 49184 | tf_op jit(solution)/shard_map/ppermute | solution.py:26
  22.1 2.3 %collective-permute-start.6 = (bf16[2,512,512]{2,1,0:T(8,128)(2,1)S(1)}, bf16[2,512,512]{2,1,0:T(8,128)(2,1)S(1)}, u32[]{:S(2)}, u32[]{:S(2)}) collective-permute-start(bf16[2,512,512]{2,1,0:T(8,128)(2,1)S(1)} %pad_maximum_fusion), channel_id=1, source_target_pairs={{0,1},{1,2},{2,3},{3,4},{4,5},{5,6},{6,7},{7,0},{8,9},{9,10},{10,1... | collective-permute-start | bytes 3145736 | tf_op jit(solution)/shard_map/ppermute | solution.py:32
  25.5 3.7 %collective-permute-done.7 = bf16[4,3,16,512]{3,2,1,0:T(8,128)(2,1)S(1)} collective-permute-done((bf16[4,3,16,512]{3,2,1,0:T(8,128)(2,1)S(1)}, bf16[4,3,16,512]{3,2,1,0:T(8,128)(2,1)S(1)}, u32[]{:S(2)}, u32[]{:S(2)}) %collective-permute-start.7) | collective-permute-done | bytes 196640 | tf_op jit(solution)/shard_map/ppermute | solution.py:26
  30.0 2.2 %collective-permute-start.10 = (bf16[2,4,3,16,512]{4,3,2,1,0:T(8,128)(2,1)}, bf16[2,4,3,16,512]{4,3,2,1,0:T(8,128)(2,1)S(1)}, u32[]{:S(2)}, u32[]{:S(2)}) collective-permute-start(bf16[2,4,3,16,512]{4,3,2,1,0:T(8,128)(2,1)} %pad_maximum_fusion.2.rest_0_), channel_id=1, source_target_pairs={{0,48},{1,49},{2,50},{3,51},{4,52},{5,53},{6,54},{7,55},{8,56},{9,... | collective-permute-start | bytes 1179656 | tf_op jit(solution)/shard_map/ppermute | solution.py:26
  34.8 3.6 %collective-permute-done.10.rest_3_ = bf16[2,4,3,16,512]{4,3,2,1,0:T(8,128)(2,1)S(1)} collective-permute-done((bf16[2,4,3,16,512]{4,3,2,1,0:T(8,128)(2,1)}, bf16[2,4,3,16,512]{4,3,2,1,0:T(8,128)(2,1)S(1)}, u32[]{:S(2)}, u32[]{:S(2)}) %collective-permute-start.10) | collective-permute-done | bytes 393248 | tf_op jit(solution)/shard_map/ppermute | solution.py:26
  39.1 6.6 %collective-permute-done.6.halo = bf16[2,512,512]{2,1,0:T(8,128)(2,1)S(1)} collective-permute-done((bf16[2,512,512]{2,1,0:T(8,128)(2,1)S(1)}, bf16[2,512,512]{2,1,0:T(8,128)(2,1)S(1)}, u32[]{:S(2)}, u32[]{:S(2)}) %collective-permute-start.6) | collective-permute-done | bytes 1048608 | tf_op jit(solution)/shard_map/ppermute | solution.py:32
  47.4 8.3 %shard_map.111 = (f32[4,3,16,512]{3,2,1,0:T(8,128)}, bf16[4,3,16,512]{3,2,1,0:T(8,128)(2,1)}, bf16[4,3,16,512]{3,2,1,0:T(8,128)(2,1)}, bf16[4,3,16,512]{3,2,1,0:...) custom-call(s32[16]{0:T(128)} %stack.168.s_ref, ...), custom_call_target="tpu_custom_call" | custom-call | flops 3221225472 | bytes 4722688 | tf_op jit(solution)/shard_map/pallas_call | solution.py:75
  55.8 2.4 %collective-permute-start.11 = (bf16[4,3,16,512]{3,2,1,0:T(8,128)(2,1)}, bf16[4,3,16,512]{3,2,1,0:T(8,128)(2,1)S(1)}, u32[]{:S(2)}, u32[]{:S(2)}) collective-permute-start(bf16[4,3,16,512]{3,2,1,0:T(8,128)(2,1)} %get-tuple-element.38), channel_id=1, source_target_pairs={{0,8},{1,9},{2,10},{3,11},{4,12},{5,13},{6,14},{7,15},{8,0},{9,1},... | collective-permute-start | bytes 589832 | tf_op jit(solution)/shard_map/ppermute | solution.py:26
  61.1 3.3 %collective-permute-start.14 = (bf16[4,3,16,512]{3,2,1,0:T(8,128)(2,1)S(1)}, bf16[4,3,16,512]{3,2,1,0:T(8,128)(2,1)S(1)}, u32[]{:S(2)}, u32[]{:S(2)}) collective-permute-start(bf16[4,3,16,512]{3,2,1,0:T(8,128)(2,1)S(1)} %copy-done.21), channel_id=1, source_target_pairs={{0,32},{1,33},{2,34},{3,35},{4,36},{5,37},{6,38},{7,39},{8,40},{9,... | collective-permute-start | bytes 589832 | tf_op jit(solution)/shard_map/ppermute | solution.py:26
  67.5 1.8 %collective-permute-start.17 = (bf16[4,3,16,512]{3,2,1,0:T(8,128)(2,1)S(1)}, bf16[4,3,16,512]{3,2,1,0:T(8,128)(2,1)S(1)}, u32[]{:S(2)}, u32[]{:S(2)}) collective-permute-start(bf16[4,3,16,512]{3,2,1,0:T(8,128)(2,1)S(1)} %copy-done.18), channel_id=1, source_target_pairs={{0,56},{1,57},{2,58},{3,59},{4,60},{5,61},{6,62},{7,63},{8,48},{9,... | collective-permute-start | bytes 589832 | tf_op jit(solution)/shard_map/ppermute | solution.py:26
  69.2 2.6 %collective-permute-done.14 = bf16[4,3,16,512]{3,2,1,0:T(8,128)(2,1)S(1)} collective-permute-done((bf16[4,3,16,512]{3,2,1,0:T(8,128)(2,1)S(1)}, bf16[4,3,16,512]{3,2,1,0:T(8,128)(2,1)S(1)}, u32[]{:S(2)}, u32[]{:S(2)}) %collective-permute-start.14) | collective-permute-done | bytes 196640 | tf_op jit(solution)/shard_map/ppermute | solution.py:26
  71.8 5.2 %collective-permute-done.15 = bf16[4,3,16,512]{3,2,1,0:T(8,128)(2,1)S(1)} collective-permute-done((bf16[4,3,16,512]{3,2,1,0:T(8,128)(2,1)S(1)}, bf16[4,3,16,512]{3,2,1,0:T(8,128)(2,1)S(1)}, u32[]{:S(2)}, u32[]{:S(2)}) %collective-permute-start.15) | collective-permute-done | bytes 196640 | tf_op jit(solution)/shard_map/ppermute | solution.py:26
  77.0 6.0 %collective-permute-done.17 = bf16[4,3,16,512]{3,2,1,0:T(8,128)(2,1)S(1)} collective-permute-done((bf16[4,3,16,512]{3,2,1,0:T(8,128)(2,1)S(1)}, bf16[4,3,16,512]{3,2,1,0:T(8,128)(2,1)S(1)}, u32[]{:S(2)}, u32[]{:S(2)}) %collective-permute-start.17) | collective-permute-done | bytes 196640 | tf_op jit(solution)/shard_map/ppermute | solution.py:26
  84.1 3.1 %collective-permute-start.23 = (bf16[3,16,512]{2,1,0:T(8,128)(2,1)S(1)}, bf16[3,16,512]{2,1,0:T(8,128)(2,1)S(1)}, u32[]{:S(2)}, u32[]{:S(2)}) collective-permute-start(bf16[3,16,512]{2,1,0:T(8,128)(2,1)S(1)} %fusion.3), channel_id=1, source_target_pairs={{0,4},{1,5},{2,6},{3,7},{4,0},{5,1},{6,2},{7,3},{8,12},{9,13},{10,... | collective-permute-start | bytes 147464 | tf_op jit(solution)/shard_map/ppermute | solution.py:26
  87.2 2.6 %collective-permute-start.24 = (bf16[3,16,512]{2,1,0:T(8,128)(2,1)S(1)}, bf16[3,16,512]{2,1,0:T(8,128)(2,1)S(1)}, u32[]{:S(2)}, u32[]{:S(2)}) collective-permute-start(bf16[3,16,512]{2,1,0:T(8,128)(2,1)S(1)} %get-tuple-element.53), channel_id=1, source_target_pairs={{0,6},{1,7},{2,4},{3,5},{4,2},{5,3},{6,0},{7,1},{8,14},{9,15},{10,... | collective-permute-start | bytes 147464 | tf_op jit(solution)/shard_map/ppermute | solution.py:26
  93.4 1.9 %collective-permute-start.25 = (bf16[3,16,512]{2,1,0:T(8,128)(2,1)S(1)}, bf16[3,16,512]{2,1,0:T(8,128)(2,1)S(1)}, u32[]{:S(2)}, u32[]{:S(2)}) collective-permute-start(bf16[3,16,512]{2,1,0:T(8,128)(2,1)S(1)} %get-tuple-element.64), channel_id=1, source_target_pairs={{0,2},{1,3},{2,0},{3,1},{4,6},{5,7},{6,4},{7,5},{8,10},{9,11},{10,... | collective-permute-start | bytes 147464 | tf_op jit(solution)/shard_map/ppermute | solution.py:26
  95.3 2.4 %collective-permute-start.26 = (bf16[3,16,512]{2,1,0:T(8,128)(2,1)S(1)}, bf16[3,16,512]{2,1,0:T(8,128)(2,1)S(1)}, u32[]{:S(2)}, u32[]{:S(2)}) collective-permute-start(bf16[3,16,512]{2,1,0:T(8,128)(2,1)S(1)} %get-tuple-element.64), channel_id=1, source_target_pairs={{0,4},{1,5},{2,6},{3,7},{4,0},{5,1},{6,2},{7,3},{8,12},{9,13},{10,... | collective-permute-start | bytes 147464 | tf_op jit(solution)/shard_map/ppermute | solution.py:26
  99.0 3.1 %collective-permute-done.26 = bf16[3,16,512]{2,1,0:T(8,128)(2,1)S(1)} collective-permute-done((bf16[3,16,512]{2,1,0:T(8,128)(2,1)S(1)}, bf16[3,16,512]{2,1,0:T(8,128)(2,1)S(1)}, u32[]{:S(2)}, u32[]{:S(2)}) %collective-permute-start.26) | collective-permute-done | bytes 49184 | tf_op jit(solution)/shard_map/ppermute | solution.py:26
  105.5 2.2 %collective-permute-done.29 = bf16[4,3,16,512]{3,2,1,0:T(8,128)(2,1)S(1)} collective-permute-done((bf16[4,3,16,512]{3,2,1,0:T(8,128)(2,1)S(1)}, bf16[4,3,16,512]{3,2,1,0:T(8,128)(2,1)S(1)}, u32[]{:S(2)}, u32[]{:S(2)}) %collective-permute-start.29) | collective-permute-done | bytes 196640 | tf_op jit(solution)/shard_map/ppermute | solution.py:26
  108.6 2.9 %collective-permute-start.31 = (bf16[2,4,3,16,512]{4,3,2,1,0:T(8,128)(2,1)S(1)}, bf16[2,4,3,16,512]{4,3,2,1,0:T(8,128)(2,1)S(1)}, u32[]{:S(2)}, u32[]{:S(2)}) collective-permute-start(bf16[2,4,3,16,512]{4,3,2,1,0:T(8,128)(2,1)S(1)} %pad_maximum_fusion.3.rest_0_), channel_id=1, source_target_pairs={{0,32},{1,33},{2,34},{3,35},{4,36},{5,37},{6,38},{7,39},{8,40},{9,... | collective-permute-start | bytes 1179656 | tf_op jit(solution)/shard_map/ppermute | solution.py:26
  111.7 4.7 %shard_map.112 = f32[512,512]{1,0:T(8,128)} custom-call(s32[16]{0:T(128)} %stack.168.s_ref, bf16[512,1024]{1,0:T(8,128)(2,1)} %q_ref.3, bf16[512,1024]{1,0:T(8,128)(2,1)} %k_ref.3, bf16[512,1024]{1,0:T(8,128)(2,1)} %v_ref.3, bf16[2,512,512]{2,1,0:T(8,128)(2,1)} %copy-done.7), custom_call_target="tpu_custom_call" | custom-call | flops 805306368 | bytes 4194304 | tf_op jit(solution)/shard_map/pallas_call | solution.py:75
  116.4 4.6 %collective-permute-done.31.rest_2_ = bf16[2,4,3,16,512]{4,3,2,1,0:T(8,128)(2,1)S(1)} collective-permute-done((bf16[2,4,3,16,512]{4,3,2,1,0:T(8,128)(2,1)S(1)}, bf16[2,4,3,16,512]{4,3,2,1,0:T(8,128)(2,1)S(1)}, u32[]{:S(2)}, u32[]{:S(2)}) %collective-permute-start.31) | collective-permute-done | bytes 393248 | tf_op jit(solution)/shard_map/ppermute | solution.py:26
  121.0 2.9 %collective-permute-done.32.rest_3_ = bf16[2,4,3,16,512]{4,3,2,1,0:T(8,128)(2,1)S(1)} collective-permute-done((bf16[2,4,3,16,512]{4,3,2,1,0:T(8,128)(2,1)S(1)}, bf16[2,4,3,16,512]{4,3,2,1,0:T(8,128)(2,1)S(1)}, u32[]{:S(2)}, u32[]{:S(2)}) %collective-permute-start.32) | collective-permute-done | bytes 393248 | tf_op jit(solution)/shard_map/ppermute | solution.py:26
  124.6 5.2 %shard_map.113 = (bf16[512,512]{1,0:T(8,128)(2,1)}, bf16[512,512]{1,0:T(8,128)(2,1)}, f32[2,512]{1,0:T(2,128)}, f32[3,16,512]{2,1,0:T(8,128)}) custom-call(s32[16]{0:T(128)} %stack.168.s_ref, bf16[512,512]{1,0:T(8,128)(2,1)} %collective-permute-done.20.q_prev, bf16[512,1024]{1,0:T(8,128)(2,1)} %q_ref.3, f32[3,512]{1,0:T(4,128)} %get-tuple-element.47.old_sq, ...), custom_call_target="tpu_custom_call" | custom-call | flops 1610612736 | bytes 3250176 | tf_op jit(solution)/shard_map/pallas_call | solution.py:75
  129.8 9.8 %collective-permute-start.33 = (f32[2,512]{1,0:T(2,128)}, f32[2,512]{1,0:T(2,128)S(1)}, u32[]{:S(2)}, u32[]{:S(2)}) collective-permute-start(f32[2,512]{1,0:T(2,128)} %get-tuple-element.57), channel_id=1, source_target_pairs={{0,64},{64,0},{128,192},{192,128},{1,65},{65,1},{129,193},{193,129... | collective-permute-start | bytes 12296 | tf_op jit(solution)/shard_map/ppermute | solution.py:336
  139.6 3.1 %collective-permute-start.34 = (f32[2,512]{1,0:T(2,128)}, f32[2,512]{1,0:T(2,128)S(1)}, u32[]{:S(2)}, u32[]{:S(2)}) collective-permute-start(f32[2,512]{1,0:T(2,128)} %get-tuple-element.57), channel_id=1, source_target_pairs={{0,128},{64,192},{128,0},{192,64},{1,129},{65,193},{129,1},{193,65... | collective-permute-start | bytes 12296 | tf_op jit(solution)/shard_map/ppermute | solution.py:336
  142.8 3.8 %collective-permute-start.37 = (bf16[512,512]{1,0:T(8,128)(2,1)}, bf16[512,512]{1,0:T(8,128)(2,1)S(1)}, u32[]{:S(2)}, u32[]{:S(2)}) collective-permute-start(bf16[512,512]{1,0:T(8,128)(2,1)} %get-tuple-element.61), channel_id=1, source_target_pairs={{0,7},{1,0},{2,1},{3,2},{4,3},{5,4},{6,5},{7,6},{8,15},{9,8},{10,9... | collective-permute-start | bytes 1572872 | tf_op jit(solution)/shard_map/ppermute | solution.py:32
  148.3 3.2 %collective-permute-start.36 = (f32[1,512]{1,0:T(1,128)S(1)}, f32[1,512]{1,0:T(1,128)S(1)}, u32[]{:S(2)}, u32[]{:S(2)}) collective-permute-start(f32[1,512]{1,0:T(1,128)S(1)} %slice.257), channel_id=1, source_target_pairs={{0,7},{1,0},{2,1},{3,2},{4,3},{5,4},{6,5},{7,6},{8,15},{9,8},{10,9... | collective-permute-start | bytes 6152 | tf_op jit(solution)/shard_map/ppermute | solution.py:32
  152.5 5.1 %shard_map.114 = f32[512,512]{1,0:T(8,128)} custom-call(s32[16]{0:T(128)} %stack.168.s_ref, bf16[512,1024]{1,0:T(8,128)(2,1)} %q_ref.3, bf16[512,1024]{1,0:T(8,128)(2,1)} %k_ref.3, bf16[512,1024]{1,0:T(8,128)(2,1)} %v_ref.3, bf16[2,512,512]{2,1,0:T(8,128)(2,1)} %copy-done.3, bf16[2,512,512]{2,1,0:T(8,128)(2,1)} %copy-done.4), custom_call_target="tpu_custom_call" | custom-call | flops 805306368 | bytes 5242880 | tf_op jit(solution)/shard_map/pallas_call | solution.py:75
  (125 shorter events, 38.6 us)
Async XLA Ops:
  1.5 6.9 %collective-permute-start = (f32[3,8,512]{2,1,0:T(8,128)S(1)}, f32[3,8,512]{2,1,0:T(8,128)S(1)}, u32[]{:S(2)}, u32[]{:S(2)}) collective-permute-start(f32[3,8,512]{2,1,0:T(8,128)S(1)} %get-tuple-element.79), channel_id=1, source_target_pairs={{0,1},{1,0},{2,3},{3,2},{4,5},{5,4},{6,7},{7,6},{8,9},{9,8},{10,11... | collective-permute-start | bytes 147464 | tf_op jit(solution)/shard_map/ppermute | solution.py:26
  6.8 15.3 %collective-permute-start.5 = (bf16[512,512]{1,0:T(8,128)(2,1)S(1)}, bf16[512,512]{1,0:T(8,128)(2,1)S(1)}, u32[]{:S(2)}, u32[]{:S(2)}) collective-permute-start(bf16[512,512]{1,0:T(8,128)(2,1)S(1)} %get-tuple-element.71), channel_id=1, source_target_pairs={{7,15},{15,23},{23,31},{31,39},{39,47},{47,55},{55,63},{71,79},{79... | collective-permute-start | bytes 1572872 | tf_op jit(solution)/shard_map/ppermute | solution.py:37
  11.0 5.8 %collective-permute-start.2 = (bf16[3,16,512]{2,1,0:T(8,128)(2,1)S(1)}, bf16[3,16,512]{2,1,0:T(8,128)(2,1)S(1)}, u32[]{:S(2)}, u32[]{:S(2)}) collective-permute-start(bf16[3,16,512]{2,1,0:T(8,128)(2,1)S(1)} %fusion.1), channel_id=1, source_target_pairs={{0,2},{1,3},{2,0},{3,1},{4,6},{5,7},{6,4},{7,5},{8,10},{9,11},{10,... | collective-permute-start | bytes 147464 | tf_op jit(solution)/shard_map/ppermute | solution.py:26
  11.5 7.0 %collective-permute-start.3 = (bf16[3,16,512]{2,1,0:T(8,128)(2,1)S(1)}, bf16[3,16,512]{2,1,0:T(8,128)(2,1)S(1)}, u32[]{:S(2)}, u32[]{:S(2)}) collective-permute-start(bf16[3,16,512]{2,1,0:T(8,128)(2,1)S(1)} %fusion.1), channel_id=1, source_target_pairs={{0,4},{1,5},{2,6},{3,7},{4,0},{5,1},{6,2},{7,3},{8,12},{9,13},{10,... | collective-permute-start | bytes 147464 | tf_op jit(solution)/shard_map/ppermute | solution.py:26
  22.1 23.6 %collective-permute-start.6 = (bf16[2,512,512]{2,1,0:T(8,128)(2,1)S(1)}, bf16[2,512,512]{2,1,0:T(8,128)(2,1)S(1)}, u32[]{:S(2)}, u32[]{:S(2)}) collective-permute-start(bf16[2,512,512]{2,1,0:T(8,128)(2,1)S(1)} %pad_maximum_fusion), channel_id=1, source_target_pairs={{0,1},{1,2},{2,3},{3,4},{4,5},{5,6},{6,7},{7,0},{8,9},{9,10},{10,1... | collective-permute-start | bytes 3145736 | tf_op jit(solution)/shard_map/ppermute | solution.py:32
  30.0 8.3 %collective-permute-start.10 = (bf16[2,4,3,16,512]{4,3,2,1,0:T(8,128)(2,1)}, bf16[2,4,3,16,512]{4,3,2,1,0:T(8,128)(2,1)S(1)}, u32[]{:S(2)}, u32[]{:S(2)}) collective-permute-start(bf16[2,4,3,16,512]{4,3,2,1,0:T(8,128)(2,1)} %pad_maximum_fusion.2.rest_0_), channel_id=1, source_target_pairs={{0,48},{1,49},{2,50},{3,51},{4,52},{5,53},{6,54},{7,55},{8,56},{9,... | collective-permute-start | bytes 1179656 | tf_op jit(solution)/shard_map/ppermute | solution.py:26
  32.2 15.1 %collective-permute-start.8 = (bf16[2,4,3,16,512]{4,3,2,1,0:T(8,128)(2,1)}, bf16[2,4,3,16,512]{4,3,2,1,0:T(8,128)(2,1)}, u32[]{:S(2)}, u32[]{:S(2)}) collective-permute-start(bf16[2,4,3,16,512]{4,3,2,1,0:T(8,128)(2,1)} %pad_maximum_fusion.2.rest_0_), channel_id=1, source_target_pairs={{0,16},{1,17},{2,18},{3,19},{4,20},{5,21},{6,22},{7,23},{8,24},{9,... | collective-permute-start | bytes 1179656 | tf_op jit(solution)/shard_map/ppermute | solution.py:26
  32.2 15.2 %collective-permute-start.9 = (bf16[2,4,3,16,512]{4,3,2,1,0:T(8,128)(2,1)}, bf16[2,4,3,16,512]{4,3,2,1,0:T(8,128)(2,1)}, u32[]{:S(2)}, u32[]{:S(2)}) collective-permute-start(bf16[2,4,3,16,512]{4,3,2,1,0:T(8,128)(2,1)} %pad_maximum_fusion.2.rest_0_), channel_id=1, source_target_pairs={{0,32},{1,33},{2,34},{3,35},{4,36},{5,37},{6,38},{7,39},{8,40},{9,... | collective-permute-start | bytes 1179656 | tf_op jit(solution)/shard_map/ppermute | solution.py:26
  38.4 21.8 %collective-permute-start.19 = (bf16[512,512]{1,0:T(8,128)(2,1)}, bf16[512,512]{1,0:T(8,128)(2,1)S(1)}, u32[]{:S(2)}, u32[]{:S(2)}) collective-permute-start(bf16[512,512]{1,0:T(8,128)(2,1)} %get-tuple-element.46), channel_id=1, source_target_pairs={{7,15},{15,23},{23,31},{31,39},{39,47},{47,55},{55,63},{71,79},{79... | collective-permute-start | bytes 1572872 | tf_op jit(solution)/shard_map/ppermute | solution.py:37
  45.7 14.4 %collective-permute-start.20 = (bf16[512,512]{1,0:T(8,128)(2,1)}, bf16[512,512]{1,0:T(8,128)(2,1)}, u32[]{:S(2)}, u32[]{:S(2)}) collective-permute-start(bf16[512,512]{1,0:T(8,128)(2,1)} %slice_select_fusion), channel_id=1, source_target_pairs={{0,1},{1,2},{2,3},{3,4},{4,5},{5,6},{6,7},{7,0},{8,9},{9,10},{10,1... | collective-permute-start | bytes 1572872 | tf_op jit(solution)/shard_map/ppermute | solution.py:32
  55.8 8.7 %collective-permute-start.11 = (bf16[4,3,16,512]{3,2,1,0:T(8,128)(2,1)}, bf16[4,3,16,512]{3,2,1,0:T(8,128)(2,1)S(1)}, u32[]{:S(2)}, u32[]{:S(2)}) collective-permute-start(bf16[4,3,16,512]{3,2,1,0:T(8,128)(2,1)} %get-tuple-element.38), channel_id=1, source_target_pairs={{0,8},{1,9},{2,10},{3,11},{4,12},{5,13},{6,14},{7,15},{8,0},{9,1},... | collective-permute-start | bytes 589832 | tf_op jit(solution)/shard_map/ppermute | solution.py:26
  58.2 7.6 %collective-permute-start.12 = (bf16[4,3,16,512]{3,2,1,0:T(8,128)(2,1)}, bf16[4,3,16,512]{3,2,1,0:T(8,128)(2,1)S(1)}, u32[]{:S(2)}, u32[]{:S(2)}) collective-permute-start(bf16[4,3,16,512]{3,2,1,0:T(8,128)(2,1)} %get-tuple-element.39), channel_id=1, source_target_pairs={{0,16},{1,17},{2,18},{3,19},{4,20},{5,21},{6,22},{7,23},{8,24},{9,... | collective-permute-start | bytes 589832 | tf_op jit(solution)/shard_map/ppermute | solution.py:26
  59.4 8.1 %collective-permute-start.13 = (bf16[4,3,16,512]{3,2,1,0:T(8,128)(2,1)}, bf16[4,3,16,512]{3,2,1,0:T(8,128)(2,1)S(1)}, u32[]{:S(2)}, u32[]{:S(2)}) collective-permute-start(bf16[4,3,16,512]{3,2,1,0:T(8,128)(2,1)} %get-tuple-element.40), channel_id=1, source_target_pairs={{0,24},{1,25},{2,26},{3,27},{4,28},{5,29},{6,30},{7,31},{8,16},{9,... | collective-permute-start | bytes 589832 | tf_op jit(solution)/shard_map/ppermute | solution.py:26
  60.4 23.6 %collective-permute-start.21 = (bf16[2,512,512]{2,1,0:T(8,128)(2,1)S(1)}, bf16[2,512,512]{2,1,0:T(8,128)(2,1)S(1)}, u32[]{:S(2)}, u32[]{:S(2)}) collective-permute-start(bf16[2,512,512]{2,1,0:T(8,128)(2,1)S(1)} %maximum_select_fusion), channel_id=1, source_target_pairs={{0,1},{1,2},{2,3},{3,4},{4,5},{5,6},{6,7},{7,0},{8,9},{9,10},{10,1... | collective-permute-start | bytes 3145736 | tf_op jit(solution)/shard_map/ppermute | solution.py:32
  61.1 10.7 %collective-permute-start.14 = (bf16[4,3,16,512]{3,2,1,0:T(8,128)(2,1)S(1)}, bf16[4,3,16,512]{3,2,1,0:T(8,128)(2,1)S(1)}, u32[]{:S(2)}, u32[]{:S(2)}) collective-permute-start(bf16[4,3,16,512]{3,2,1,0:T(8,128)(2,1)S(1)} %copy-done.21), channel_id=1, source_target_pairs={{0,32},{1,33},{2,34},{3,35},{4,36},{5,37},{6,38},{7,39},{8,40},{9,... | collective-permute-start | bytes 589832 | tf_op jit(solution)/shard_map/ppermute | solution.py:26
  64.4 12.6 %collective-permute-start.15 = (bf16[4,3,16,512]{3,2,1,0:T(8,128)(2,1)S(1)}, bf16[4,3,16,512]{3,2,1,0:T(8,128)(2,1)S(1)}, u32[]{:S(2)}, u32[]{:S(2)}) collective-permute-start(bf16[4,3,16,512]{3,2,1,0:T(8,128)(2,1)S(1)} %copy-done.20), channel_id=1, source_target_pairs={{0,40},{1,41},{2,42},{3,43},{4,44},{5,45},{6,46},{7,47},{8,32},{9,... | collective-permute-start | bytes 589832 | tf_op jit(solution)/shard_map/ppermute | solution.py:26
  65.8 11.3 %collective-permute-start.16 = (bf16[4,3,16,512]{3,2,1,0:T(8,128)(2,1)S(1)}, bf16[4,3,16,512]{3,2,1,0:T(8,128)(2,1)S(1)}, u32[]{:S(2)}, u32[]{:S(2)}) collective-permute-start(bf16[4,3,16,512]{3,2,1,0:T(8,128)(2,1)S(1)} %copy-done.19), channel_id=1, source_target_pairs={{0,48},{1,49},{2,50},{3,51},{4,52},{5,53},{6,54},{7,55},{8,56},{9,... | collective-permute-start | bytes 589832 | tf_op jit(solution)/shard_map/ppermute | solution.py:26
  67.5 15.6 %collective-permute-start.17 = (bf16[4,3,16,512]{3,2,1,0:T(8,128)(2,1)S(1)}, bf16[4,3,16,512]{3,2,1,0:T(8,128)(2,1)S(1)}, u32[]{:S(2)}, u32[]{:S(2)}) collective-permute-start(bf16[4,3,16,512]{3,2,1,0:T(8,128)(2,1)S(1)} %copy-done.18), channel_id=1, source_target_pairs={{0,56},{1,57},{2,58},{3,59},{4,60},{5,61},{6,62},{7,63},{8,48},{9,... | collective-permute-start | bytes 589832 | tf_op jit(solution)/shard_map/ppermute | solution.py:26
  83.2 19.5 %collective-permute-start.18 = (bf16[2,512,512]{2,1,0:T(8,128)(2,1)S(1)}, bf16[2,512,512]{2,1,0:T(8,128)(2,1)S(1)}, u32[]{:S(2)}, u32[]{:S(2)}) collective-permute-start(bf16[2,512,512]{2,1,0:T(8,128)(2,1)S(1)} %copy-done.6), channel_id=1, source_target_pairs={{7,15},{15,23},{23,31},{31,39},{39,47},{47,55},{55,63},{71,79},{79... | collective-permute-start | bytes 3145736 | tf_op jit(solution)/shard_map/ppermute | solution.py:37
  84.0 5.7 %collective-permute-start.22 = (bf16[3,16,512]{2,1,0:T(8,128)(2,1)S(1)}, bf16[3,16,512]{2,1,0:T(8,128)(2,1)S(1)}, u32[]{:S(2)}, u32[]{:S(2)}) collective-permute-start(bf16[3,16,512]{2,1,0:T(8,128)(2,1)S(1)} %get-tuple-element.51), channel_id=1, source_target_pairs={{0,2},{1,3},{2,0},{3,1},{4,6},{5,7},{6,4},{7,5},{8,10},{9,11},{10,... | collective-permute-start | bytes 147464 | tf_op jit(solution)/shard_map/ppermute | solution.py:26
  84.1 7.0 %collective-permute-start.23 = (bf16[3,16,512]{2,1,0:T(8,128)(2,1)S(1)}, bf16[3,16,512]{2,1,0:T(8,128)(2,1)S(1)}, u32[]{:S(2)}, u32[]{:S(2)}) collective-permute-start(bf16[3,16,512]{2,1,0:T(8,128)(2,1)S(1)} %fusion.3), channel_id=1, source_target_pairs={{0,4},{1,5},{2,6},{3,7},{4,0},{5,1},{6,2},{7,3},{8,12},{9,13},{10,... | collective-permute-start | bytes 147464 | tf_op jit(solution)/shard_map/ppermute | solution.py:26
  93.4 5.7 %collective-permute-start.25 = (bf16[3,16,512]{2,1,0:T(8,128)(2,1)S(1)}, bf16[3,16,512]{2,1,0:T(8,128)(2,1)S(1)}, u32[]{:S(2)}, u32[]{:S(2)}) collective-permute-start(bf16[3,16,512]{2,1,0:T(8,128)(2,1)S(1)} %get-tuple-element.64), channel_id=1, source_target_pairs={{0,2},{1,3},{2,0},{3,1},{4,6},{5,7},{6,4},{7,5},{8,10},{9,11},{10,... | collective-permute-start | bytes 147464 | tf_op jit(solution)/shard_map/ppermute | solution.py:26
  95.3 6.8 %collective-permute-start.26 = (bf16[3,16,512]{2,1,0:T(8,128)(2,1)S(1)}, bf16[3,16,512]{2,1,0:T(8,128)(2,1)S(1)}, u32[]{:S(2)}, u32[]{:S(2)}) collective-permute-start(bf16[3,16,512]{2,1,0:T(8,128)(2,1)S(1)} %get-tuple-element.64), channel_id=1, source_target_pairs={{0,4},{1,5},{2,6},{3,7},{4,0},{5,1},{6,2},{7,3},{8,12},{9,13},{10,... | collective-permute-start | bytes 147464 | tf_op jit(solution)/shard_map/ppermute | solution.py:26
  104.2 47.3 %collective-permute-start.28 = (bf16[2,512,512]{2,1,0:T(8,128)(2,1)S(1)}, bf16[2,512,512]{2,1,0:T(8,128)(2,1)S(1)}, u32[]{:S(2)}, u32[]{:S(2)}) collective-permute-start(bf16[2,512,512]{2,1,0:T(8,128)(2,1)S(1)} %collective-permute-done.18), channel_id=1, source_target_pairs={{7,0},{15,8},{23,16},{31,24},{39,32},{47,40},{55,48},{63,56},{71,6... | collective-permute-start | bytes 3145736 | tf_op jit(solution)/shard_map/ppermute | solution.py:42
  107.7 8.7 %collective-permute-start.30 = (bf16[2,4,3,16,512]{4,3,2,1,0:T(8,128)(2,1)S(1)}, bf16[2,4,3,16,512]{4,3,2,1,0:T(8,128)(2,1)S(1)}, u32[]{:S(2)}, u32[]{:S(2)}) collective-permute-start(bf16[2,4,3,16,512]{4,3,2,1,0:T(8,128)(2,1)S(1)} %pad_maximum_fusion.3.rest_0_), channel_id=1, source_target_pairs={{0,16},{1,17},{2,18},{3,19},{4,20},{5,21},{6,22},{7,23},{8,24},{9,... | collective-permute-start | bytes 1179656 | tf_op jit(solution)/shard_map/ppermute | solution.py:26
  108.6 12.3 %collective-permute-start.31 = (bf16[2,4,3,16,512]{4,3,2,1,0:T(8,128)(2,1)S(1)}, bf16[2,4,3,16,512]{4,3,2,1,0:T(8,128)(2,1)S(1)}, u32[]{:S(2)}, u32[]{:S(2)}) collective-permute-start(bf16[2,4,3,16,512]{4,3,2,1,0:T(8,128)(2,1)S(1)} %pad_maximum_fusion.3.rest_0_), channel_id=1, source_target_pairs={{0,32},{1,33},{2,34},{3,35},{4,36},{5,37},{6,38},{7,39},{8,40},{9,... | collective-permute-start | bytes 1179656 | tf_op jit(solution)/shard_map/ppermute | solution.py:26
  111.5 12.3 %collective-permute-start.32 = (bf16[2,4,3,16,512]{4,3,2,1,0:T(8,128)(2,1)S(1)}, bf16[2,4,3,16,512]{4,3,2,1,0:T(8,128)(2,1)S(1)}, u32[]{:S(2)}, u32[]{:S(2)}) collective-permute-start(bf16[2,4,3,16,512]{4,3,2,1,0:T(8,128)(2,1)S(1)} %pad_maximum_fusion.3.rest_0_), channel_id=1, source_target_pairs={{0,48},{1,49},{2,50},{3,51},{4,52},{5,53},{6,54},{7,55},{8,56},{9,... | collective-permute-start | bytes 1179656 | tf_op jit(solution)/shard_map/ppermute | solution.py:26
  129.8 17.6 %collective-permute-start.33 = (f32[2,512]{1,0:T(2,128)}, f32[2,512]{1,0:T(2,128)S(1)}, u32[]{:S(2)}, u32[]{:S(2)}) collective-permute-start(f32[2,512]{1,0:T(2,128)} %get-tuple-element.57), channel_id=1, source_target_pairs={{0,64},{64,0},{128,192},{192,128},{1,65},{65,1},{129,193},{193,129... | collective-permute-start | bytes 12296 | tf_op jit(solution)/shard_map/ppermute | solution.py:336
  139.6 7.9 %collective-permute-start.34 = (f32[2,512]{1,0:T(2,128)}, f32[2,512]{1,0:T(2,128)S(1)}, u32[]{:S(2)}, u32[]{:S(2)}) collective-permute-start(f32[2,512]{1,0:T(2,128)} %get-tuple-element.57), channel_id=1, source_target_pairs={{0,128},{64,192},{128,0},{192,64},{1,129},{65,193},{129,1},{193,65... | collective-permute-start | bytes 12296 | tf_op jit(solution)/shard_map/ppermute | solution.py:336
  142.8 15.4 %collective-permute-start.37 = (bf16[512,512]{1,0:T(8,128)(2,1)}, bf16[512,512]{1,0:T(8,128)(2,1)S(1)}, u32[]{:S(2)}, u32[]{:S(2)}) collective-permute-start(bf16[512,512]{1,0:T(8,128)(2,1)} %get-tuple-element.61), channel_id=1, source_target_pairs={{0,7},{1,0},{2,1},{3,2},{4,3},{5,4},{6,5},{7,6},{8,15},{9,8},{10,9... | collective-permute-start | bytes 1572872 | tf_op jit(solution)/shard_map/ppermute | solution.py:32
  147.4 10.8 %collective-permute-start.38 = (f32[3,8,512]{2,1,0:T(8,128)S(1)}, f32[3,8,512]{2,1,0:T(8,128)S(1)}, u32[]{:S(2)}, u32[]{:S(2)}) collective-permute-start(f32[3,8,512]{2,1,0:T(8,128)S(1)} %get-tuple-element.78), channel_id=1, source_target_pairs={{0,1},{1,0},{2,3},{3,2},{4,5},{5,4},{6,7},{7,6},{8,9},{9,8},{10,11... | collective-permute-start | bytes 147464 | tf_op jit(solution)/shard_map/ppermute | solution.py:26
  148.3 10.0 %collective-permute-start.36 = (f32[1,512]{1,0:T(1,128)S(1)}, f32[1,512]{1,0:T(1,128)S(1)}, u32[]{:S(2)}, u32[]{:S(2)}) collective-permute-start(f32[1,512]{1,0:T(1,128)S(1)} %slice.257), channel_id=1, source_target_pairs={{0,7},{1,0},{2,1},{3,2},{4,3},{5,4},{6,5},{7,6},{8,15},{9,8},{10,9... | collective-permute-start | bytes 6152 | tf_op jit(solution)/shard_map/ppermute | solution.py:32
  (30 other events, 264.0 us)

commit v5 on v4

--- a/solution.py
+++ b/solution.py
@@ -14,7 +14,7 @@
 TILE = 512
 EPS = 1e-06
 NEG = -1e30
-VMEM_LIMIT = 56 * 1024 * 1024
+VMEM_LIMIT = 40 * 1024 * 1024
 F32 = jnp.float32
 BF16 = jnp.bfloat16
 
@@ -65,6 +65,9 @@
 
 def head_block(pick):
     return pl.BlockSpec((BLK, HD), lambda i, s: (0, s[pick]))
+
+
+IN_VMEM = pl.BlockSpec(memory_space=pltpu.VMEM)
 
 
 def call(kernel, scalars, ins, in_specs, outs, scratch=(), flops=0):
@@ -285,12 +288,12 @@
             flops=4 * BLK * 768 * HD,
         )
 
-    block_specs = [whole((2, ZQ, 3, 16, HD))] * (XY // 2)
+    block_specs = [IN_VMEM] * (XY // 2)
     grad_out = call(
         gradient_kernel,
         scalars,
         [halo, keys, values, rate_prev, rate_mine] + w_blocks,
-        [whole((2, BLK, HD)), head_block(0), head_block(0), whole((1, BLK)), whole((1, BLK))]
+        [IN_VMEM, head_block(0), head_block(0), whole((1, BLK)), whole((1, BLK))]
         + block_specs,
         [shape((ZQ, 3, 16, HD), F32)] + [shape((ZQ, 3, 16, HD), BF16)] * (XY - 1) + [shape((3, HD), F32)],
         [pltpu.VMEM((3, HD, HD), BF16)]

time: 162 us -> 162 us (level)
  Pallas kernels: 23.4 us -> 13.6 us
  starting transfers between devices: 69.1 us -> 76.3 us
  waiting for transfers between devices: 52.6 us -> 58.7 us
  local copies, waits for them, and re-layouts: 3.81 us -> 1.74 us
    pallas_call x4, Pallas kernels: 23.4 us -> 13.6 us  [call(): pl.pallas_call(kernel, out_shape=outs, grid_spec=pltpu.PrefetchScalarGrid...]
    ppermute x6, starting transfers between devices: 10.2 us -> 16 us  [ring(): return lax.ppermute(value, 'seq', pairs)]
    ppermute x26, waiting for transfers between devices: 42.7 us -> 47.7 us  [move_xor(): return lax.ppermute(value, 'seq', [(i, i ^ mask) for i in range(n)])]
  transfers between devices with their start and end apart: 39 -> 39, of which waited for: 18 -> 19; matrix products, arithmetic and copies ran while one was open for 5% -> 5% of each run, Pallas kernels for 14% -> 8%
where the time goes in v5:
time: 162 us
  starting transfers between devices  76.3 us (47%)
  waiting for transfers between devices  58.7 us (36%)
  Pallas kernels  13.6 us (8%)
  other arithmetic  10.8 us (7%)
  local copies, waits for them, and re-layouts  1.74 us (1%)
    ppermute x26, waiting for transfers between devices, move_xor(): return lax.ppermute(value, 'seq', [(i, i ^ mask) for i in range(n)])  47.7 us
    ppermute x26, starting transfers between devices, move_xor(): return lax.ppermute(value, 'seq', [(i, i ^ mask) for i in range(n)])  43.8 us
    ppermute x6, starting transfers between devices, ring(): return lax.ppermute(value, 'seq', pairs)  16 us
    pallas_call x4, Pallas kernels, call(): pl.pallas_call(kernel, out_shape=outs, grid_spec=pltpu.PrefetchScalarGrid...  13.6 us
    ppermute x3, starting transfers between devices, local(): lax.ppermute(sq, 'head', [(i, i ^ k) for i in range(heads)])  11.5 us
    ppermute x6, waiting for transfers between devices, ring(): return lax.ppermute(value, 'seq', pairs)  10.9 us
    ppermute x3, starting transfers between devices, to_next_plane(): lax.ppermute(value, 'seq', [(i, i + RING) for i in range(RING - 1, n - RI...  3.65 us
    slice x2, other arithmetic, head_of(): return jnp.where(flag, array[:, :HD], array[:, HD:])  3.28 us
  transfers between devices with their start and end apart: 39, of which 19 were waited for; matrix products, arithmetic and copies ran while one was open for 5% of the time, Pallas kernels for 8%

profile of v5, /device:TPU:1, one launch (start us, length us, event | category | flops | bytes accessed | tf_op | source)
XLA Modules:
  0.0 162.0 jit_solution(9860609925084800738)
XLA Ops:
  1.5 2.6 %collective-permute-start = (f32[3,8,512]{2,1,0:T(8,128)S(1)}, f32[3,8,512]{2,1,0:T(8,128)S(1)}, u32[]{:S(2)}, u32[]{:S(2)}) collective-permute-start(f32[3,8,512]{2,1,0:T(8,128)S(1)} %get-tuple-element.79), channel_id=1, source_target_pairs={{0,1},{1,0},{2,3},{3,2},{4,5},{5,4},{6,7},{7,6},{8,9},{9,8},{10,11... | collective-permute-start | bytes 147464 | tf_op jit(solution)/shard_map/ppermute | solution.py:26
  4.8 2.2 %fusion.9 = (bf16[512,512]{1,0:T(8,128)(2,1)S(1)}, bf16[1,512,512]{2,1,0:T(8,128)(2,1)}, bf16[1,512,512]{2,1,0:T(8,128)(2,1)S(1)}) fusion(bf16[512,1024]{1,0:T(8,128)(2,1)} %k_ref.3, pred[]{:T(512)S(6)} %eq.6, pred[]{:T(512)S(6)} %not.2), kind=kLoop, calls=%fused_computation.43 | loop fusion | flops 524288 | bytes 2621442 | tf_op jit(solution)/shard_map/slice | solution.py:249
  10.4 2.3 %collective-permute-start.2 = (bf16[3,16,512]{2,1,0:T(8,128)(2,1)S(1)}, bf16[3,16,512]{2,1,0:T(8,128)(2,1)S(1)}, u32[]{:S(2)}, u32[]{:S(2)}) collective-permute-start(bf16[3,16,512]{2,1,0:T(8,128)(2,1)S(1)} %fusion.1), channel_id=1, source_target_pairs={{0,2},{1,3},{2,0},{3,1},{4,6},{5,7},{6,4},{7,5},{8,10},{9,11},{10,... | collective-permute-start | bytes 147464 | tf_op jit(solution)/shard_map/ppermute | solution.py:26
  12.7 4.9 %collective-permute-start.3 = (bf16[3,16,512]{2,1,0:T(8,128)(2,1)S(1)}, bf16[3,16,512]{2,1,0:T(8,128)(2,1)S(1)}, u32[]{:S(2)}, u32[]{:S(2)}) collective-permute-start(bf16[3,16,512]{2,1,0:T(8,128)(2,1)S(1)} %fusion.1), channel_id=1, source_target_pairs={{0,4},{1,5},{2,6},{3,7},{4,0},{5,1},{6,2},{7,3},{8,12},{9,13},{10,... | collective-permute-start | bytes 147464 | tf_op jit(solution)/shard_map/ppermute | solution.py:26
  19.6 3.1 %collective-permute-done.4 = bf16[3,16,512]{2,1,0:T(8,128)(2,1)S(1)} collective-permute-done((bf16[3,16,512]{2,1,0:T(8,128)(2,1)S(1)}, bf16[3,16,512]{2,1,0:T(8,128)(2,1)S(1)}, u32[]{:S(2)}, u32[]{:S(2)}) %collective-permute-start.4) | collective-permute-done | bytes 49184 | tf_op jit(solution)/shard_map/ppermute | solution.py:26
  22.7 2.9 %collective-permute-start.6 = (bf16[2,512,512]{2,1,0:T(8,128)(2,1)S(1)}, bf16[2,512,512]{2,1,0:T(8,128)(2,1)S(1)}, u32[]{:S(2)}, u32[]{:S(2)}) collective-permute-start(bf16[2,512,512]{2,1,0:T(8,128)(2,1)S(1)} %pad_maximum_fusion), channel_id=1, source_target_pairs={{0,1},{1,2},{2,3},{3,4},{4,5},{5,6},{6,7},{7,0},{8,9},{9,10},{10,1... | collective-permute-start | bytes 3145736 | tf_op jit(solution)/shard_map/ppermute | solution.py:32
  25.8 4.7 %collective-permute-done.7 = bf16[4,3,16,512]{3,2,1,0:T(8,128)(2,1)S(1)} collective-permute-done((bf16[4,3,16,512]{3,2,1,0:T(8,128)(2,1)S(1)}, bf16[4,3,16,512]{3,2,1,0:T(8,128)(2,1)S(1)}, u32[]{:S(2)}, u32[]{:S(2)}) %collective-permute-start.7) | collective-permute-done | bytes 196640 | tf_op jit(solution)/shard_map/ppermute | solution.py:26
  31.6 2.8 %collective-permute-start.9 = (bf16[2,4,3,16,512]{4,3,2,1,0:T(8,128)(2,1)S(1)}, bf16[2,4,3,16,512]{4,3,2,1,0:T(8,128)(2,1)}, u32[]{:S(2)}, u32[]{:S(2)}) collective-permute-start(bf16[2,4,3,16,512]{4,3,2,1,0:T(8,128)(2,1)S(1)} %pad_maximum_fusion.2.rest_0_), channel_id=1, source_target_pairs={{0,32},{1,33},{2,34},{3,35},{4,36},{5,37},{6,38},{7,39},{8,40},{9,... | collective-permute-start | bytes 1179656 | tf_op jit(solution)/shard_map/ppermute | solution.py:26
  35.3 3.4 %collective-permute-done.10.rest_3_ = bf16[2,4,3,16,512]{4,3,2,1,0:T(8,128)(2,1)S(1)} collective-permute-done((bf16[2,4,3,16,512]{4,3,2,1,0:T(8,128)(2,1)S(1)}, bf16[2,4,3,16,512]{4,3,2,1,0:T(8,128)(2,1)S(1)}, u32[]{:S(2)}, u32[]{:S(2)}) %collective-permute-start.10) | collective-permute-done | bytes 393248 | tf_op jit(solution)/shard_map/ppermute | solution.py:26
  40.9 4.8 %collective-permute-done.6.halo = bf16[2,512,512]{2,1,0:T(8,128)(2,1)S(1)} collective-permute-done((bf16[2,512,512]{2,1,0:T(8,128)(2,1)S(1)}, bf16[2,512,512]{2,1,0:T(8,128)(2,1)S(1)}, u32[]{:S(2)}, u32[]{:S(2)}) %collective-permute-start.6) | collective-permute-done | bytes 1048608 | tf_op jit(solution)/shard_map/ppermute | solution.py:32
  45.7 2.0 %collective-permute-start.20 = (bf16[512,512]{1,0:T(8,128)(2,1)}, bf16[512,512]{1,0:T(8,128)(2,1)}, u32[]{:S(2)}, u32[]{:S(2)}) collective-permute-start(bf16[512,512]{1,0:T(8,128)(2,1)} %slice_select_fusion), channel_id=1, source_target_pairs={{0,1},{1,2},{2,3},{3,4},{4,5},{5,6},{6,7},{7,0},{8,9},{9,10},{10,1... | collective-permute-start | bytes 1572872 | tf_op jit(solution)/shard_map/ppermute | solution.py:32
  49.4 6.1 %shard_map.111 = (f32[4,3,16,512]{3,2,1,0:T(8,128)S(1)}, bf16[4,3,16,512]{3,2,1,0:T(8,128)(2,1)S(1)}, bf16[4,3,16,512]{3,2,1,0:T(8,128)(2,1)S(1)}, bf16[4,3,16,5...) custom-call(s32[16]{0:T(128)S(1)} %stack.168.s_ref, ...), custom_call_target="tpu_custom_call" | custom-call | flops 3221225472 | bytes 4722688 | tf_op jit(solution)/shard_map/pallas_call | solution.py:78
  61.9 3.5 %collective-permute-start.14 = (bf16[4,3,16,512]{3,2,1,0:T(8,128)(2,1)S(1)}, bf16[4,3,16,512]{3,2,1,0:T(8,128)(2,1)S(1)}, u32[]{:S(2)}, u32[]{:S(2)}) collective-permute-start(bf16[4,3,16,512]{3,2,1,0:T(8,128)(2,1)S(1)} %get-tuple-element.41), channel_id=1, source_target_pairs={{0,32},{1,33},{2,34},{3,35},{4,36},{5,37},{6,38},{7,39},{8,40},{9,... | collective-permute-start | bytes 589832 | tf_op jit(solution)/shard_map/ppermute | solution.py:26
  66.0 2.5 %collective-permute-start.16 = (bf16[4,3,16,512]{3,2,1,0:T(8,128)(2,1)S(1)}, bf16[4,3,16,512]{3,2,1,0:T(8,128)(2,1)S(1)}, u32[]{:S(2)}, u32[]{:S(2)}) collective-permute-start(bf16[4,3,16,512]{3,2,1,0:T(8,128)(2,1)S(1)} %get-tuple-element.43), channel_id=1, source_target_pairs={{0,48},{1,49},{2,50},{3,51},{4,52},{5,53},{6,54},{7,55},{8,56},{9,... | collective-permute-start | bytes 589832 | tf_op jit(solution)/shard_map/ppermute | solution.py:26
  70.8 5.7 %collective-permute-done.15 = bf16[4,3,16,512]{3,2,1,0:T(8,128)(2,1)S(1)} collective-permute-done((bf16[4,3,16,512]{3,2,1,0:T(8,128)(2,1)S(1)}, bf16[4,3,16,512]{3,2,1,0:T(8,128)(2,1)S(1)}, u32[]{:S(2)}, u32[]{:S(2)}) %collective-permute-start.15) | collective-permute-done | bytes 196640 | tf_op jit(solution)/shard_map/ppermute | solution.py:26
  76.5 3.3 %collective-permute-done.16 = bf16[4,3,16,512]{3,2,1,0:T(8,128)(2,1)S(1)} collective-permute-done((bf16[4,3,16,512]{3,2,1,0:T(8,128)(2,1)S(1)}, bf16[4,3,16,512]{3,2,1,0:T(8,128)(2,1)S(1)}, u32[]{:S(2)}, u32[]{:S(2)}) %collective-permute-start.16) | collective-permute-done | bytes 196640 | tf_op jit(solution)/shard_map/ppermute | solution.py:26
  79.8 4.2 %collective-permute-done.17 = bf16[4,3,16,512]{3,2,1,0:T(8,128)(2,1)S(1)} collective-permute-done((bf16[4,3,16,512]{3,2,1,0:T(8,128)(2,1)S(1)}, bf16[4,3,16,512]{3,2,1,0:T(8,128)(2,1)S(1)}, u32[]{:S(2)}, u32[]{:S(2)}) %collective-permute-start.17) | collective-permute-done | bytes 196640 | tf_op jit(solution)/shard_map/ppermute | solution.py:26
  85.1 3.9 %collective-permute-start.23 = (bf16[3,16,512]{2,1,0:T(8,128)(2,1)S(1)}, bf16[3,16,512]{2,1,0:T(8,128)(2,1)S(1)}, u32[]{:S(2)}, u32[]{:S(2)}) collective-permute-start(bf16[3,16,512]{2,1,0:T(8,128)(2,1)S(1)} %fusion.3), channel_id=1, source_target_pairs={{0,4},{1,5},{2,6},{3,7},{4,0},{5,1},{6,2},{7,3},{8,12},{9,13},{10,... | collective-permute-start | bytes 147464 | tf_op jit(solution)/shard_map/ppermute | solution.py:26
  92.0 2.0 %collective-permute-done.24 = bf16[3,16,512]{2,1,0:T(8,128)(2,1)S(1)} collective-permute-done((bf16[3,16,512]{2,1,0:T(8,128)(2,1)S(1)}, bf16[3,16,512]{2,1,0:T(8,128)(2,1)S(1)}, u32[]{:S(2)}, u32[]{:S(2)}) %collective-permute-start.24) | collective-permute-done | bytes 49184 | tf_op jit(solution)/shard_map/ppermute | solution.py:26
  94.2 2.1 %collective-permute-start.25 = (bf16[3,16,512]{2,1,0:T(8,128)(2,1)S(1)}, bf16[3,16,512]{2,1,0:T(8,128)(2,1)S(1)}, u32[]{:S(2)}, u32[]{:S(2)}) collective-permute-start(bf16[3,16,512]{2,1,0:T(8,128)(2,1)S(1)} %get-tuple-element.64), channel_id=1, source_target_pairs={{0,2},{1,3},{2,0},{3,1},{4,6},{5,7},{6,4},{7,5},{8,10},{9,11},{10,... | collective-permute-start | bytes 147464 | tf_op jit(solution)/shard_map/ppermute | solution.py:26
  99.9 3.2 %collective-permute-done.26 = bf16[3,16,512]{2,1,0:T(8,128)(2,1)S(1)} collective-permute-done((bf16[3,16,512]{2,1,0:T(8,128)(2,1)S(1)}, bf16[3,16,512]{2,1,0:T(8,128)(2,1)S(1)}, u32[]{:S(2)}, u32[]{:S(2)}) %collective-permute-start.26) | collective-permute-done | bytes 49184 | tf_op jit(solution)/shard_map/ppermute | solution.py:26
  106.9 2.1 %collective-permute-done.29 = bf16[4,3,16,512]{3,2,1,0:T(8,128)(2,1)S(1)} collective-permute-done((bf16[4,3,16,512]{3,2,1,0:T(8,128)(2,1)S(1)}, bf16[4,3,16,512]{3,2,1,0:T(8,128)(2,1)S(1)}, u32[]{:S(2)}, u32[]{:S(2)}) %collective-permute-start.29) | collective-permute-done | bytes 196640 | tf_op jit(solution)/shard_map/ppermute | solution.py:26
  109.0 2.5 %collective-permute-start.30 = (bf16[2,4,3,16,512]{4,3,2,1,0:T(8,128)(2,1)S(1)}, bf16[2,4,3,16,512]{4,3,2,1,0:T(8,128)(2,1)S(1)}, u32[]{:S(2)}, u32[]{:S(2)}) collective-permute-start(bf16[2,4,3,16,512]{4,3,2,1,0:T(8,128)(2,1)S(1)} %pad_maximum_fusion.3.rest_0_), channel_id=1, source_target_pairs={{0,16},{1,17},{2,18},{3,19},{4,20},{5,21},{6,22},{7,23},{8,24},{9,... | collective-permute-start | bytes 1179656 | tf_op jit(solution)/shard_map/ppermute | solution.py:26
  111.5 2.9 %collective-permute-start.31 = (bf16[2,4,3,16,512]{4,3,2,1,0:T(8,128)(2,1)S(1)}, bf16[2,4,3,16,512]{4,3,2,1,0:T(8,128)(2,1)S(1)}, u32[]{:S(2)}, u32[]{:S(2)}) collective-permute-start(bf16[2,4,3,16,512]{4,3,2,1,0:T(8,128)(2,1)S(1)} %pad_maximum_fusion.3.rest_0_), channel_id=1, source_target_pairs={{0,32},{1,33},{2,34},{3,35},{4,36},{5,37},{6,38},{7,39},{8,40},{9,... | collective-permute-start | bytes 1179656 | tf_op jit(solution)/shard_map/ppermute | solution.py:26
  116.7 8.3 %collective-permute-done.31.rest_2_ = bf16[2,4,3,16,512]{4,3,2,1,0:T(8,128)(2,1)S(1)} collective-permute-done((bf16[2,4,3,16,512]{4,3,2,1,0:T(8,128)(2,1)S(1)}, bf16[2,4,3,16,512]{4,3,2,1,0:T(8,128)(2,1)S(1)}, u32[]{:S(2)}, u32[]{:S(2)}) %collective-permute-start.31) | collective-permute-done | bytes 393248 | tf_op jit(solution)/shard_map/ppermute | solution.py:26
  125.0 2.3 %collective-permute-done.32.rest_3_ = bf16[2,4,3,16,512]{4,3,2,1,0:T(8,128)(2,1)S(1)} collective-permute-done((bf16[2,4,3,16,512]{4,3,2,1,0:T(8,128)(2,1)S(1)}, bf16[2,4,3,16,512]{4,3,2,1,0:T(8,128)(2,1)S(1)}, u32[]{:S(2)}, u32[]{:S(2)}) %collective-permute-start.32) | collective-permute-done | bytes 393248 | tf_op jit(solution)/shard_map/ppermute | solution.py:26
  127.3 3.6 %shard_map.113 = (bf16[512,512]{1,0:T(8,128)(2,1)S(1)}, bf16[512,512]{1,0:T(8,128)(2,1)S(1)}, f32[2,512]{1,0:T(2,128)S(1)}, f32[3,16,512]{2,1,0:T(8,128)S(1)}) custom-call(s32[16]{0:T(128)S(1)} %stack.168.s_ref, bf16[512,512]{1,0:T(8,128)(2,1)} %collective-permute-done.20.q_prev, bf16[512,1024]{1,0:T(8,128)(2,1)S(1)} %copy-done.2, ...), custom_call_target="tpu_custom_call" | custom-call | flops 1610612736 | bytes 3250176 | tf_op jit(solution)/shard_map/pallas_call | solution.py:78
  130.9 8.3 %collective-permute-start.33 = (f32[2,512]{1,0:T(2,128)S(1)}, f32[2,512]{1,0:T(2,128)S(1)}, u32[]{:S(2)}, u32[]{:S(2)}) collective-permute-start(f32[2,512]{1,0:T(2,128)S(1)} %get-tuple-element.57), channel_id=1, source_target_pairs={{0,64},{64,0},{128,192},{192,128},{1,65},{65,1},{129,193},{193,129... | collective-permute-start | bytes 12296 | tf_op jit(solution)/shard_map/ppermute | solution.py:339
  139.2 2.9 %collective-permute-start.34 = (f32[2,512]{1,0:T(2,128)S(1)}, f32[2,512]{1,0:T(2,128)S(1)}, u32[]{:S(2)}, u32[]{:S(2)}) collective-permute-start(f32[2,512]{1,0:T(2,128)S(1)} %get-tuple-element.57), channel_id=1, source_target_pairs={{0,128},{64,192},{128,0},{192,64},{1,129},{65,193},{129,1},{193,65... | collective-permute-start | bytes 12296 | tf_op jit(solution)/shard_map/ppermute | solution.py:339
  142.4 6.0 %collective-permute-start.37 = (bf16[512,512]{1,0:T(8,128)(2,1)S(1)}, bf16[512,512]{1,0:T(8,128)(2,1)S(1)}, u32[]{:S(2)}, u32[]{:S(2)}) collective-permute-start(bf16[512,512]{1,0:T(8,128)(2,1)S(1)} %get-tuple-element.61), channel_id=1, source_target_pairs={{0,7},{1,0},{2,1},{3,2},{4,3},{5,4},{6,5},{7,6},{8,15},{9,8},{10,9... | collective-permute-start | bytes 1572872 | tf_op jit(solution)/shard_map/ppermute | solution.py:32
  148.6 3.8 %collective-permute-start.36 = (f32[1,512]{1,0:T(1,128)S(1)}, f32[1,512]{1,0:T(1,128)S(1)}, u32[]{:S(2)}, u32[]{:S(2)}) collective-permute-start(f32[1,512]{1,0:T(1,128)S(1)} %slice.257), channel_id=1, source_target_pairs={{0,7},{1,0},{2,1},{3,2},{4,3},{5,4},{6,5},{7,6},{8,15},{9,8},{10,9... | collective-permute-start | bytes 6152 | tf_op jit(solution)/shard_map/ppermute | solution.py:32
  154.4 5.3 %collective-permute-done.36 = f32[1,512]{1,0:T(1,128)S(1)} collective-permute-done((f32[1,512]{1,0:T(1,128)S(1)}, f32[1,512]{1,0:T(1,128)S(1)}, u32[]{:S(2)}, u32[]{:S(2)}) %collective-permute-start.36) | collective-permute-done | bytes 2080 | tf_op jit(solution)/shard_map/ppermute | solution.py:32
  (103 shorter events, 41.1 us)
Async XLA Ops:
  1.5 8.1 %collective-permute-start = (f32[3,8,512]{2,1,0:T(8,128)S(1)}, f32[3,8,512]{2,1,0:T(8,128)S(1)}, u32[]{:S(2)}, u32[]{:S(2)}) collective-permute-start(f32[3,8,512]{2,1,0:T(8,128)S(1)} %get-tuple-element.79), channel_id=1, source_target_pairs={{0,1},{1,0},{2,3},{3,2},{4,5},{5,4},{6,7},{7,6},{8,9},{9,8},{10,11... | collective-permute-start | bytes 147464 | tf_op jit(solution)/shard_map/ppermute | solution.py:26
  7.0 15.7 %collective-permute-start.5 = (bf16[512,512]{1,0:T(8,128)(2,1)S(1)}, bf16[512,512]{1,0:T(8,128)(2,1)}, u32[]{:S(2)}, u32[]{:S(2)}) collective-permute-start(bf16[512,512]{1,0:T(8,128)(2,1)S(1)} %get-tuple-element.71), channel_id=1, source_target_pairs={{7,15},{15,23},{23,31},{31,39},{39,47},{47,55},{55,63},{71,79},{79... | collective-permute-start | bytes 1572872 | tf_op jit(solution)/shard_map/ppermute | solution.py:37
  10.4 7.3 %collective-permute-start.2 = (bf16[3,16,512]{2,1,0:T(8,128)(2,1)S(1)}, bf16[3,16,512]{2,1,0:T(8,128)(2,1)S(1)}, u32[]{:S(2)}, u32[]{:S(2)}) collective-permute-start(bf16[3,16,512]{2,1,0:T(8,128)(2,1)S(1)} %fusion.1), channel_id=1, source_target_pairs={{0,2},{1,3},{2,0},{3,1},{4,6},{5,7},{6,4},{7,5},{8,10},{9,11},{10,... | collective-permute-start | bytes 147464 | tf_op jit(solution)/shard_map/ppermute | solution.py:26
  12.7 6.9 %collective-permute-start.3 = (bf16[3,16,512]{2,1,0:T(8,128)(2,1)S(1)}, bf16[3,16,512]{2,1,0:T(8,128)(2,1)S(1)}, u32[]{:S(2)}, u32[]{:S(2)}) collective-permute-start(bf16[3,16,512]{2,1,0:T(8,128)(2,1)S(1)} %fusion.1), channel_id=1, source_target_pairs={{0,4},{1,5},{2,6},{3,7},{4,0},{5,1},{6,2},{7,3},{8,12},{9,13},{10,... | collective-permute-start | bytes 147464 | tf_op jit(solution)/shard_map/ppermute | solution.py:26
  22.7 23.0 %collective-permute-start.6 = (bf16[2,512,512]{2,1,0:T(8,128)(2,1)S(1)}, bf16[2,512,512]{2,1,0:T(8,128)(2,1)S(1)}, u32[]{:S(2)}, u32[]{:S(2)}) collective-permute-start(bf16[2,512,512]{2,1,0:T(8,128)(2,1)S(1)} %pad_maximum_fusion), channel_id=1, source_target_pairs={{0,1},{1,2},{2,3},{3,4},{4,5},{5,6},{6,7},{7,0},{8,9},{9,10},{10,1... | collective-permute-start | bytes 3145736 | tf_op jit(solution)/shard_map/ppermute | solution.py:32
  30.5 8.2 %collective-permute-start.10 = (bf16[2,4,3,16,512]{4,3,2,1,0:T(8,128)(2,1)S(1)}, bf16[2,4,3,16,512]{4,3,2,1,0:T(8,128)(2,1)S(1)}, u32[]{:S(2)}, u32[]{:S(2)}) collective-permute-start(bf16[2,4,3,16,512]{4,3,2,1,0:T(8,128)(2,1)S(1)} %pad_maximum_fusion.2.rest_0_), channel_id=1, source_target_pairs={{0,48},{1,49},{2,50},{3,51},{4,52},{5,53},{6,54},{7,55},{8,56},{9,... | collective-permute-start | bytes 1179656 | tf_op jit(solution)/shard_map/ppermute | solution.py:26
  31.6 17.6 %collective-permute-start.8 = (bf16[2,4,3,16,512]{4,3,2,1,0:T(8,128)(2,1)S(1)}, bf16[2,4,3,16,512]{4,3,2,1,0:T(8,128)(2,1)}, u32[]{:S(2)}, u32[]{:S(2)}) collective-permute-start(bf16[2,4,3,16,512]{4,3,2,1,0:T(8,128)(2,1)S(1)} %pad_maximum_fusion.2.rest_0_), channel_id=1, source_target_pairs={{0,16},{1,17},{2,18},{3,19},{4,20},{5,21},{6,22},{7,23},{8,24},{9,... | collective-permute-start | bytes 1179656 | tf_op jit(solution)/shard_map/ppermute | solution.py:26
  31.6 17.6 %collective-permute-start.9 = (bf16[2,4,3,16,512]{4,3,2,1,0:T(8,128)(2,1)S(1)}, bf16[2,4,3,16,512]{4,3,2,1,0:T(8,128)(2,1)}, u32[]{:S(2)}, u32[]{:S(2)}) collective-permute-start(bf16[2,4,3,16,512]{4,3,2,1,0:T(8,128)(2,1)S(1)} %pad_maximum_fusion.2.rest_0_), channel_id=1, source_target_pairs={{0,32},{1,33},{2,34},{3,35},{4,36},{5,37},{6,38},{7,39},{8,40},{9,... | collective-permute-start | bytes 1179656 | tf_op jit(solution)/shard_map/ppermute | solution.py:26
  39.5 19.7 %collective-permute-start.19 = (bf16[512,512]{1,0:T(8,128)(2,1)}, bf16[512,512]{1,0:T(8,128)(2,1)}, u32[]{:S(2)}, u32[]{:S(2)}) collective-permute-start(bf16[512,512]{1,0:T(8,128)(2,1)} %get-tuple-element.46), channel_id=1, source_target_pairs={{7,15},{15,23},{23,31},{31,39},{39,47},{47,55},{55,63},{71,79},{79... | collective-permute-start | bytes 1572872 | tf_op jit(solution)/shard_map/ppermute | solution.py:37
  45.7 13.5 %collective-permute-start.20 = (bf16[512,512]{1,0:T(8,128)(2,1)}, bf16[512,512]{1,0:T(8,128)(2,1)}, u32[]{:S(2)}, u32[]{:S(2)}) collective-permute-start(bf16[512,512]{1,0:T(8,128)(2,1)} %slice_select_fusion), channel_id=1, source_target_pairs={{0,1},{1,2},{2,3},{3,4},{4,5},{5,6},{6,7},{7,0},{8,9},{9,10},{10,1... | collective-permute-start | bytes 1572872 | tf_op jit(solution)/shard_map/ppermute | solution.py:32
  55.6 9.8 %collective-permute-start.11 = (bf16[4,3,16,512]{3,2,1,0:T(8,128)(2,1)S(1)}, bf16[4,3,16,512]{3,2,1,0:T(8,128)(2,1)S(1)}, u32[]{:S(2)}, u32[]{:S(2)}) collective-permute-start(bf16[4,3,16,512]{3,2,1,0:T(8,128)(2,1)S(1)} %get-tuple-element.38), channel_id=1, source_target_pairs={{0,8},{1,9},{2,10},{3,11},{4,12},{5,13},{6,14},{7,15},{8,0},{9,1},... | collective-permute-start | bytes 589832 | tf_op jit(solution)/shard_map/ppermute | solution.py:26
  56.8 9.2 %collective-permute-start.12 = (bf16[4,3,16,512]{3,2,1,0:T(8,128)(2,1)S(1)}, bf16[4,3,16,512]{3,2,1,0:T(8,128)(2,1)S(1)}, u32[]{:S(2)}, u32[]{:S(2)}) collective-permute-start(bf16[4,3,16,512]{3,2,1,0:T(8,128)(2,1)S(1)} %get-tuple-element.39), channel_id=1, source_target_pairs={{0,16},{1,17},{2,18},{3,19},{4,20},{5,21},{6,22},{7,23},{8,24},{9,... | collective-permute-start | bytes 589832 | tf_op jit(solution)/shard_map/ppermute | solution.py:26
  58.1 10.4 %collective-permute-start.13 = (bf16[4,3,16,512]{3,2,1,0:T(8,128)(2,1)S(1)}, bf16[4,3,16,512]{3,2,1,0:T(8,128)(2,1)S(1)}, u32[]{:S(2)}, u32[]{:S(2)}) collective-permute-start(bf16[4,3,16,512]{3,2,1,0:T(8,128)(2,1)S(1)} %get-tuple-element.40), channel_id=1, source_target_pairs={{0,24},{1,25},{2,26},{3,27},{4,28},{5,29},{6,30},{7,31},{8,16},{9,... | collective-permute-start | bytes 589832 | tf_op jit(solution)/shard_map/ppermute | solution.py:26
  60.6 24.3 %collective-permute-start.21 = (bf16[2,512,512]{2,1,0:T(8,128)(2,1)S(1)}, bf16[2,512,512]{2,1,0:T(8,128)(2,1)S(1)}, u32[]{:S(2)}, u32[]{:S(2)}) collective-permute-start(bf16[2,512,512]{2,1,0:T(8,128)(2,1)S(1)} %maximum_select_fusion), channel_id=1, source_target_pairs={{0,1},{1,2},{2,3},{3,4},{4,5},{5,6},{6,7},{7,0},{8,9},{9,10},{10,1... | collective-permute-start | bytes 3145736 | tf_op jit(solution)/shard_map/ppermute | solution.py:32
  61.9 8.9 %collective-permute-start.14 = (bf16[4,3,16,512]{3,2,1,0:T(8,128)(2,1)S(1)}, bf16[4,3,16,512]{3,2,1,0:T(8,128)(2,1)S(1)}, u32[]{:S(2)}, u32[]{:S(2)}) collective-permute-start(bf16[4,3,16,512]{3,2,1,0:T(8,128)(2,1)S(1)} %get-tuple-element.41), channel_id=1, source_target_pairs={{0,32},{1,33},{2,34},{3,35},{4,36},{5,37},{6,38},{7,39},{8,40},{9,... | collective-permute-start | bytes 589832 | tf_op jit(solution)/shard_map/ppermute | solution.py:26
  65.4 11.0 %collective-permute-start.15 = (bf16[4,3,16,512]{3,2,1,0:T(8,128)(2,1)S(1)}, bf16[4,3,16,512]{3,2,1,0:T(8,128)(2,1)S(1)}, u32[]{:S(2)}, u32[]{:S(2)}) collective-permute-start(bf16[4,3,16,512]{3,2,1,0:T(8,128)(2,1)S(1)} %get-tuple-element.42), channel_id=1, source_target_pairs={{0,40},{1,41},{2,42},{3,43},{4,44},{5,45},{6,46},{7,47},{8,32},{9,... | collective-permute-start | bytes 589832 | tf_op jit(solution)/shard_map/ppermute | solution.py:26
  66.0 13.8 %collective-permute-start.16 = (bf16[4,3,16,512]{3,2,1,0:T(8,128)(2,1)S(1)}, bf16[4,3,16,512]{3,2,1,0:T(8,128)(2,1)S(1)}, u32[]{:S(2)}, u32[]{:S(2)}) collective-permute-start(bf16[4,3,16,512]{3,2,1,0:T(8,128)(2,1)S(1)} %get-tuple-element.43), channel_id=1, source_target_pairs={{0,48},{1,49},{2,50},{3,51},{4,52},{5,53},{6,54},{7,55},{8,56},{9,... | collective-permute-start | bytes 589832 | tf_op jit(solution)/shard_map/ppermute | solution.py:26
  68.5 15.5 %collective-permute-start.17 = (bf16[4,3,16,512]{3,2,1,0:T(8,128)(2,1)S(1)}, bf16[4,3,16,512]{3,2,1,0:T(8,128)(2,1)S(1)}, u32[]{:S(2)}, u32[]{:S(2)}) collective-permute-start(bf16[4,3,16,512]{3,2,1,0:T(8,128)(2,1)S(1)} %get-tuple-element.44), channel_id=1, source_target_pairs={{0,56},{1,57},{2,58},{3,59},{4,60},{5,61},{6,62},{7,63},{8,48},{9,... | collective-permute-start | bytes 589832 | tf_op jit(solution)/shard_map/ppermute | solution.py:26
  84.1 19.5 %collective-permute-start.18 = (bf16[2,512,512]{2,1,0:T(8,128)(2,1)S(1)}, bf16[2,512,512]{2,1,0:T(8,128)(2,1)S(1)}, u32[]{:S(2)}, u32[]{:S(2)}) collective-permute-start(bf16[2,512,512]{2,1,0:T(8,128)(2,1)S(1)} %copy-done.6), channel_id=1, source_target_pairs={{7,15},{15,23},{23,31},{31,39},{39,47},{47,55},{55,63},{71,79},{79... | collective-permute-start | bytes 3145736 | tf_op jit(solution)/shard_map/ppermute | solution.py:37
  84.9 5.7 %collective-permute-start.22 = (bf16[3,16,512]{2,1,0:T(8,128)(2,1)S(1)}, bf16[3,16,512]{2,1,0:T(8,128)(2,1)S(1)}, u32[]{:S(2)}, u32[]{:S(2)}) collective-permute-start(bf16[3,16,512]{2,1,0:T(8,128)(2,1)S(1)} %get-tuple-element.51), channel_id=1, source_target_pairs={{0,2},{1,3},{2,0},{3,1},{4,6},{5,7},{6,4},{7,5},{8,10},{9,11},{10,... | collective-permute-start | bytes 147464 | tf_op jit(solution)/shard_map/ppermute | solution.py:26
  85.1 6.9 %collective-permute-start.23 = (bf16[3,16,512]{2,1,0:T(8,128)(2,1)S(1)}, bf16[3,16,512]{2,1,0:T(8,128)(2,1)S(1)}, u32[]{:S(2)}, u32[]{:S(2)}) collective-permute-start(bf16[3,16,512]{2,1,0:T(8,128)(2,1)S(1)} %fusion.3), channel_id=1, source_target_pairs={{0,4},{1,5},{2,6},{3,7},{4,0},{5,1},{6,2},{7,3},{8,12},{9,13},{10,... | collective-permute-start | bytes 147464 | tf_op jit(solution)/shard_map/ppermute | solution.py:26
  96.2 6.9 %collective-permute-start.26 = (bf16[3,16,512]{2,1,0:T(8,128)(2,1)S(1)}, bf16[3,16,512]{2,1,0:T(8,128)(2,1)S(1)}, u32[]{:S(2)}, u32[]{:S(2)}) collective-permute-start(bf16[3,16,512]{2,1,0:T(8,128)(2,1)S(1)} %get-tuple-element.64), channel_id=1, source_target_pairs={{0,4},{1,5},{2,6},{3,7},{4,0},{5,1},{6,2},{7,3},{8,12},{9,13},{10,... | collective-permute-start | bytes 147464 | tf_op jit(solution)/shard_map/ppermute | solution.py:26
  105.6 46.8 %collective-permute-start.28 = (bf16[2,512,512]{2,1,0:T(8,128)(2,1)S(1)}, bf16[2,512,512]{2,1,0:T(8,128)(2,1)S(1)}, u32[]{:S(2)}, u32[]{:S(2)}) collective-permute-start(bf16[2,512,512]{2,1,0:T(8,128)(2,1)S(1)} %collective-permute-done.18), channel_id=1, source_target_pairs={{7,0},{15,8},{23,16},{31,24},{39,32},{47,40},{55,48},{63,56},{71,6... | collective-permute-start | bytes 3145736 | tf_op jit(solution)/shard_map/ppermute | solution.py:42
  109.0 7.7 %collective-permute-start.30 = (bf16[2,4,3,16,512]{4,3,2,1,0:T(8,128)(2,1)S(1)}, bf16[2,4,3,16,512]{4,3,2,1,0:T(8,128)(2,1)S(1)}, u32[]{:S(2)}, u32[]{:S(2)}) collective-permute-start(bf16[2,4,3,16,512]{4,3,2,1,0:T(8,128)(2,1)S(1)} %pad_maximum_fusion.3.rest_0_), channel_id=1, source_target_pairs={{0,16},{1,17},{2,18},{3,19},{4,20},{5,21},{6,22},{7,23},{8,24},{9,... | collective-permute-start | bytes 1179656 | tf_op jit(solution)/shard_map/ppermute | solution.py:26
  111.5 13.5 %collective-permute-start.31 = (bf16[2,4,3,16,512]{4,3,2,1,0:T(8,128)(2,1)S(1)}, bf16[2,4,3,16,512]{4,3,2,1,0:T(8,128)(2,1)S(1)}, u32[]{:S(2)}, u32[]{:S(2)}) collective-permute-start(bf16[2,4,3,16,512]{4,3,2,1,0:T(8,128)(2,1)S(1)} %pad_maximum_fusion.3.rest_0_), channel_id=1, source_target_pairs={{0,32},{1,33},{2,34},{3,35},{4,36},{5,37},{6,38},{7,39},{8,40},{9,... | collective-permute-start | bytes 1179656 | tf_op jit(solution)/shard_map/ppermute | solution.py:26
  114.4 12.9 %collective-permute-start.32 = (bf16[2,4,3,16,512]{4,3,2,1,0:T(8,128)(2,1)S(1)}, bf16[2,4,3,16,512]{4,3,2,1,0:T(8,128)(2,1)S(1)}, u32[]{:S(2)}, u32[]{:S(2)}) collective-permute-start(bf16[2,4,3,16,512]{4,3,2,1,0:T(8,128)(2,1)S(1)} %pad_maximum_fusion.3.rest_0_), channel_id=1, source_target_pairs={{0,48},{1,49},{2,50},{3,51},{4,52},{5,53},{6,54},{7,55},{8,56},{9,... | collective-permute-start | bytes 1179656 | tf_op jit(solution)/shard_map/ppermute | solution.py:26
  130.9 17.6 %collective-permute-start.33 = (f32[2,512]{1,0:T(2,128)S(1)}, f32[2,512]{1,0:T(2,128)S(1)}, u32[]{:S(2)}, u32[]{:S(2)}) collective-permute-start(f32[2,512]{1,0:T(2,128)S(1)} %get-tuple-element.57), channel_id=1, source_target_pairs={{0,64},{64,0},{128,192},{192,128},{1,65},{65,1},{129,193},{193,129... | collective-permute-start | bytes 12296 | tf_op jit(solution)/shard_map/ppermute | solution.py:339
  139.2 9.4 %collective-permute-start.34 = (f32[2,512]{1,0:T(2,128)S(1)}, f32[2,512]{1,0:T(2,128)S(1)}, u32[]{:S(2)}, u32[]{:S(2)}) collective-permute-start(f32[2,512]{1,0:T(2,128)S(1)} %get-tuple-element.57), channel_id=1, source_target_pairs={{0,128},{64,192},{128,0},{192,64},{1,129},{65,193},{129,1},{193,65... | collective-permute-start | bytes 12296 | tf_op jit(solution)/shard_map/ppermute | solution.py:339
  142.1 6.4 %collective-permute-start.35 = (f32[2,512]{1,0:T(2,128)S(1)}, f32[2,512]{1,0:T(2,128)S(1)}, u32[]{:S(2)}, u32[]{:S(2)}) collective-permute-start(f32[2,512]{1,0:T(2,128)S(1)} %get-tuple-element.57), channel_id=1, source_target_pairs={{0,192},{64,128},{128,64},{192,0},{1,193},{65,129},{129,65},{193,1... | collective-permute-start | bytes 12296 | tf_op jit(solution)/shard_map/ppermute | solution.py:339
  142.4 17.3 %collective-permute-start.37 = (bf16[512,512]{1,0:T(8,128)(2,1)S(1)}, bf16[512,512]{1,0:T(8,128)(2,1)S(1)}, u32[]{:S(2)}, u32[]{:S(2)}) collective-permute-start(bf16[512,512]{1,0:T(8,128)(2,1)S(1)} %get-tuple-element.61), channel_id=1, source_target_pairs={{0,7},{1,0},{2,1},{3,2},{4,3},{5,4},{6,5},{7,6},{8,15},{9,8},{10,9... | collective-permute-start | bytes 1572872 | tf_op jit(solution)/shard_map/ppermute | solution.py:32
  148.5 11.2 %collective-permute-start.38 = (f32[3,8,512]{2,1,0:T(8,128)S(1)}, f32[3,8,512]{2,1,0:T(8,128)S(1)}, u32[]{:S(2)}, u32[]{:S(2)}) collective-permute-start(f32[3,8,512]{2,1,0:T(8,128)S(1)} %get-tuple-element.78), channel_id=1, source_target_pairs={{0,1},{1,0},{2,3},{3,2},{4,5},{5,4},{6,7},{7,6},{8,9},{9,8},{10,11... | collective-permute-start | bytes 147464 | tf_op jit(solution)/shard_map/ppermute | solution.py:26
  148.6 11.0 %collective-permute-start.36 = (f32[1,512]{1,0:T(1,128)S(1)}, f32[1,512]{1,0:T(1,128)S(1)}, u32[]{:S(2)}, u32[]{:S(2)}) collective-permute-start(f32[1,512]{1,0:T(1,128)S(1)} %slice.257), channel_id=1, source_target_pairs={{0,7},{1,0},{2,1},{3,2},{4,3},{5,4},{6,5},{7,6},{8,15},{9,8},{10,9... | collective-permute-start | bytes 6152 | tf_op jit(solution)/shard_map/ppermute | solution.py:32
  (19 other events, 208.8 us)

commit v6 on v5

--- a/solution.py
+++ b/solution.py
@@ -334,11 +334,12 @@
     )
     f_back = ring(f_prev, -1)
     heads = lax.axis_size("head")
+    attn_own = attend(0, [halo, after(closing, sq)])
+    sq = after(sq, attn_own)
     totals = sq
     for k in range(1, heads):
         totals = totals + lax.ppermute(sq, "head", [(i, i ^ k) for i in range(heads)])
-    attn_own = attend(0, [halo, after(closing, totals)])
-    sums = totals[1:2] + after(ring(totals[0:1], -1), attn_own)
+    sums = totals[1:2] + ring(after(totals[0:1], f_back), -1)
     new_mine = jnp.where(even, new[:, :8], new[:, 8:])
     new_theirs = after(move_xor(jnp.where(even, new[:, 8:], new[:, :8]), 1), f_back)
     new_all = jnp.where(

time: 162 us -> 161 us (level)
  starting transfers between devices: 76.3 us -> 73.6 us
    ppermute x3, waiting for transfers between devices: 0.01 us -> 3.76 us  [local(): lax.ppermute(sq, 'head', [(i, i ^ k) for i in range(heads)])]
    ppermute x6, waiting for transfers between devices: 10.9 us -> 7.4 us  [ring(): return lax.ppermute(value, 'seq', pairs)]
  transfers between devices with their start and end apart: 39 -> 39, of which waited for: 19 -> 21; matrix products, arithmetic and copies ran while one was open for 5% -> 6% of each run, Pallas kernels for 8% -> 8%
where the time goes in v6:
time: 161 us; the launch traced here: 160 us
  starting transfers between devices  73.6 us (46%)
  waiting for transfers between devices  59.6 us (37%)
  Pallas kernels  13.6 us (8%)
  other arithmetic  10.8 us (7%)
  local copies, waits for them, and re-layouts  1.74 us (1%)
    ppermute x26, waiting for transfers between devices, move_xor(): return lax.ppermute(value, 'seq', [(i, i ^ mask) for i in range(n)])  48.4 us
    ppermute x26, starting transfers between devices, move_xor(): return lax.ppermute(value, 'seq', [(i, i ^ mask) for i in range(n)])  43.8 us
    ppermute x6, starting transfers between devices, ring(): return lax.ppermute(value, 'seq', pairs)  14.8 us
    pallas_call x4, Pallas kernels, call(): pl.pallas_call(kernel, out_shape=outs, grid_spec=pltpu.PrefetchScalarGrid...  13.6 us
    ppermute x3, starting transfers between devices, local(): lax.ppermute(sq, 'head', [(i, i ^ k) for i in range(heads)])  10.1 us
    ppermute x6, waiting for transfers between devices, ring(): return lax.ppermute(value, 'seq', pairs)  7.4 us
    ppermute x3, waiting for transfers between devices, local(): lax.ppermute(sq, 'head', [(i, i ^ k) for i in range(heads)])  3.76 us
    ppermute x3, starting transfers between devices, to_next_plane(): lax.ppermute(value, 'seq', [(i, i + RING) for i in range(RING - 1, n - RI...  3.65 us
  transfers between devices with their start and end apart: 39, of which 21 were waited for; matrix products, arithmetic and copies ran while one was open for 6% of the time, Pallas kernels for 8%

profile of v6, /device:TPU:1, one launch (start us, length us, event | category | flops | bytes accessed | tf_op | source)
XLA Modules:
  0.0 160.3 jit_solution(10235257605957850609)
XLA Ops:
  1.5 2.6 %collective-permute-start = (f32[3,8,512]{2,1,0:T(8,128)S(1)}, f32[3,8,512]{2,1,0:T(8,128)S(1)}, u32[]{:S(2)}, u32[]{:S(2)}) collective-permute-start(f32[3,8,512]{2,1,0:T(8,128)S(1)} %get-tuple-element.81), channel_id=1, source_target_pairs={{0,1},{1,0},{2,3},{3,2},{4,5},{5,4},{6,7},{7,6},{8,9},{9,8},{10,11... | collective-permute-start | bytes 147464 | tf_op jit(solution)/shard_map/ppermute | solution.py:26
  4.8 2.2 %fusion.9 = (bf16[512,512]{1,0:T(8,128)(2,1)S(1)}, bf16[1,512,512]{2,1,0:T(8,128)(2,1)}, bf16[1,512,512]{2,1,0:T(8,128)(2,1)S(1)}) fusion(bf16[512,1024]{1,0:T(8,128)(2,1)} %k_ref.3, pred[]{:T(512)S(6)} %eq.6, pred[]{:T(512)S(6)} %not.2), kind=kLoop, calls=%fused_computation.43 | loop fusion | flops 524288 | bytes 2621442 | tf_op jit(solution)/shard_map/slice | solution.py:249
  10.4 2.3 %collective-permute-start.2 = (bf16[3,16,512]{2,1,0:T(8,128)(2,1)S(1)}, bf16[3,16,512]{2,1,0:T(8,128)(2,1)S(1)}, u32[]{:S(2)}, u32[]{:S(2)}) collective-permute-start(bf16[3,16,512]{2,1,0:T(8,128)(2,1)S(1)} %fusion.1), channel_id=1, source_target_pairs={{0,2},{1,3},{2,0},{3,1},{4,6},{5,7},{6,4},{7,5},{8,10},{9,11},{10,... | collective-permute-start | bytes 147464 | tf_op jit(solution)/shard_map/ppermute | solution.py:26
  12.7 4.9 %collective-permute-start.3 = (bf16[3,16,512]{2,1,0:T(8,128)(2,1)S(1)}, bf16[3,16,512]{2,1,0:T(8,128)(2,1)S(1)}, u32[]{:S(2)}, u32[]{:S(2)}) collective-permute-start(bf16[3,16,512]{2,1,0:T(8,128)(2,1)S(1)} %fusion.1), channel_id=1, source_target_pairs={{0,4},{1,5},{2,6},{3,7},{4,0},{5,1},{6,2},{7,3},{8,12},{9,13},{10,... | collective-permute-start | bytes 147464 | tf_op jit(solution)/shard_map/ppermute | solution.py:26
  19.6 3.1 %collective-permute-done.4 = bf16[3,16,512]{2,1,0:T(8,128)(2,1)S(1)} collective-permute-done((bf16[3,16,512]{2,1,0:T(8,128)(2,1)S(1)}, bf16[3,16,512]{2,1,0:T(8,128)(2,1)S(1)}, u32[]{:S(2)}, u32[]{:S(2)}) %collective-permute-start.4) | collective-permute-done | bytes 49184 | tf_op jit(solution)/shard_map/ppermute | solution.py:26
  22.7 2.9 %collective-permute-start.6 = (bf16[2,512,512]{2,1,0:T(8,128)(2,1)S(1)}, bf16[2,512,512]{2,1,0:T(8,128)(2,1)S(1)}, u32[]{:S(2)}, u32[]{:S(2)}) collective-permute-start(bf16[2,512,512]{2,1,0:T(8,128)(2,1)S(1)} %pad_maximum_fusion), channel_id=1, source_target_pairs={{0,1},{1,2},{2,3},{3,4},{4,5},{5,6},{6,7},{7,0},{8,9},{9,10},{10,1... | collective-permute-start | bytes 3145736 | tf_op jit(solution)/shard_map/ppermute | solution.py:32
  25.8 4.7 %collective-permute-done.7 = bf16[4,3,16,512]{3,2,1,0:T(8,128)(2,1)S(1)} collective-permute-done((bf16[4,3,16,512]{3,2,1,0:T(8,128)(2,1)S(1)}, bf16[4,3,16,512]{3,2,1,0:T(8,128)(2,1)S(1)}, u32[]{:S(2)}, u32[]{:S(2)}) %collective-permute-start.7) | collective-permute-done | bytes 196640 | tf_op jit(solution)/shard_map/ppermute | solution.py:26
  31.6 2.8 %collective-permute-start.9 = (bf16[2,4,3,16,512]{4,3,2,1,0:T(8,128)(2,1)S(1)}, bf16[2,4,3,16,512]{4,3,2,1,0:T(8,128)(2,1)}, u32[]{:S(2)}, u32[]{:S(2)}) collective-permute-start(bf16[2,4,3,16,512]{4,3,2,1,0:T(8,128)(2,1)S(1)} %pad_maximum_fusion.2.rest_0_), channel_id=1, source_target_pairs={{0,32},{1,33},{2,34},{3,35},{4,36},{5,37},{6,38},{7,39},{8,40},{9,... | collective-permute-start | bytes 1179656 | tf_op jit(solution)/shard_map/ppermute | solution.py:26
  35.3 3.4 %collective-permute-done.10.rest_3_ = bf16[2,4,3,16,512]{4,3,2,1,0:T(8,128)(2,1)S(1)} collective-permute-done((bf16[2,4,3,16,512]{4,3,2,1,0:T(8,128)(2,1)S(1)}, bf16[2,4,3,16,512]{4,3,2,1,0:T(8,128)(2,1)S(1)}, u32[]{:S(2)}, u32[]{:S(2)}) %collective-permute-start.10) | collective-permute-done | bytes 393248 | tf_op jit(solution)/shard_map/ppermute | solution.py:26
  40.9 4.8 %collective-permute-done.6.halo = bf16[2,512,512]{2,1,0:T(8,128)(2,1)S(1)} collective-permute-done((bf16[2,512,512]{2,1,0:T(8,128)(2,1)S(1)}, bf16[2,512,512]{2,1,0:T(8,128)(2,1)S(1)}, u32[]{:S(2)}, u32[]{:S(2)}) %collective-permute-start.6) | collective-permute-done | bytes 1048608 | tf_op jit(solution)/shard_map/ppermute | solution.py:32
  45.7 2.0 %collective-permute-start.20 = (bf16[512,512]{1,0:T(8,128)(2,1)}, bf16[512,512]{1,0:T(8,128)(2,1)}, u32[]{:S(2)}, u32[]{:S(2)}) collective-permute-start(bf16[512,512]{1,0:T(8,128)(2,1)} %slice_select_fusion), channel_id=1, source_target_pairs={{0,1},{1,2},{2,3},{3,4},{4,5},{5,6},{6,7},{7,0},{8,9},{9,10},{10,1... | collective-permute-start | bytes 1572872 | tf_op jit(solution)/shard_map/ppermute | solution.py:32
  49.4 6.1 %shard_map.111 = (f32[4,3,16,512]{3,2,1,0:T(8,128)S(1)}, bf16[4,3,16,512]{3,2,1,0:T(8,128)(2,1)S(1)}, bf16[4,3,16,512]{3,2,1,0:T(8,128)(2,1)S(1)}, bf16[4,3,16,5...) custom-call(s32[16]{0:T(128)S(1)} %stack.168.s_ref, ...), custom_call_target="tpu_custom_call" | custom-call | flops 3221225472 | bytes 4722688 | tf_op jit(solution)/shard_map/pallas_call | solution.py:78
  61.9 3.5 %collective-permute-start.14 = (bf16[4,3,16,512]{3,2,1,0:T(8,128)(2,1)S(1)}, bf16[4,3,16,512]{3,2,1,0:T(8,128)(2,1)S(1)}, u32[]{:S(2)}, u32[]{:S(2)}) collective-permute-start(bf16[4,3,16,512]{3,2,1,0:T(8,128)(2,1)S(1)} %get-tuple-element.42), channel_id=1, source_target_pairs={{0,32},{1,33},{2,34},{3,35},{4,36},{5,37},{6,38},{7,39},{8,40},{9,... | collective-permute-start | bytes 589832 | tf_op jit(solution)/shard_map/ppermute | solution.py:26
  66.0 2.5 %collective-permute-start.16 = (bf16[4,3,16,512]{3,2,1,0:T(8,128)(2,1)S(1)}, bf16[4,3,16,512]{3,2,1,0:T(8,128)(2,1)S(1)}, u32[]{:S(2)}, u32[]{:S(2)}) collective-permute-start(bf16[4,3,16,512]{3,2,1,0:T(8,128)(2,1)S(1)} %get-tuple-element.44), channel_id=1, source_target_pairs={{0,48},{1,49},{2,50},{3,51},{4,52},{5,53},{6,54},{7,55},{8,56},{9,... | collective-permute-start | bytes 589832 | tf_op jit(solution)/shard_map/ppermute | solution.py:26
  70.8 5.7 %collective-permute-done.15 = bf16[4,3,16,512]{3,2,1,0:T(8,128)(2,1)S(1)} collective-permute-done((bf16[4,3,16,512]{3,2,1,0:T(8,128)(2,1)S(1)}, bf16[4,3,16,512]{3,2,1,0:T(8,128)(2,1)S(1)}, u32[]{:S(2)}, u32[]{:S(2)}) %collective-permute-start.15) | collective-permute-done | bytes 196640 | tf_op jit(solution)/shard_map/ppermute | solution.py:26
  76.5 3.3 %collective-permute-done.16 = bf16[4,3,16,512]{3,2,1,0:T(8,128)(2,1)S(1)} collective-permute-done((bf16[4,3,16,512]{3,2,1,0:T(8,128)(2,1)S(1)}, bf16[4,3,16,512]{3,2,1,0:T(8,128)(2,1)S(1)}, u32[]{:S(2)}, u32[]{:S(2)}) %collective-permute-start.16) | collective-permute-done | bytes 196640 | tf_op jit(solution)/shard_map/ppermute | solution.py:26
  79.8 4.2 %collective-permute-done.17 = bf16[4,3,16,512]{3,2,1,0:T(8,128)(2,1)S(1)} collective-permute-done((bf16[4,3,16,512]{3,2,1,0:T(8,128)(2,1)S(1)}, bf16[4,3,16,512]{3,2,1,0:T(8,128)(2,1)S(1)}, u32[]{:S(2)}, u32[]{:S(2)}) %collective-permute-start.17) | collective-permute-done | bytes 196640 | tf_op jit(solution)/shard_map/ppermute | solution.py:26
  85.1 3.9 %collective-permute-start.23 = (bf16[3,16,512]{2,1,0:T(8,128)(2,1)S(1)}, bf16[3,16,512]{2,1,0:T(8,128)(2,1)S(1)}, u32[]{:S(2)}, u32[]{:S(2)}) collective-permute-start(bf16[3,16,512]{2,1,0:T(8,128)(2,1)S(1)} %fusion.3), channel_id=1, source_target_pairs={{0,4},{1,5},{2,6},{3,7},{4,0},{5,1},{6,2},{7,3},{8,12},{9,13},{10,... | collective-permute-start | bytes 147464 | tf_op jit(solution)/shard_map/ppermute | solution.py:26
  92.0 2.0 %collective-permute-done.24 = bf16[3,16,512]{2,1,0:T(8,128)(2,1)S(1)} collective-permute-done((bf16[3,16,512]{2,1,0:T(8,128)(2,1)S(1)}, bf16[3,16,512]{2,1,0:T(8,128)(2,1)S(1)}, u32[]{:S(2)}, u32[]{:S(2)}) %collective-permute-start.24) | collective-permute-done | bytes 49184 | tf_op jit(solution)/shard_map/ppermute | solution.py:26
  94.2 2.1 %collective-permute-start.25 = (bf16[3,16,512]{2,1,0:T(8,128)(2,1)S(1)}, bf16[3,16,512]{2,1,0:T(8,128)(2,1)S(1)}, u32[]{:S(2)}, u32[]{:S(2)}) collective-permute-start(bf16[3,16,512]{2,1,0:T(8,128)(2,1)S(1)} %get-tuple-element.66), channel_id=1, source_target_pairs={{0,2},{1,3},{2,0},{3,1},{4,6},{5,7},{6,4},{7,5},{8,10},{9,11},{10,... | collective-permute-start | bytes 147464 | tf_op jit(solution)/shard_map/ppermute | solution.py:26
  99.9 3.2 %collective-permute-done.26 = bf16[3,16,512]{2,1,0:T(8,128)(2,1)S(1)} collective-permute-done((bf16[3,16,512]{2,1,0:T(8,128)(2,1)S(1)}, bf16[3,16,512]{2,1,0:T(8,128)(2,1)S(1)}, u32[]{:S(2)}, u32[]{:S(2)}) %collective-permute-start.26) | collective-permute-done | bytes 49184 | tf_op jit(solution)/shard_map/ppermute | solution.py:26
  104.9 2.0 %collective-permute-start.29 = (bf16[4,3,16,512]{3,2,1,0:T(8,128)(2,1)S(1)}, bf16[4,3,16,512]{3,2,1,0:T(8,128)(2,1)S(1)}, u32[]{:S(2)}, u32[]{:S(2)}) collective-permute-start(bf16[4,3,16,512]{3,2,1,0:T(8,128)(2,1)S(1)} %pad_maximum_fusion.5), channel_id=1, source_target_pairs={{0,8},{1,9},{2,10},{3,11},{4,12},{5,13},{6,14},{7,15},{8,0},{9,1},... | collective-permute-start | bytes 589832 | tf_op jit(solution)/shard_map/ppermute | solution.py:26
  106.9 3.1 %collective-permute-done.29 = bf16[4,3,16,512]{3,2,1,0:T(8,128)(2,1)S(1)} collective-permute-done((bf16[4,3,16,512]{3,2,1,0:T(8,128)(2,1)S(1)}, bf16[4,3,16,512]{3,2,1,0:T(8,128)(2,1)S(1)}, u32[]{:S(2)}, u32[]{:S(2)}) %collective-permute-start.29) | collective-permute-done | bytes 196640 | tf_op jit(solution)/shard_map/ppermute | solution.py:26
  110.0 2.5 %collective-permute-start.30 = (bf16[2,4,3,16,512]{4,3,2,1,0:T(8,128)(2,1)S(1)}, bf16[2,4,3,16,512]{4,3,2,1,0:T(8,128)(2,1)S(1)}, u32[]{:S(2)}, u32[]{:S(2)}) collective-permute-start(bf16[2,4,3,16,512]{4,3,2,1,0:T(8,128)(2,1)S(1)} %pad_maximum_fusion.3.rest_0_), channel_id=1, source_target_pairs={{0,16},{1,17},{2,18},{3,19},{4,20},{5,21},{6,22},{7,23},{8,24},{9,... | collective-permute-start | bytes 1179656 | tf_op jit(solution)/shard_map/ppermute | solution.py:26
  112.5 2.9 %collective-permute-start.31 = (bf16[2,4,3,16,512]{4,3,2,1,0:T(8,128)(2,1)S(1)}, bf16[2,4,3,16,512]{4,3,2,1,0:T(8,128)(2,1)S(1)}, u32[]{:S(2)}, u32[]{:S(2)}) collective-permute-start(bf16[2,4,3,16,512]{4,3,2,1,0:T(8,128)(2,1)S(1)} %pad_maximum_fusion.3.rest_0_), channel_id=1, source_target_pairs={{0,32},{1,33},{2,34},{3,35},{4,36},{5,37},{6,38},{7,39},{8,40},{9,... | collective-permute-start | bytes 1179656 | tf_op jit(solution)/shard_map/ppermute | solution.py:26
  118.0 7.7 %collective-permute-done.31.rest_2_ = bf16[2,4,3,16,512]{4,3,2,1,0:T(8,128)(2,1)S(1)} collective-permute-done((bf16[2,4,3,16,512]{4,3,2,1,0:T(8,128)(2,1)S(1)}, bf16[2,4,3,16,512]{4,3,2,1,0:T(8,128)(2,1)S(1)}, u32[]{:S(2)}, u32[]{:S(2)}) %collective-permute-start.31) | collective-permute-done | bytes 393248 | tf_op jit(solution)/shard_map/ppermute | solution.py:26
  125.7 2.3 %collective-permute-done.32.rest_3_ = bf16[2,4,3,16,512]{4,3,2,1,0:T(8,128)(2,1)S(1)} collective-permute-done((bf16[2,4,3,16,512]{4,3,2,1,0:T(8,128)(2,1)S(1)}, bf16[2,4,3,16,512]{4,3,2,1,0:T(8,128)(2,1)S(1)}, u32[]{:S(2)}, u32[]{:S(2)}) %collective-permute-start.32) | collective-permute-done | bytes 393248 | tf_op jit(solution)/shard_map/ppermute | solution.py:26
  128.0 3.6 %shard_map.113 = (bf16[512,512]{1,0:T(8,128)(2,1)S(1)}, bf16[512,512]{1,0:T(8,128)(2,1)S(1)}, f32[2,512]{1,0:T(2,128)S(1)}, f32[3,16,512]{2,1,0:T(8,128)S(1)}) custom-call(s32[16]{0:T(128)S(1)} %stack.168.s_ref, bf16[512,512]{1,0:T(8,128)(2,1)} %collective-permute-done.20.q_prev, bf16[512,1024]{1,0:T(8,128)(2,1)S(1)} %copy-done.2, ...), custom_call_target="tpu_custom_call" | custom-call | flops 1610612736 | bytes 3250176 | tf_op jit(solution)/shard_map/pallas_call | solution.py:78
  131.6 8.5 %collective-permute-start.36 = (bf16[512,512]{1,0:T(8,128)(2,1)S(1)}, bf16[512,512]{1,0:T(8,128)(2,1)S(1)}, u32[]{:S(2)}, u32[]{:S(2)}) collective-permute-start(bf16[512,512]{1,0:T(8,128)(2,1)S(1)} %get-tuple-element.62), channel_id=1, source_target_pairs={{0,7},{1,0},{2,1},{3,2},{4,3},{5,4},{6,5},{7,6},{8,15},{9,8},{10,9... | collective-permute-start | bytes 1572872 | tf_op jit(solution)/shard_map/ppermute | solution.py:32
  142.1 6.9 %collective-permute-start.33 = (f32[2,512]{1,0:T(2,128)S(1)}, f32[2,512]{1,0:T(2,128)S(1)}, u32[]{:S(2)}, u32[]{:S(2)}) collective-permute-start(f32[2,512]{1,0:T(2,128)S(1)} %get-tuple-element.61), channel_id=1, source_target_pairs={{0,64},{64,0},{128,192},{192,128},{1,65},{65,1},{129,193},{193,129... | collective-permute-start | bytes 12296 | tf_op jit(solution)/shard_map/ppermute | solution.py:341
  149.0 2.6 %collective-permute-start.34 = (f32[2,512]{1,0:T(2,128)S(1)}, f32[2,512]{1,0:T(2,128)S(1)}, u32[]{:S(2)}, u32[]{:S(2)}) collective-permute-start(f32[2,512]{1,0:T(2,128)S(1)} %get-tuple-element.61), channel_id=1, source_target_pairs={{0,128},{64,192},{128,0},{192,64},{1,129},{65,193},{129,1},{193,65... | collective-permute-start | bytes 12296 | tf_op jit(solution)/shard_map/ppermute | solution.py:341
  153.0 3.1 %collective-permute-done.35 = f32[2,512]{1,0:T(2,128)S(1)} collective-permute-done((f32[2,512]{1,0:T(2,128)S(1)}, f32[2,512]{1,0:T(2,128)S(1)}, u32[]{:S(2)}, u32[]{:S(2)}) %collective-permute-start.35) | collective-permute-done | bytes 4128 | tf_op jit(solution)/shard_map/ppermute | solution.py:341
  (103 shorter events, 42.2 us)
Async XLA Ops:
  1.5 8.1 %collective-permute-start = (f32[3,8,512]{2,1,0:T(8,128)S(1)}, f32[3,8,512]{2,1,0:T(8,128)S(1)}, u32[]{:S(2)}, u32[]{:S(2)}) collective-permute-start(f32[3,8,512]{2,1,0:T(8,128)S(1)} %get-tuple-element.81), channel_id=1, source_target_pairs={{0,1},{1,0},{2,3},{3,2},{4,5},{5,4},{6,7},{7,6},{8,9},{9,8},{10,11... | collective-permute-start | bytes 147464 | tf_op jit(solution)/shard_map/ppermute | solution.py:26
  4.8 5.6 %collective-permute-start.1 = (f32[1,512]{1,0:T(1,128)S(1)}, f32[1,512]{1,0:T(1,128)S(1)}, u32[]{:S(2)}, u32[]{:S(2)}) collective-permute-start(f32[1,512]{1,0:T(1,128)S(1)} %get-tuple-element.88), channel_id=1, source_target_pairs={{0,1},{1,2},{2,3},{3,4},{4,5},{5,6},{6,7},{7,0},{8,9},{9,10},{10,1... | collective-permute-start | bytes 6152 | tf_op jit(solution)/shard_map/ppermute | solution.py:32
  7.0 15.7 %collective-permute-start.5 = (bf16[512,512]{1,0:T(8,128)(2,1)S(1)}, bf16[512,512]{1,0:T(8,128)(2,1)}, u32[]{:S(2)}, u32[]{:S(2)}) collective-permute-start(bf16[512,512]{1,0:T(8,128)(2,1)S(1)} %get-tuple-element.73), channel_id=1, source_target_pairs={{7,15},{15,23},{23,31},{31,39},{39,47},{47,55},{55,63},{71,79},{79... | collective-permute-start | bytes 1572872 | tf_op jit(solution)/shard_map/ppermute | solution.py:37
  10.4 7.3 %collective-permute-start.2 = (bf16[3,16,512]{2,1,0:T(8,128)(2,1)S(1)}, bf16[3,16,512]{2,1,0:T(8,128)(2,1)S(1)}, u32[]{:S(2)}, u32[]{:S(2)}) collective-permute-start(bf16[3,16,512]{2,1,0:T(8,128)(2,1)S(1)} %fusion.1), channel_id=1, source_target_pairs={{0,2},{1,3},{2,0},{3,1},{4,6},{5,7},{6,4},{7,5},{8,10},{9,11},{10,... | collective-permute-start | bytes 147464 | tf_op jit(solution)/shard_map/ppermute | solution.py:26
  12.7 6.9 %collective-permute-start.3 = (bf16[3,16,512]{2,1,0:T(8,128)(2,1)S(1)}, bf16[3,16,512]{2,1,0:T(8,128)(2,1)S(1)}, u32[]{:S(2)}, u32[]{:S(2)}) collective-permute-start(bf16[3,16,512]{2,1,0:T(8,128)(2,1)S(1)} %fusion.1), channel_id=1, source_target_pairs={{0,4},{1,5},{2,6},{3,7},{4,0},{5,1},{6,2},{7,3},{8,12},{9,13},{10,... | collective-permute-start | bytes 147464 | tf_op jit(solution)/shard_map/ppermute | solution.py:26
  17.6 5.1 %collective-permute-start.4 = (bf16[3,16,512]{2,1,0:T(8,128)(2,1)S(1)}, bf16[3,16,512]{2,1,0:T(8,128)(2,1)S(1)}, u32[]{:S(2)}, u32[]{:S(2)}) collective-permute-start(bf16[3,16,512]{2,1,0:T(8,128)(2,1)S(1)} %fusion.1), channel_id=1, source_target_pairs={{0,6},{1,7},{2,4},{3,5},{4,2},{5,3},{6,0},{7,1},{8,14},{9,15},{10,... | collective-permute-start | bytes 147464 | tf_op jit(solution)/shard_map/ppermute | solution.py:26
  22.7 23.0 %collective-permute-start.6 = (bf16[2,512,512]{2,1,0:T(8,128)(2,1)S(1)}, bf16[2,512,512]{2,1,0:T(8,128)(2,1)S(1)}, u32[]{:S(2)}, u32[]{:S(2)}) collective-permute-start(bf16[2,512,512]{2,1,0:T(8,128)(2,1)S(1)} %pad_maximum_fusion), channel_id=1, source_target_pairs={{0,1},{1,2},{2,3},{3,4},{4,5},{5,6},{6,7},{7,0},{8,9},{9,10},{10,1... | collective-permute-start | bytes 3145736 | tf_op jit(solution)/shard_map/ppermute | solution.py:32
  30.5 8.2 %collective-permute-start.10 = (bf16[2,4,3,16,512]{4,3,2,1,0:T(8,128)(2,1)S(1)}, bf16[2,4,3,16,512]{4,3,2,1,0:T(8,128)(2,1)S(1)}, u32[]{:S(2)}, u32[]{:S(2)}) collective-permute-start(bf16[2,4,3,16,512]{4,3,2,1,0:T(8,128)(2,1)S(1)} %pad_maximum_fusion.2.rest_0_), channel_id=1, source_target_pairs={{0,48},{1,49},{2,50},{3,51},{4,52},{5,53},{6,54},{7,55},{8,56},{9,... | collective-permute-start | bytes 1179656 | tf_op jit(solution)/shard_map/ppermute | solution.py:26
  31.6 17.6 %collective-permute-start.8 = (bf16[2,4,3,16,512]{4,3,2,1,0:T(8,128)(2,1)S(1)}, bf16[2,4,3,16,512]{4,3,2,1,0:T(8,128)(2,1)}, u32[]{:S(2)}, u32[]{:S(2)}) collective-permute-start(bf16[2,4,3,16,512]{4,3,2,1,0:T(8,128)(2,1)S(1)} %pad_maximum_fusion.2.rest_0_), channel_id=1, source_target_pairs={{0,16},{1,17},{2,18},{3,19},{4,20},{5,21},{6,22},{7,23},{8,24},{9,... | collective-permute-start | bytes 1179656 | tf_op jit(solution)/shard_map/ppermute | solution.py:26
  31.6 17.6 %collective-permute-start.9 = (bf16[2,4,3,16,512]{4,3,2,1,0:T(8,128)(2,1)S(1)}, bf16[2,4,3,16,512]{4,3,2,1,0:T(8,128)(2,1)}, u32[]{:S(2)}, u32[]{:S(2)}) collective-permute-start(bf16[2,4,3,16,512]{4,3,2,1,0:T(8,128)(2,1)S(1)} %pad_maximum_fusion.2.rest_0_), channel_id=1, source_target_pairs={{0,32},{1,33},{2,34},{3,35},{4,36},{5,37},{6,38},{7,39},{8,40},{9,... | collective-permute-start | bytes 1179656 | tf_op jit(solution)/shard_map/ppermute | solution.py:26
  39.5 19.7 %collective-permute-start.19 = (bf16[512,512]{1,0:T(8,128)(2,1)}, bf16[512,512]{1,0:T(8,128)(2,1)}, u32[]{:S(2)}, u32[]{:S(2)}) collective-permute-start(bf16[512,512]{1,0:T(8,128)(2,1)} %get-tuple-element.47), channel_id=1, source_target_pairs={{7,15},{15,23},{23,31},{31,39},{39,47},{47,55},{55,63},{71,79},{79... | collective-permute-start | bytes 1572872 | tf_op jit(solution)/shard_map/ppermute | solution.py:37
  45.7 13.5 %collective-permute-start.20 = (bf16[512,512]{1,0:T(8,128)(2,1)}, bf16[512,512]{1,0:T(8,128)(2,1)}, u32[]{:S(2)}, u32[]{:S(2)}) collective-permute-start(bf16[512,512]{1,0:T(8,128)(2,1)} %slice_select_fusion), channel_id=1, source_target_pairs={{0,1},{1,2},{2,3},{3,4},{4,5},{5,6},{6,7},{7,0},{8,9},{9,10},{10,1... | collective-permute-start | bytes 1572872 | tf_op jit(solution)/shard_map/ppermute | solution.py:32
  55.6 9.8 %collective-permute-start.11 = (bf16[4,3,16,512]{3,2,1,0:T(8,128)(2,1)S(1)}, bf16[4,3,16,512]{3,2,1,0:T(8,128)(2,1)S(1)}, u32[]{:S(2)}, u32[]{:S(2)}) collective-permute-start(bf16[4,3,16,512]{3,2,1,0:T(8,128)(2,1)S(1)} %get-tuple-element.39), channel_id=1, source_target_pairs={{0,8},{1,9},{2,10},{3,11},{4,12},{5,13},{6,14},{7,15},{8,0},{9,1},... | collective-permute-start | bytes 589832 | tf_op jit(solution)/shard_map/ppermute | solution.py:26
  56.8 9.2 %collective-permute-start.12 = (bf16[4,3,16,512]{3,2,1,0:T(8,128)(2,1)S(1)}, bf16[4,3,16,512]{3,2,1,0:T(8,128)(2,1)S(1)}, u32[]{:S(2)}, u32[]{:S(2)}) collective-permute-start(bf16[4,3,16,512]{3,2,1,0:T(8,128)(2,1)S(1)} %get-tuple-element.40), channel_id=1, source_target_pairs={{0,16},{1,17},{2,18},{3,19},{4,20},{5,21},{6,22},{7,23},{8,24},{9,... | collective-permute-start | bytes 589832 | tf_op jit(solution)/shard_map/ppermute | solution.py:26
  58.1 10.4 %collective-permute-start.13 = (bf16[4,3,16,512]{3,2,1,0:T(8,128)(2,1)S(1)}, bf16[4,3,16,512]{3,2,1,0:T(8,128)(2,1)S(1)}, u32[]{:S(2)}, u32[]{:S(2)}) collective-permute-start(bf16[4,3,16,512]{3,2,1,0:T(8,128)(2,1)S(1)} %get-tuple-element.41), channel_id=1, source_target_pairs={{0,24},{1,25},{2,26},{3,27},{4,28},{5,29},{6,30},{7,31},{8,16},{9,... | collective-permute-start | bytes 589832 | tf_op jit(solution)/shard_map/ppermute | solution.py:26
  60.6 24.3 %collective-permute-start.21 = (bf16[2,512,512]{2,1,0:T(8,128)(2,1)S(1)}, bf16[2,512,512]{2,1,0:T(8,128)(2,1)S(1)}, u32[]{:S(2)}, u32[]{:S(2)}) collective-permute-start(bf16[2,512,512]{2,1,0:T(8,128)(2,1)S(1)} %maximum_select_fusion), channel_id=1, source_target_pairs={{0,1},{1,2},{2,3},{3,4},{4,5},{5,6},{6,7},{7,0},{8,9},{9,10},{10,1... | collective-permute-start | bytes 3145736 | tf_op jit(solution)/shard_map/ppermute | solution.py:32
  61.9 8.9 %collective-permute-start.14 = (bf16[4,3,16,512]{3,2,1,0:T(8,128)(2,1)S(1)}, bf16[4,3,16,512]{3,2,1,0:T(8,128)(2,1)S(1)}, u32[]{:S(2)}, u32[]{:S(2)}) collective-permute-start(bf16[4,3,16,512]{3,2,1,0:T(8,128)(2,1)S(1)} %get-tuple-element.42), channel_id=1, source_target_pairs={{0,32},{1,33},{2,34},{3,35},{4,36},{5,37},{6,38},{7,39},{8,40},{9,... | collective-permute-start | bytes 589832 | tf_op jit(solution)/shard_map/ppermute | solution.py:26
  65.4 11.0 %collective-permute-start.15 = (bf16[4,3,16,512]{3,2,1,0:T(8,128)(2,1)S(1)}, bf16[4,3,16,512]{3,2,1,0:T(8,128)(2,1)S(1)}, u32[]{:S(2)}, u32[]{:S(2)}) collective-permute-start(bf16[4,3,16,512]{3,2,1,0:T(8,128)(2,1)S(1)} %get-tuple-element.43), channel_id=1, source_target_pairs={{0,40},{1,41},{2,42},{3,43},{4,44},{5,45},{6,46},{7,47},{8,32},{9,... | collective-permute-start | bytes 589832 | tf_op jit(solution)/shard_map/ppermute | solution.py:26
  66.0 13.8 %collective-permute-start.16 = (bf16[4,3,16,512]{3,2,1,0:T(8,128)(2,1)S(1)}, bf16[4,3,16,512]{3,2,1,0:T(8,128)(2,1)S(1)}, u32[]{:S(2)}, u32[]{:S(2)}) collective-permute-start(bf16[4,3,16,512]{3,2,1,0:T(8,128)(2,1)S(1)} %get-tuple-element.44), channel_id=1, source_target_pairs={{0,48},{1,49},{2,50},{3,51},{4,52},{5,53},{6,54},{7,55},{8,56},{9,... | collective-permute-start | bytes 589832 | tf_op jit(solution)/shard_map/ppermute | solution.py:26
  68.5 15.5 %collective-permute-start.17 = (bf16[4,3,16,512]{3,2,1,0:T(8,128)(2,1)S(1)}, bf16[4,3,16,512]{3,2,1,0:T(8,128)(2,1)S(1)}, u32[]{:S(2)}, u32[]{:S(2)}) collective-permute-start(bf16[4,3,16,512]{3,2,1,0:T(8,128)(2,1)S(1)} %get-tuple-element.45), channel_id=1, source_target_pairs={{0,56},{1,57},{2,58},{3,59},{4,60},{5,61},{6,62},{7,63},{8,48},{9,... | collective-permute-start | bytes 589832 | tf_op jit(solution)/shard_map/ppermute | solution.py:26
  84.1 19.5 %collective-permute-start.18 = (bf16[2,512,512]{2,1,0:T(8,128)(2,1)S(1)}, bf16[2,512,512]{2,1,0:T(8,128)(2,1)S(1)}, u32[]{:S(2)}, u32[]{:S(2)}) collective-permute-start(bf16[2,512,512]{2,1,0:T(8,128)(2,1)S(1)} %copy-done.6), channel_id=1, source_target_pairs={{7,15},{15,23},{23,31},{31,39},{39,47},{47,55},{55,63},{71,79},{79... | collective-permute-start | bytes 3145736 | tf_op jit(solution)/shard_map/ppermute | solution.py:37
  84.9 5.7 %collective-permute-start.22 = (bf16[3,16,512]{2,1,0:T(8,128)(2,1)S(1)}, bf16[3,16,512]{2,1,0:T(8,128)(2,1)S(1)}, u32[]{:S(2)}, u32[]{:S(2)}) collective-permute-start(bf16[3,16,512]{2,1,0:T(8,128)(2,1)S(1)} %get-tuple-element.52), channel_id=1, source_target_pairs={{0,2},{1,3},{2,0},{3,1},{4,6},{5,7},{6,4},{7,5},{8,10},{9,11},{10,... | collective-permute-start | bytes 147464 | tf_op jit(solution)/shard_map/ppermute | solution.py:26
  85.1 6.9 %collective-permute-start.23 = (bf16[3,16,512]{2,1,0:T(8,128)(2,1)S(1)}, bf16[3,16,512]{2,1,0:T(8,128)(2,1)S(1)}, u32[]{:S(2)}, u32[]{:S(2)}) collective-permute-start(bf16[3,16,512]{2,1,0:T(8,128)(2,1)S(1)} %fusion.3), channel_id=1, source_target_pairs={{0,4},{1,5},{2,6},{3,7},{4,0},{5,1},{6,2},{7,3},{8,12},{9,13},{10,... | collective-permute-start | bytes 147464 | tf_op jit(solution)/shard_map/ppermute | solution.py:26
  94.2 5.7 %collective-permute-start.25 = (bf16[3,16,512]{2,1,0:T(8,128)(2,1)S(1)}, bf16[3,16,512]{2,1,0:T(8,128)(2,1)S(1)}, u32[]{:S(2)}, u32[]{:S(2)}) collective-permute-start(bf16[3,16,512]{2,1,0:T(8,128)(2,1)S(1)} %get-tuple-element.66), channel_id=1, source_target_pairs={{0,2},{1,3},{2,0},{3,1},{4,6},{5,7},{6,4},{7,5},{8,10},{9,11},{10,... | collective-permute-start | bytes 147464 | tf_op jit(solution)/shard_map/ppermute | solution.py:26
  96.2 6.9 %collective-permute-start.26 = (bf16[3,16,512]{2,1,0:T(8,128)(2,1)S(1)}, bf16[3,16,512]{2,1,0:T(8,128)(2,1)S(1)}, u32[]{:S(2)}, u32[]{:S(2)}) collective-permute-start(bf16[3,16,512]{2,1,0:T(8,128)(2,1)S(1)} %get-tuple-element.66), channel_id=1, source_target_pairs={{0,4},{1,5},{2,6},{3,7},{4,0},{5,1},{6,2},{7,3},{8,12},{9,13},{10,... | collective-permute-start | bytes 147464 | tf_op jit(solution)/shard_map/ppermute | solution.py:26
  98.0 5.6 %collective-permute-start.27 = (bf16[3,16,512]{2,1,0:T(8,128)(2,1)S(1)}, bf16[3,16,512]{2,1,0:T(8,128)(2,1)S(1)}, u32[]{:S(2)}, u32[]{:S(2)}) collective-permute-start(bf16[3,16,512]{2,1,0:T(8,128)(2,1)S(1)} %get-tuple-element.66), channel_id=1, source_target_pairs={{0,6},{1,7},{2,4},{3,5},{4,2},{5,3},{6,0},{7,1},{8,14},{9,15},{10,... | collective-permute-start | bytes 147464 | tf_op jit(solution)/shard_map/ppermute | solution.py:26
  103.6 36.5 %collective-permute-start.28 = (bf16[2,512,512]{2,1,0:T(8,128)(2,1)S(1)}, bf16[2,512,512]{2,1,0:T(8,128)(2,1)S(1)}, u32[]{:S(2)}, u32[]{:S(2)}) collective-permute-start(bf16[2,512,512]{2,1,0:T(8,128)(2,1)S(1)} %collective-permute-done.18), channel_id=1, source_target_pairs={{7,0},{15,8},{23,16},{31,24},{39,32},{47,40},{55,48},{63,56},{71,6... | collective-permute-start | bytes 3145736 | tf_op jit(solution)/shard_map/ppermute | solution.py:42
  110.0 8.0 %collective-permute-start.30 = (bf16[2,4,3,16,512]{4,3,2,1,0:T(8,128)(2,1)S(1)}, bf16[2,4,3,16,512]{4,3,2,1,0:T(8,128)(2,1)S(1)}, u32[]{:S(2)}, u32[]{:S(2)}) collective-permute-start(bf16[2,4,3,16,512]{4,3,2,1,0:T(8,128)(2,1)S(1)} %pad_maximum_fusion.3.rest_0_), channel_id=1, source_target_pairs={{0,16},{1,17},{2,18},{3,19},{4,20},{5,21},{6,22},{7,23},{8,24},{9,... | collective-permute-start | bytes 1179656 | tf_op jit(solution)/shard_map/ppermute | solution.py:26
  112.5 13.2 %collective-permute-start.31 = (bf16[2,4,3,16,512]{4,3,2,1,0:T(8,128)(2,1)S(1)}, bf16[2,4,3,16,512]{4,3,2,1,0:T(8,128)(2,1)S(1)}, u32[]{:S(2)}, u32[]{:S(2)}) collective-permute-start(bf16[2,4,3,16,512]{4,3,2,1,0:T(8,128)(2,1)S(1)} %pad_maximum_fusion.3.rest_0_), channel_id=1, source_target_pairs={{0,32},{1,33},{2,34},{3,35},{4,36},{5,37},{6,38},{7,39},{8,40},{9,... | collective-permute-start | bytes 1179656 | tf_op jit(solution)/shard_map/ppermute | solution.py:26
  115.4 12.7 %collective-permute-start.32 = (bf16[2,4,3,16,512]{4,3,2,1,0:T(8,128)(2,1)S(1)}, bf16[2,4,3,16,512]{4,3,2,1,0:T(8,128)(2,1)S(1)}, u32[]{:S(2)}, u32[]{:S(2)}) collective-permute-start(bf16[2,4,3,16,512]{4,3,2,1,0:T(8,128)(2,1)S(1)} %pad_maximum_fusion.3.rest_0_), channel_id=1, source_target_pairs={{0,48},{1,49},{2,50},{3,51},{4,52},{5,53},{6,54},{7,55},{8,56},{9,... | collective-permute-start | bytes 1179656 | tf_op jit(solution)/shard_map/ppermute | solution.py:26
  131.6 24.5 %collective-permute-start.36 = (bf16[512,512]{1,0:T(8,128)(2,1)S(1)}, bf16[512,512]{1,0:T(8,128)(2,1)S(1)}, u32[]{:S(2)}, u32[]{:S(2)}) collective-permute-start(bf16[512,512]{1,0:T(8,128)(2,1)S(1)} %get-tuple-element.62), channel_id=1, source_target_pairs={{0,7},{1,0},{2,1},{3,2},{4,3},{5,4},{6,5},{7,6},{8,15},{9,8},{10,9... | collective-permute-start | bytes 1572872 | tf_op jit(solution)/shard_map/ppermute | solution.py:32
  142.1 10.2 %collective-permute-start.33 = (f32[2,512]{1,0:T(2,128)S(1)}, f32[2,512]{1,0:T(2,128)S(1)}, u32[]{:S(2)}, u32[]{:S(2)}) collective-permute-start(f32[2,512]{1,0:T(2,128)S(1)} %get-tuple-element.61), channel_id=1, source_target_pairs={{0,64},{64,0},{128,192},{192,128},{1,65},{65,1},{129,193},{193,129... | collective-permute-start | bytes 12296 | tf_op jit(solution)/shard_map/ppermute | solution.py:341
  (19 other events, 202.7 us)

commit v7 on v6

--- a/solution.py
+++ b/solution.py
@@ -275,7 +275,7 @@
     w_blocks = gather_xy(w_block)
     halo = ring(after(send_other, w_block), 1)
     last = (seq_pos & (RING - 1)) == RING - 1
-    plane_v = to_next_plane(after(values[:, HD:], w_blocks[-1]))
+    plane_v = to_next_plane(after(values, w_blocks[-1])[:, HD:])
     q_prev = ring(after(head_of(queries, False), halo), 1)
 
     def attend(pick, prev):

time: 161 us -> 162 us (level)
    ppermute x6, starting transfers between devices: 14.8 us -> 12.9 us  [ring(): return lax.ppermute(value, 'seq', pairs)]
    slice x2 -> x1, other arithmetic: 3.28 us -> 2.19 us  [head_of(): return jnp.where(flag, array[:, :HD], array[:, HD:])]
  transfers between devices with their start and end apart: 39 -> 39, of which waited for: 21 -> 20; matrix products, arithmetic and copies ran while one was open for 6% -> 6% of each run, Pallas kernels for 8% -> 8%
where the time goes in v7:
time: 162 us; the launch traced here: 161 us
  starting transfers between devices  73.5 us (45%)
  waiting for transfers between devices  60.9 us (38%)
  Pallas kernels  13.6 us (8%)
  other arithmetic  10.5 us (6%)
  local copies, waits for them, and re-layouts  1.86 us (1%)
    ppermute x26, waiting for transfers between devices, move_xor(): return lax.ppermute(value, 'seq', [(i, i ^ mask) for i in range(n)])  49.6 us
    ppermute x26, starting transfers between devices, move_xor(): return lax.ppermute(value, 'seq', [(i, i ^ mask) for i in range(n)])  45.3 us
    pallas_call x4, Pallas kernels, call(): pl.pallas_call(kernel, out_shape=outs, grid_spec=pltpu.PrefetchScalarGrid...  13.6 us
    ppermute x6, starting transfers between devices, ring(): return lax.ppermute(value, 'seq', pairs)  12.9 us
    ppermute x3, starting transfers between devices, local(): lax.ppermute(sq, 'head', [(i, i ^ k) for i in range(heads)])  10.4 us
    ppermute x6, waiting for transfers between devices, ring(): return lax.ppermute(value, 'seq', pairs)  7.49 us
    ppermute x3, waiting for transfers between devices, local(): lax.ppermute(sq, 'head', [(i, i ^ k) for i in range(heads)])  3.81 us
    ppermute x3, starting transfers between devices, to_next_plane(): lax.ppermute(value, 'seq', [(i, i + RING) for i in range(RING - 1, n - RI...  3.67 us
  transfers between devices with their start and end apart: 39, of which 20 were waited for; matrix products, arithmetic and copies ran while one was open for 6% of the time, Pallas kernels for 8%

profile of v7, /device:TPU:1, one launch (start us, length us, event | category | flops | bytes accessed | tf_op | source)
XLA Modules:
  0.0 161.3 jit_solution(257043181656814476)
XLA Ops:
  1.5 2.6 %collective-permute-start = (f32[3,8,512]{2,1,0:T(8,128)S(1)}, f32[3,8,512]{2,1,0:T(8,128)S(1)}, u32[]{:S(2)}, u32[]{:S(2)}) collective-permute-start(f32[3,8,512]{2,1,0:T(8,128)S(1)} %get-tuple-element.80), channel_id=1, source_target_pairs={{0,1},{1,0},{2,3},{3,2},{4,5},{5,4},{6,7},{7,6},{8,9},{9,8},{10,11... | collective-permute-start | bytes 147464 | tf_op jit(solution)/shard_map/ppermute | solution.py:26
  4.8 2.2 %fusion.8 = (bf16[512,512]{1,0:T(8,128)(2,1)S(1)}, bf16[1,512,512]{2,1,0:T(8,128)(2,1)}, bf16[1,512,512]{2,1,0:T(8,128)(2,1)S(1)}) fusion(bf16[512,1024]{1,0:T(8,128)(2,1)} %k_ref.3, pred[]{:T(512)S(6)} %eq.6, pred[]{:T(512)S(6)} %not.2), kind=kLoop, calls=%fused_computation.42 | loop fusion | flops 524288 | bytes 2621442 | tf_op jit(solution)/shard_map/slice | solution.py:249
  10.4 2.0 %collective-permute-start.2 = (bf16[3,16,512]{2,1,0:T(8,128)(2,1)S(1)}, bf16[3,16,512]{2,1,0:T(8,128)(2,1)S(1)}, u32[]{:S(2)}, u32[]{:S(2)}) collective-permute-start(bf16[3,16,512]{2,1,0:T(8,128)(2,1)S(1)} %fusion.1), channel_id=1, source_target_pairs={{0,2},{1,3},{2,0},{3,1},{4,6},{5,7},{6,4},{7,5},{8,10},{9,11},{10,... | collective-permute-start | bytes 147464 | tf_op jit(solution)/shard_map/ppermute | solution.py:26
  12.4 4.9 %collective-permute-start.3 = (bf16[3,16,512]{2,1,0:T(8,128)(2,1)S(1)}, bf16[3,16,512]{2,1,0:T(8,128)(2,1)S(1)}, u32[]{:S(2)}, u32[]{:S(2)}) collective-permute-start(bf16[3,16,512]{2,1,0:T(8,128)(2,1)S(1)} %fusion.1), channel_id=1, source_target_pairs={{0,4},{1,5},{2,6},{3,7},{4,0},{5,1},{6,2},{7,3},{8,12},{9,13},{10,... | collective-permute-start | bytes 147464 | tf_op jit(solution)/shard_map/ppermute | solution.py:26
  19.4 3.1 %collective-permute-done.4 = bf16[3,16,512]{2,1,0:T(8,128)(2,1)S(1)} collective-permute-done((bf16[3,16,512]{2,1,0:T(8,128)(2,1)S(1)}, bf16[3,16,512]{2,1,0:T(8,128)(2,1)S(1)}, u32[]{:S(2)}, u32[]{:S(2)}) %collective-permute-start.4) | collective-permute-done | bytes 49184 | tf_op jit(solution)/shard_map/ppermute | solution.py:26
  22.5 2.9 %collective-permute-start.6 = (bf16[2,512,512]{2,1,0:T(8,128)(2,1)S(1)}, bf16[2,512,512]{2,1,0:T(8,128)(2,1)S(1)}, u32[]{:S(2)}, u32[]{:S(2)}) collective-permute-start(bf16[2,512,512]{2,1,0:T(8,128)(2,1)S(1)} %pad_maximum_fusion), channel_id=1, source_target_pairs={{0,1},{1,2},{2,3},{3,4},{4,5},{5,6},{6,7},{7,0},{8,9},{9,10},{10,1... | collective-permute-start | bytes 3145736 | tf_op jit(solution)/shard_map/ppermute | solution.py:32
  25.5 4.7 %collective-permute-done.7 = bf16[4,3,16,512]{3,2,1,0:T(8,128)(2,1)S(1)} collective-permute-done((bf16[4,3,16,512]{3,2,1,0:T(8,128)(2,1)S(1)}, bf16[4,3,16,512]{3,2,1,0:T(8,128)(2,1)S(1)}, u32[]{:S(2)}, u32[]{:S(2)}) %collective-permute-start.7) | collective-permute-done | bytes 196640 | tf_op jit(solution)/shard_map/ppermute | solution.py:26
  31.4 2.8 %collective-permute-start.9 = (bf16[2,4,3,16,512]{4,3,2,1,0:T(8,128)(2,1)S(1)}, bf16[2,4,3,16,512]{4,3,2,1,0:T(8,128)(2,1)}, u32[]{:S(2)}, u32[]{:S(2)}) collective-permute-start(bf16[2,4,3,16,512]{4,3,2,1,0:T(8,128)(2,1)S(1)} %pad_maximum_fusion.2.rest_0_), channel_id=1, source_target_pairs={{0,32},{1,33},{2,34},{3,35},{4,36},{5,37},{6,38},{7,39},{8,40},{9,... | collective-permute-start | bytes 1179656 | tf_op jit(solution)/shard_map/ppermute | solution.py:26
  35.1 3.4 %collective-permute-done.10.rest_3_ = bf16[2,4,3,16,512]{4,3,2,1,0:T(8,128)(2,1)S(1)} collective-permute-done((bf16[2,4,3,16,512]{4,3,2,1,0:T(8,128)(2,1)S(1)}, bf16[2,4,3,16,512]{4,3,2,1,0:T(8,128)(2,1)S(1)}, u32[]{:S(2)}, u32[]{:S(2)}) %collective-permute-start.10) | collective-permute-done | bytes 393248 | tf_op jit(solution)/shard_map/ppermute | solution.py:26
  40.8 4.7 %collective-permute-done.6.halo = bf16[2,512,512]{2,1,0:T(8,128)(2,1)S(1)} collective-permute-done((bf16[2,512,512]{2,1,0:T(8,128)(2,1)S(1)}, bf16[2,512,512]{2,1,0:T(8,128)(2,1)S(1)}, u32[]{:S(2)}, u32[]{:S(2)}) %collective-permute-start.6) | collective-permute-done | bytes 1048608 | tf_op jit(solution)/shard_map/ppermute | solution.py:32
  45.5 2.0 %collective-permute-start.20 = (bf16[512,512]{1,0:T(8,128)(2,1)}, bf16[512,512]{1,0:T(8,128)(2,1)}, u32[]{:S(2)}, u32[]{:S(2)}) collective-permute-start(bf16[512,512]{1,0:T(8,128)(2,1)} %slice_select_fusion), channel_id=1, source_target_pairs={{0,1},{1,2},{2,3},{3,4},{4,5},{5,6},{6,7},{7,0},{8,9},{9,10},{10,1... | collective-permute-start | bytes 1572872 | tf_op jit(solution)/shard_map/ppermute | solution.py:32
  49.2 6.1 %shard_map.111 = (f32[4,3,16,512]{3,2,1,0:T(8,128)S(1)}, bf16[4,3,16,512]{3,2,1,0:T(8,128)(2,1)S(1)}, bf16[4,3,16,512]{3,2,1,0:T(8,128)(2,1)S(1)}, bf16[4,3,16,5...) custom-call(s32[16]{0:T(128)S(1)} %stack.168.s_ref, ...), custom_call_target="tpu_custom_call" | custom-call | flops 3221225472 | bytes 4722688 | tf_op jit(solution)/shard_map/pallas_call | solution.py:78
  61.7 3.7 %collective-permute-start.14 = (bf16[4,3,16,512]{3,2,1,0:T(8,128)(2,1)S(1)}, bf16[4,3,16,512]{3,2,1,0:T(8,128)(2,1)S(1)}, u32[]{:S(2)}, u32[]{:S(2)}) collective-permute-start(bf16[4,3,16,512]{3,2,1,0:T(8,128)(2,1)S(1)} %get-tuple-element.42), channel_id=1, source_target_pairs={{0,32},{1,33},{2,34},{3,35},{4,36},{5,37},{6,38},{7,39},{8,40},{9,... | collective-permute-start | bytes 589832 | tf_op jit(solution)/shard_map/ppermute | solution.py:26
  65.7 2.5 %collective-permute-start.16 = (bf16[4,3,16,512]{3,2,1,0:T(8,128)(2,1)S(1)}, bf16[4,3,16,512]{3,2,1,0:T(8,128)(2,1)S(1)}, u32[]{:S(2)}, u32[]{:S(2)}) collective-permute-start(bf16[4,3,16,512]{3,2,1,0:T(8,128)(2,1)S(1)} %get-tuple-element.44), channel_id=1, source_target_pairs={{0,48},{1,49},{2,50},{3,51},{4,52},{5,53},{6,54},{7,55},{8,56},{9,... | collective-permute-start | bytes 589832 | tf_op jit(solution)/shard_map/ppermute | solution.py:26
  70.8 5.7 %collective-permute-done.15 = bf16[4,3,16,512]{3,2,1,0:T(8,128)(2,1)S(1)} collective-permute-done((bf16[4,3,16,512]{3,2,1,0:T(8,128)(2,1)S(1)}, bf16[4,3,16,512]{3,2,1,0:T(8,128)(2,1)S(1)}, u32[]{:S(2)}, u32[]{:S(2)}) %collective-permute-start.15) | collective-permute-done | bytes 196640 | tf_op jit(solution)/shard_map/ppermute | solution.py:26
  76.5 3.3 %collective-permute-done.16 = bf16[4,3,16,512]{3,2,1,0:T(8,128)(2,1)S(1)} collective-permute-done((bf16[4,3,16,512]{3,2,1,0:T(8,128)(2,1)S(1)}, bf16[4,3,16,512]{3,2,1,0:T(8,128)(2,1)S(1)}, u32[]{:S(2)}, u32[]{:S(2)}) %collective-permute-start.16) | collective-permute-done | bytes 196640 | tf_op jit(solution)/shard_map/ppermute | solution.py:26
  79.8 4.2 %collective-permute-done.17 = bf16[4,3,16,512]{3,2,1,0:T(8,128)(2,1)S(1)} collective-permute-done((bf16[4,3,16,512]{3,2,1,0:T(8,128)(2,1)S(1)}, bf16[4,3,16,512]{3,2,1,0:T(8,128)(2,1)S(1)}, u32[]{:S(2)}, u32[]{:S(2)}) %collective-permute-start.17) | collective-permute-done | bytes 196640 | tf_op jit(solution)/shard_map/ppermute | solution.py:26
  85.0 4.0 %collective-permute-start.23 = (bf16[3,16,512]{2,1,0:T(8,128)(2,1)S(1)}, bf16[3,16,512]{2,1,0:T(8,128)(2,1)S(1)}, u32[]{:S(2)}, u32[]{:S(2)}) collective-permute-start(bf16[3,16,512]{2,1,0:T(8,128)(2,1)S(1)} %fusion.3), channel_id=1, source_target_pairs={{0,4},{1,5},{2,6},{3,7},{4,0},{5,1},{6,2},{7,3},{8,12},{9,13},{10,... | collective-permute-start | bytes 147464 | tf_op jit(solution)/shard_map/ppermute | solution.py:26
  92.0 2.0 %collective-permute-done.24 = bf16[3,16,512]{2,1,0:T(8,128)(2,1)S(1)} collective-permute-done((bf16[3,16,512]{2,1,0:T(8,128)(2,1)S(1)}, bf16[3,16,512]{2,1,0:T(8,128)(2,1)S(1)}, u32[]{:S(2)}, u32[]{:S(2)}) %collective-permute-start.24) | collective-permute-done | bytes 49184 | tf_op jit(solution)/shard_map/ppermute | solution.py:26
  96.0 2.1 %collective-permute-start.26 = (bf16[3,16,512]{2,1,0:T(8,128)(2,1)S(1)}, bf16[3,16,512]{2,1,0:T(8,128)(2,1)S(1)}, u32[]{:S(2)}, u32[]{:S(2)}) collective-permute-start(bf16[3,16,512]{2,1,0:T(8,128)(2,1)S(1)} %get-tuple-element.66), channel_id=1, source_target_pairs={{0,4},{1,5},{2,6},{3,7},{4,0},{5,1},{6,2},{7,3},{8,12},{9,13},{10,... | collective-permute-start | bytes 147464 | tf_op jit(solution)/shard_map/ppermute | solution.py:26
  99.9 3.0 %collective-permute-done.26 = bf16[3,16,512]{2,1,0:T(8,128)(2,1)S(1)} collective-permute-done((bf16[3,16,512]{2,1,0:T(8,128)(2,1)S(1)}, bf16[3,16,512]{2,1,0:T(8,128)(2,1)S(1)}, u32[]{:S(2)}, u32[]{:S(2)}) %collective-permute-start.26) | collective-permute-done | bytes 49184 | tf_op jit(solution)/shard_map/ppermute | solution.py:26
  104.7 2.1 %collective-permute-start.29 = (bf16[4,3,16,512]{3,2,1,0:T(8,128)(2,1)S(1)}, bf16[4,3,16,512]{3,2,1,0:T(8,128)(2,1)S(1)}, u32[]{:S(2)}, u32[]{:S(2)}) collective-permute-start(bf16[4,3,16,512]{3,2,1,0:T(8,128)(2,1)S(1)} %pad_maximum_fusion.5), channel_id=1, source_target_pairs={{0,8},{1,9},{2,10},{3,11},{4,12},{5,13},{6,14},{7,15},{8,0},{9,1},... | collective-permute-start | bytes 589832 | tf_op jit(solution)/shard_map/ppermute | solution.py:26
  106.8 3.1 %collective-permute-done.29 = bf16[4,3,16,512]{3,2,1,0:T(8,128)(2,1)S(1)} collective-permute-done((bf16[4,3,16,512]{3,2,1,0:T(8,128)(2,1)S(1)}, bf16[4,3,16,512]{3,2,1,0:T(8,128)(2,1)S(1)}, u32[]{:S(2)}, u32[]{:S(2)}) %collective-permute-start.29) | collective-permute-done | bytes 196640 | tf_op jit(solution)/shard_map/ppermute | solution.py:26
  109.9 2.3 %collective-permute-start.30 = (bf16[2,4,3,16,512]{4,3,2,1,0:T(8,128)(2,1)S(1)}, bf16[2,4,3,16,512]{4,3,2,1,0:T(8,128)(2,1)S(1)}, u32[]{:S(2)}, u32[]{:S(2)}) collective-permute-start(bf16[2,4,3,16,512]{4,3,2,1,0:T(8,128)(2,1)S(1)} %pad_maximum_fusion.3.rest_0_), channel_id=1, source_target_pairs={{0,16},{1,17},{2,18},{3,19},{4,20},{5,21},{6,22},{7,23},{8,24},{9,... | collective-permute-start | bytes 1179656 | tf_op jit(solution)/shard_map/ppermute | solution.py:26
  112.2 4.2 %collective-permute-start.31 = (bf16[2,4,3,16,512]{4,3,2,1,0:T(8,128)(2,1)S(1)}, bf16[2,4,3,16,512]{4,3,2,1,0:T(8,128)(2,1)S(1)}, u32[]{:S(2)}, u32[]{:S(2)}) collective-permute-start(bf16[2,4,3,16,512]{4,3,2,1,0:T(8,128)(2,1)S(1)} %pad_maximum_fusion.3.rest_0_), channel_id=1, source_target_pairs={{0,32},{1,33},{2,34},{3,35},{4,36},{5,37},{6,38},{7,39},{8,40},{9,... | collective-permute-start | bytes 1179656 | tf_op jit(solution)/shard_map/ppermute | solution.py:26
  118.4 9.4 %collective-permute-done.31.rest_2_ = bf16[2,4,3,16,512]{4,3,2,1,0:T(8,128)(2,1)S(1)} collective-permute-done((bf16[2,4,3,16,512]{4,3,2,1,0:T(8,128)(2,1)S(1)}, bf16[2,4,3,16,512]{4,3,2,1,0:T(8,128)(2,1)S(1)}, u32[]{:S(2)}, u32[]{:S(2)}) %collective-permute-start.31) | collective-permute-done | bytes 393248 | tf_op jit(solution)/shard_map/ppermute | solution.py:26
  127.8 2.7 %collective-permute-done.32.rest_3_ = bf16[2,4,3,16,512]{4,3,2,1,0:T(8,128)(2,1)S(1)} collective-permute-done((bf16[2,4,3,16,512]{4,3,2,1,0:T(8,128)(2,1)S(1)}, bf16[2,4,3,16,512]{4,3,2,1,0:T(8,128)(2,1)S(1)}, u32[]{:S(2)}, u32[]{:S(2)}) %collective-permute-start.32) | collective-permute-done | bytes 393248 | tf_op jit(solution)/shard_map/ppermute | solution.py:26
  130.5 3.6 %shard_map.113 = (bf16[512,512]{1,0:T(8,128)(2,1)S(1)}, bf16[512,512]{1,0:T(8,128)(2,1)S(1)}, f32[2,512]{1,0:T(2,128)S(1)}, f32[3,16,512]{2,1,0:T(8,128)S(1)}) custom-call(s32[16]{0:T(128)S(1)} %stack.168.s_ref, bf16[512,512]{1,0:T(8,128)(2,1)} %collective-permute-done.20.q_prev, bf16[512,1024]{1,0:T(8,128)(2,1)S(1)} %copy-done.2, ...), custom_call_target="tpu_custom_call" | custom-call | flops 1610612736 | bytes 3250176 | tf_op jit(solution)/shard_map/pallas_call | solution.py:78
  134.1 6.8 %collective-permute-start.36 = (bf16[512,512]{1,0:T(8,128)(2,1)S(1)}, bf16[512,512]{1,0:T(8,128)(2,1)S(1)}, u32[]{:S(2)}, u32[]{:S(2)}) collective-permute-start(bf16[512,512]{1,0:T(8,128)(2,1)S(1)} %get-tuple-element.62), channel_id=1, source_target_pairs={{0,7},{1,0},{2,1},{3,2},{4,3},{5,4},{6,5},{7,6},{8,15},{9,8},{10,9... | collective-permute-start | bytes 1572872 | tf_op jit(solution)/shard_map/ppermute | solution.py:32
  142.8 7.1 %collective-permute-start.33 = (f32[2,512]{1,0:T(2,128)S(1)}, f32[2,512]{1,0:T(2,128)S(1)}, u32[]{:S(2)}, u32[]{:S(2)}) collective-permute-start(f32[2,512]{1,0:T(2,128)S(1)} %get-tuple-element.61), channel_id=1, source_target_pairs={{0,64},{64,0},{128,192},{192,128},{1,65},{65,1},{129,193},{193,129... | collective-permute-start | bytes 12296 | tf_op jit(solution)/shard_map/ppermute | solution.py:341
  149.9 2.6 %collective-permute-start.34 = (f32[2,512]{1,0:T(2,128)S(1)}, f32[2,512]{1,0:T(2,128)S(1)}, u32[]{:S(2)}, u32[]{:S(2)}) collective-permute-start(f32[2,512]{1,0:T(2,128)S(1)} %get-tuple-element.61), channel_id=1, source_target_pairs={{0,128},{64,192},{128,0},{192,64},{1,129},{65,193},{129,1},{193,65... | collective-permute-start | bytes 12296 | tf_op jit(solution)/shard_map/ppermute | solution.py:341
  153.9 3.2 %collective-permute-done.35 = f32[2,512]{1,0:T(2,128)S(1)} collective-permute-done((f32[2,512]{1,0:T(2,128)S(1)}, f32[2,512]{1,0:T(2,128)S(1)}, u32[]{:S(2)}, u32[]{:S(2)}) %collective-permute-start.35) | collective-permute-done | bytes 4128 | tf_op jit(solution)/shard_map/ppermute | solution.py:341
  (104 shorter events, 41.5 us)
Async XLA Ops:
  1.5 7.9 %collective-permute-start = (f32[3,8,512]{2,1,0:T(8,128)S(1)}, f32[3,8,512]{2,1,0:T(8,128)S(1)}, u32[]{:S(2)}, u32[]{:S(2)}) collective-permute-start(f32[3,8,512]{2,1,0:T(8,128)S(1)} %get-tuple-element.80), channel_id=1, source_target_pairs={{0,1},{1,0},{2,3},{3,2},{4,5},{5,4},{6,7},{7,6},{8,9},{9,8},{10,11... | collective-permute-start | bytes 147464 | tf_op jit(solution)/shard_map/ppermute | solution.py:26
  4.8 5.6 %collective-permute-start.1 = (f32[1,512]{1,0:T(1,128)S(1)}, f32[1,512]{1,0:T(1,128)S(1)}, u32[]{:S(2)}, u32[]{:S(2)}) collective-permute-start(f32[1,512]{1,0:T(1,128)S(1)} %get-tuple-element.87), channel_id=1, source_target_pairs={{0,1},{1,2},{2,3},{3,4},{4,5},{5,6},{6,7},{7,0},{8,9},{9,10},{10,1... | collective-permute-start | bytes 6152 | tf_op jit(solution)/shard_map/ppermute | solution.py:32
  7.0 15.5 %collective-permute-start.5 = (bf16[512,512]{1,0:T(8,128)(2,1)S(1)}, bf16[512,512]{1,0:T(8,128)(2,1)}, u32[]{:S(2)}, u32[]{:S(2)}) collective-permute-start(bf16[512,512]{1,0:T(8,128)(2,1)S(1)} %get-tuple-element.70), channel_id=1, source_target_pairs={{7,15},{15,23},{23,31},{31,39},{39,47},{47,55},{55,63},{71,79},{79... | collective-permute-start | bytes 1572872 | tf_op jit(solution)/shard_map/ppermute | solution.py:37
  10.4 7.1 %collective-permute-start.2 = (bf16[3,16,512]{2,1,0:T(8,128)(2,1)S(1)}, bf16[3,16,512]{2,1,0:T(8,128)(2,1)S(1)}, u32[]{:S(2)}, u32[]{:S(2)}) collective-permute-start(bf16[3,16,512]{2,1,0:T(8,128)(2,1)S(1)} %fusion.1), channel_id=1, source_target_pairs={{0,2},{1,3},{2,0},{3,1},{4,6},{5,7},{6,4},{7,5},{8,10},{9,11},{10,... | collective-permute-start | bytes 147464 | tf_op jit(solution)/shard_map/ppermute | solution.py:26
  12.4 6.9 %collective-permute-start.3 = (bf16[3,16,512]{2,1,0:T(8,128)(2,1)S(1)}, bf16[3,16,512]{2,1,0:T(8,128)(2,1)S(1)}, u32[]{:S(2)}, u32[]{:S(2)}) collective-permute-start(bf16[3,16,512]{2,1,0:T(8,128)(2,1)S(1)} %fusion.1), channel_id=1, source_target_pairs={{0,4},{1,5},{2,6},{3,7},{4,0},{5,1},{6,2},{7,3},{8,12},{9,13},{10,... | collective-permute-start | bytes 147464 | tf_op jit(solution)/shard_map/ppermute | solution.py:26
  22.5 23.0 %collective-permute-start.6 = (bf16[2,512,512]{2,1,0:T(8,128)(2,1)S(1)}, bf16[2,512,512]{2,1,0:T(8,128)(2,1)S(1)}, u32[]{:S(2)}, u32[]{:S(2)}) collective-permute-start(bf16[2,512,512]{2,1,0:T(8,128)(2,1)S(1)} %pad_maximum_fusion), channel_id=1, source_target_pairs={{0,1},{1,2},{2,3},{3,4},{4,5},{5,6},{6,7},{7,0},{8,9},{9,10},{10,1... | collective-permute-start | bytes 3145736 | tf_op jit(solution)/shard_map/ppermute | solution.py:32
  30.2 8.2 %collective-permute-start.10 = (bf16[2,4,3,16,512]{4,3,2,1,0:T(8,128)(2,1)S(1)}, bf16[2,4,3,16,512]{4,3,2,1,0:T(8,128)(2,1)S(1)}, u32[]{:S(2)}, u32[]{:S(2)}) collective-permute-start(bf16[2,4,3,16,512]{4,3,2,1,0:T(8,128)(2,1)S(1)} %pad_maximum_fusion.2.rest_0_), channel_id=1, source_target_pairs={{0,48},{1,49},{2,50},{3,51},{4,52},{5,53},{6,54},{7,55},{8,56},{9,... | collective-permute-start | bytes 1179656 | tf_op jit(solution)/shard_map/ppermute | solution.py:26
  31.4 17.6 %collective-permute-start.8 = (bf16[2,4,3,16,512]{4,3,2,1,0:T(8,128)(2,1)S(1)}, bf16[2,4,3,16,512]{4,3,2,1,0:T(8,128)(2,1)}, u32[]{:S(2)}, u32[]{:S(2)}) collective-permute-start(bf16[2,4,3,16,512]{4,3,2,1,0:T(8,128)(2,1)S(1)} %pad_maximum_fusion.2.rest_0_), channel_id=1, source_target_pairs={{0,16},{1,17},{2,18},{3,19},{4,20},{5,21},{6,22},{7,23},{8,24},{9,... | collective-permute-start | bytes 1179656 | tf_op jit(solution)/shard_map/ppermute | solution.py:26
  31.4 17.6 %collective-permute-start.9 = (bf16[2,4,3,16,512]{4,3,2,1,0:T(8,128)(2,1)S(1)}, bf16[2,4,3,16,512]{4,3,2,1,0:T(8,128)(2,1)}, u32[]{:S(2)}, u32[]{:S(2)}) collective-permute-start(bf16[2,4,3,16,512]{4,3,2,1,0:T(8,128)(2,1)S(1)} %pad_maximum_fusion.2.rest_0_), channel_id=1, source_target_pairs={{0,32},{1,33},{2,34},{3,35},{4,36},{5,37},{6,38},{7,39},{8,40},{9,... | collective-permute-start | bytes 1179656 | tf_op jit(solution)/shard_map/ppermute | solution.py:26
  39.4 19.8 %collective-permute-start.19 = (bf16[512,512]{1,0:T(8,128)(2,1)}, bf16[512,512]{1,0:T(8,128)(2,1)}, u32[]{:S(2)}, u32[]{:S(2)}) collective-permute-start(bf16[512,512]{1,0:T(8,128)(2,1)} %slice.199), channel_id=1, source_target_pairs={{7,15},{15,23},{23,31},{31,39},{39,47},{47,55},{55,63},{71,79},{79... | collective-permute-start | bytes 1572872 | tf_op jit(solution)/shard_map/ppermute | solution.py:37
  45.5 13.7 %collective-permute-start.20 = (bf16[512,512]{1,0:T(8,128)(2,1)}, bf16[512,512]{1,0:T(8,128)(2,1)}, u32[]{:S(2)}, u32[]{:S(2)}) collective-permute-start(bf16[512,512]{1,0:T(8,128)(2,1)} %slice_select_fusion), channel_id=1, source_target_pairs={{0,1},{1,2},{2,3},{3,4},{4,5},{5,6},{6,7},{7,0},{8,9},{9,10},{10,1... | collective-permute-start | bytes 1572872 | tf_op jit(solution)/shard_map/ppermute | solution.py:32
  55.4 10.1 %collective-permute-start.11 = (bf16[4,3,16,512]{3,2,1,0:T(8,128)(2,1)S(1)}, bf16[4,3,16,512]{3,2,1,0:T(8,128)(2,1)S(1)}, u32[]{:S(2)}, u32[]{:S(2)}) collective-permute-start(bf16[4,3,16,512]{3,2,1,0:T(8,128)(2,1)S(1)} %get-tuple-element.39), channel_id=1, source_target_pairs={{0,8},{1,9},{2,10},{3,11},{4,12},{5,13},{6,14},{7,15},{8,0},{9,1},... | collective-permute-start | bytes 589832 | tf_op jit(solution)/shard_map/ppermute | solution.py:26
  56.8 9.0 %collective-permute-start.12 = (bf16[4,3,16,512]{3,2,1,0:T(8,128)(2,1)S(1)}, bf16[4,3,16,512]{3,2,1,0:T(8,128)(2,1)S(1)}, u32[]{:S(2)}, u32[]{:S(2)}) collective-permute-start(bf16[4,3,16,512]{3,2,1,0:T(8,128)(2,1)S(1)} %get-tuple-element.40), channel_id=1, source_target_pairs={{0,16},{1,17},{2,18},{3,19},{4,20},{5,21},{6,22},{7,23},{8,24},{9,... | collective-permute-start | bytes 589832 | tf_op jit(solution)/shard_map/ppermute | solution.py:26
  58.1 10.1 %collective-permute-start.13 = (bf16[4,3,16,512]{3,2,1,0:T(8,128)(2,1)S(1)}, bf16[4,3,16,512]{3,2,1,0:T(8,128)(2,1)S(1)}, u32[]{:S(2)}, u32[]{:S(2)}) collective-permute-start(bf16[4,3,16,512]{3,2,1,0:T(8,128)(2,1)S(1)} %get-tuple-element.41), channel_id=1, source_target_pairs={{0,24},{1,25},{2,26},{3,27},{4,28},{5,29},{6,30},{7,31},{8,16},{9,... | collective-permute-start | bytes 589832 | tf_op jit(solution)/shard_map/ppermute | solution.py:26
  60.6 24.3 %collective-permute-start.21 = (bf16[2,512,512]{2,1,0:T(8,128)(2,1)S(1)}, bf16[2,512,512]{2,1,0:T(8,128)(2,1)S(1)}, u32[]{:S(2)}, u32[]{:S(2)}) collective-permute-start(bf16[2,512,512]{2,1,0:T(8,128)(2,1)S(1)} %maximum_select_fusion), channel_id=1, source_target_pairs={{0,1},{1,2},{2,3},{3,4},{4,5},{5,6},{6,7},{7,0},{8,9},{9,10},{10,1... | collective-permute-start | bytes 3145736 | tf_op jit(solution)/shard_map/ppermute | solution.py:32
  61.7 9.1 %collective-permute-start.14 = (bf16[4,3,16,512]{3,2,1,0:T(8,128)(2,1)S(1)}, bf16[4,3,16,512]{3,2,1,0:T(8,128)(2,1)S(1)}, u32[]{:S(2)}, u32[]{:S(2)}) collective-permute-start(bf16[4,3,16,512]{3,2,1,0:T(8,128)(2,1)S(1)} %get-tuple-element.42), channel_id=1, source_target_pairs={{0,32},{1,33},{2,34},{3,35},{4,36},{5,37},{6,38},{7,39},{8,40},{9,... | collective-permute-start | bytes 589832 | tf_op jit(solution)/shard_map/ppermute | solution.py:26
  65.4 11.1 %collective-permute-start.15 = (bf16[4,3,16,512]{3,2,1,0:T(8,128)(2,1)S(1)}, bf16[4,3,16,512]{3,2,1,0:T(8,128)(2,1)S(1)}, u32[]{:S(2)}, u32[]{:S(2)}) collective-permute-start(bf16[4,3,16,512]{3,2,1,0:T(8,128)(2,1)S(1)} %get-tuple-element.43), channel_id=1, source_target_pairs={{0,40},{1,41},{2,42},{3,43},{4,44},{5,45},{6,46},{7,47},{8,32},{9,... | collective-permute-start | bytes 589832 | tf_op jit(solution)/shard_map/ppermute | solution.py:26
  65.7 14.0 %collective-permute-start.16 = (bf16[4,3,16,512]{3,2,1,0:T(8,128)(2,1)S(1)}, bf16[4,3,16,512]{3,2,1,0:T(8,128)(2,1)S(1)}, u32[]{:S(2)}, u32[]{:S(2)}) collective-permute-start(bf16[4,3,16,512]{3,2,1,0:T(8,128)(2,1)S(1)} %get-tuple-element.44), channel_id=1, source_target_pairs={{0,48},{1,49},{2,50},{3,51},{4,52},{5,53},{6,54},{7,55},{8,56},{9,... | collective-permute-start | bytes 589832 | tf_op jit(solution)/shard_map/ppermute | solution.py:26
  68.2 15.8 %collective-permute-start.17 = (bf16[4,3,16,512]{3,2,1,0:T(8,128)(2,1)S(1)}, bf16[4,3,16,512]{3,2,1,0:T(8,128)(2,1)S(1)}, u32[]{:S(2)}, u32[]{:S(2)}) collective-permute-start(bf16[4,3,16,512]{3,2,1,0:T(8,128)(2,1)S(1)} %get-tuple-element.45), channel_id=1, source_target_pairs={{0,56},{1,57},{2,58},{3,59},{4,60},{5,61},{6,62},{7,63},{8,48},{9,... | collective-permute-start | bytes 589832 | tf_op jit(solution)/shard_map/ppermute | solution.py:26
  84.1 19.3 %collective-permute-start.18 = (bf16[2,512,512]{2,1,0:T(8,128)(2,1)S(1)}, bf16[2,512,512]{2,1,0:T(8,128)(2,1)S(1)}, u32[]{:S(2)}, u32[]{:S(2)}) collective-permute-start(bf16[2,512,512]{2,1,0:T(8,128)(2,1)S(1)} %copy-done.6), channel_id=1, source_target_pairs={{7,15},{15,23},{23,31},{31,39},{39,47},{47,55},{55,63},{71,79},{79... | collective-permute-start | bytes 3145736 | tf_op jit(solution)/shard_map/ppermute | solution.py:37
  84.9 5.7 %collective-permute-start.22 = (bf16[3,16,512]{2,1,0:T(8,128)(2,1)S(1)}, bf16[3,16,512]{2,1,0:T(8,128)(2,1)S(1)}, u32[]{:S(2)}, u32[]{:S(2)}) collective-permute-start(bf16[3,16,512]{2,1,0:T(8,128)(2,1)S(1)} %get-tuple-element.52), channel_id=1, source_target_pairs={{0,2},{1,3},{2,0},{3,1},{4,6},{5,7},{6,4},{7,5},{8,10},{9,11},{10,... | collective-permute-start | bytes 147464 | tf_op jit(solution)/shard_map/ppermute | solution.py:26
  85.0 7.0 %collective-permute-start.23 = (bf16[3,16,512]{2,1,0:T(8,128)(2,1)S(1)}, bf16[3,16,512]{2,1,0:T(8,128)(2,1)S(1)}, u32[]{:S(2)}, u32[]{:S(2)}) collective-permute-start(bf16[3,16,512]{2,1,0:T(8,128)(2,1)S(1)} %fusion.3), channel_id=1, source_target_pairs={{0,4},{1,5},{2,6},{3,7},{4,0},{5,1},{6,2},{7,3},{8,12},{9,13},{10,... | collective-permute-start | bytes 147464 | tf_op jit(solution)/shard_map/ppermute | solution.py:26
  94.2 5.7 %collective-permute-start.25 = (bf16[3,16,512]{2,1,0:T(8,128)(2,1)S(1)}, bf16[3,16,512]{2,1,0:T(8,128)(2,1)S(1)}, u32[]{:S(2)}, u32[]{:S(2)}) collective-permute-start(bf16[3,16,512]{2,1,0:T(8,128)(2,1)S(1)} %get-tuple-element.66), channel_id=1, source_target_pairs={{0,2},{1,3},{2,0},{3,1},{4,6},{5,7},{6,4},{7,5},{8,10},{9,11},{10,... | collective-permute-start | bytes 147464 | tf_op jit(solution)/shard_map/ppermute | solution.py:26
  96.0 6.9 %collective-permute-start.26 = (bf16[3,16,512]{2,1,0:T(8,128)(2,1)S(1)}, bf16[3,16,512]{2,1,0:T(8,128)(2,1)S(1)}, u32[]{:S(2)}, u32[]{:S(2)}) collective-permute-start(bf16[3,16,512]{2,1,0:T(8,128)(2,1)S(1)} %get-tuple-element.66), channel_id=1, source_target_pairs={{0,4},{1,5},{2,6},{3,7},{4,0},{5,1},{6,2},{7,3},{8,12},{9,13},{10,... | collective-permute-start | bytes 147464 | tf_op jit(solution)/shard_map/ppermute | solution.py:26
  98.1 5.3 %collective-permute-start.27 = (bf16[3,16,512]{2,1,0:T(8,128)(2,1)S(1)}, bf16[3,16,512]{2,1,0:T(8,128)(2,1)S(1)}, u32[]{:S(2)}, u32[]{:S(2)}) collective-permute-start(bf16[3,16,512]{2,1,0:T(8,128)(2,1)S(1)} %get-tuple-element.66), channel_id=1, source_target_pairs={{0,6},{1,7},{2,4},{3,5},{4,2},{5,3},{6,0},{7,1},{8,14},{9,15},{10,... | collective-permute-start | bytes 147464 | tf_op jit(solution)/shard_map/ppermute | solution.py:26
  103.4 37.4 %collective-permute-start.28 = (bf16[2,512,512]{2,1,0:T(8,128)(2,1)S(1)}, bf16[2,512,512]{2,1,0:T(8,128)(2,1)S(1)}, u32[]{:S(2)}, u32[]{:S(2)}) collective-permute-start(bf16[2,512,512]{2,1,0:T(8,128)(2,1)S(1)} %collective-permute-done.18), channel_id=1, source_target_pairs={{7,0},{15,8},{23,16},{31,24},{39,32},{47,40},{55,48},{63,56},{71,6... | collective-permute-start | bytes 3145736 | tf_op jit(solution)/shard_map/ppermute | solution.py:42
  104.7 5.2 %collective-permute-start.29 = (bf16[4,3,16,512]{3,2,1,0:T(8,128)(2,1)S(1)}, bf16[4,3,16,512]{3,2,1,0:T(8,128)(2,1)S(1)}, u32[]{:S(2)}, u32[]{:S(2)}) collective-permute-start(bf16[4,3,16,512]{3,2,1,0:T(8,128)(2,1)S(1)} %pad_maximum_fusion.5), channel_id=1, source_target_pairs={{0,8},{1,9},{2,10},{3,11},{4,12},{5,13},{6,14},{7,15},{8,0},{9,1},... | collective-permute-start | bytes 589832 | tf_op jit(solution)/shard_map/ppermute | solution.py:26
  109.9 8.5 %collective-permute-start.30 = (bf16[2,4,3,16,512]{4,3,2,1,0:T(8,128)(2,1)S(1)}, bf16[2,4,3,16,512]{4,3,2,1,0:T(8,128)(2,1)S(1)}, u32[]{:S(2)}, u32[]{:S(2)}) collective-permute-start(bf16[2,4,3,16,512]{4,3,2,1,0:T(8,128)(2,1)S(1)} %pad_maximum_fusion.3.rest_0_), channel_id=1, source_target_pairs={{0,16},{1,17},{2,18},{3,19},{4,20},{5,21},{6,22},{7,23},{8,24},{9,... | collective-permute-start | bytes 1179656 | tf_op jit(solution)/shard_map/ppermute | solution.py:26
  112.2 15.5 %collective-permute-start.31 = (bf16[2,4,3,16,512]{4,3,2,1,0:T(8,128)(2,1)S(1)}, bf16[2,4,3,16,512]{4,3,2,1,0:T(8,128)(2,1)S(1)}, u32[]{:S(2)}, u32[]{:S(2)}) collective-permute-start(bf16[2,4,3,16,512]{4,3,2,1,0:T(8,128)(2,1)S(1)} %pad_maximum_fusion.3.rest_0_), channel_id=1, source_target_pairs={{0,32},{1,33},{2,34},{3,35},{4,36},{5,37},{6,38},{7,39},{8,40},{9,... | collective-permute-start | bytes 1179656 | tf_op jit(solution)/shard_map/ppermute | solution.py:26
  116.5 14.0 %collective-permute-start.32 = (bf16[2,4,3,16,512]{4,3,2,1,0:T(8,128)(2,1)S(1)}, bf16[2,4,3,16,512]{4,3,2,1,0:T(8,128)(2,1)S(1)}, u32[]{:S(2)}, u32[]{:S(2)}) collective-permute-start(bf16[2,4,3,16,512]{4,3,2,1,0:T(8,128)(2,1)S(1)} %pad_maximum_fusion.3.rest_0_), channel_id=1, source_target_pairs={{0,48},{1,49},{2,50},{3,51},{4,52},{5,53},{6,54},{7,55},{8,56},{9,... | collective-permute-start | bytes 1179656 | tf_op jit(solution)/shard_map/ppermute | solution.py:26
  134.1 23.1 %collective-permute-start.36 = (bf16[512,512]{1,0:T(8,128)(2,1)S(1)}, bf16[512,512]{1,0:T(8,128)(2,1)S(1)}, u32[]{:S(2)}, u32[]{:S(2)}) collective-permute-start(bf16[512,512]{1,0:T(8,128)(2,1)S(1)} %get-tuple-element.62), channel_id=1, source_target_pairs={{0,7},{1,0},{2,1},{3,2},{4,3},{5,4},{6,5},{7,6},{8,15},{9,8},{10,9... | collective-permute-start | bytes 1572872 | tf_op jit(solution)/shard_map/ppermute | solution.py:32
  142.8 10.5 %collective-permute-start.33 = (f32[2,512]{1,0:T(2,128)S(1)}, f32[2,512]{1,0:T(2,128)S(1)}, u32[]{:S(2)}, u32[]{:S(2)}) collective-permute-start(f32[2,512]{1,0:T(2,128)S(1)} %get-tuple-element.61), channel_id=1, source_target_pairs={{0,64},{64,0},{128,192},{192,128},{1,65},{65,1},{129,193},{193,129... | collective-permute-start | bytes 12296 | tf_op jit(solution)/shard_map/ppermute | solution.py:341
  (19 other events, 208.6 us)
